TPU v7x, 32 devices: a whole 2x2x4 slice. The times are simulated.
32 devices in a mesh: tm: 8 (over z, y), lm: 4 (over x, core).
Axes of the slice: x: 2, y: 2, z: 4, core: 2. Of those that a mesh axis runs over, the one named last changes fastest.
Arguments:
- knot_right_side: float32 [6, 128, 128], P(None, 'tm')
- land_rhs: float32 [3, 131072], P(None, ('tm', 'lm'))
- jac_knot: bfloat16 [3072, 32, 384], P(('tm', 'lm')), may hold values from -0.21875 to 0.21875
- jac_land: bfloat16 [3072, 32, 192], P(('tm', 'lm')), may hold values from -0.5 to 0.5
- obs_knot: int32 [3072], P(('tm', 'lm')), may hold values from 0 to 31
- obs_slot: int32 [3072], P(('tm', 'lm')), may hold values from 0 to 127
- obs_count: int32 [3072], P(('tm', 'lm')), may hold values from 8 to 32
- send_list: int32 [32, 32, 4], P(('tm', 'lm')), may hold values from 0 to 63
- couple: float32 [6, 6, 128, 128], P(None, None, 'tm')
- knot_dinv: float32 [6, 6, 128, 128], P(None, None, 'tm')
- cuts: int32 [128, 128], P('tm'), may hold values 0 or 1
- land_pinv: float32 [3, 3, 131072], P(None, None, ('tm', 'lm'))
- knot_damp: float32 [6, 128, 128], P(None, 'tm'), may hold values from 0.3 to 3
- land_damp: float32 [3, 131072], P(None, ('tm', 'lm')), may hold values from 0.3 to 3
Outputs:
- knot_step: float32 [6, 128, 128], P(None, 'tm')
- land_step: float32 [3, 131072], P(None, ('tm', 'lm'))
- knot_resid: float32 [6, 128, 128], P(None, 'tm')
- land_resid: float32 [3, 131072], P(None, ('tm', 'lm'))
Inputs may be any that keep to these rules, and one draw needn't show every extreme that they name: send_list[s, d, c] is the local landmark block of device s that device s places into its slot c for device d; blocks may repeat. Observation block o sees the landmark block that device obs_slot[o] // 4 places into slot obs_slot[o] % 4 for device o // 96. obs_knot[o] = j names the knot block of vehicles 4 * j to 4 * j + 3 on the time index o // 384.
All inputs are finite; a program needn't handle non-finite values. No bound on the sum of `cuts` on one device may be relied on, other than what follows from the above.
Results may differ from a plain program's by a relative error of at most 0.00115.
Values may be sent and summed in bfloat16 or wider, within the bound.
No kernel may reach another device: no remote copies, remote signals or barrier semaphores. Data moves between devices by JAX's collectives and lax.ppermute only.
A program may use at most 192 MiB of HBM per device.

v0:
```python
import functools
import jax
import jax.numpy as jnp
from jax import lax
from jax.experimental import pallas as pl
from jax.experimental.pallas import tpu as pltpu
from jax.sharding import PartitionSpec as P

VB = 4
LB = 64
ITERS = 3
LANES = 128
AXES = ("tm", "lm")
F32 = jnp.float32
BF16 = jnp.bfloat16

NT = (((1,), (1,)), ((), ()))
TN = (((0,), (0,)), ((), ()))
NN = (((1,), (0,)), ((), ()))


def up8(value):
    return (value + 7) // 8 * 8


def bf_dot(left, right, dims):
    return lax.dot_general(left, right, dims, preferred_element_type=F32)


def matvec(tiles, vector):
    total = tiles[0] * vector[0:1]
    for index in range(1, len(tiles)):
        total = total + tiles[index] * vector[index : index + 1]
    return total


def whole_sum(value):
    return jnp.sum(jnp.sum(value, axis=0, keepdims=True), axis=1, keepdims=True)


class Plan:
    def __init__(self, comps, knots, land, rows, n_tm, n_lm, cap, width):
        self.comps, self.knots, self.land, self.rows = comps, knots, land, rows
        self.n_tm, self.n_lm, self.cap = n_tm, n_lm, cap
        self.devices = n_tm * n_lm
        self.slots = self.devices * cap
        self.width = width
        self.field = comps * knots
        self.pairs = land // LANES
        self.blocks = land // LB
        self.zrows = up8(2 * cap)
        self.items = 3
        self.items0 = 3 + 2 * comps
        self.held = -(-self.items // n_lm)
        self.held0 = -(-self.items0 // n_lm)
        self.rw = self.zrows + up8(comps * self.held)
        self.rw0 = self.zrows + up8(comps * self.held0)

    def item_row(self, source, item, rw):
        holder = source * self.n_lm + item % self.n_lm
        return holder * rw + self.zrows + self.comps * (item // self.n_lm)


def col_tiles(ref, plan, k):
    step = plan.comps * plan.knots
    return [
        ref[pl.ds(b * plan.knots + k, plan.comps, stride=step), :] for b in range(plan.comps)
    ]


def row_tiles(ref, plan, k):
    step = plan.comps * plan.knots
    return [
        ref[pl.ds(a * step + k, plan.comps, stride=plan.knots), :] for a in range(plan.comps)
    ]


def local_sweeps(plan, resid_ref, couple_ref, dinv_ref, cuts_ref, zloc_ref, maps=None):
    comps, knots = plan.comps, plan.knots
    lanes = couple_ref.shape[1]
    minus = cuts_ref[...].astype(F32) - 1.0
    carry = None
    basis = []
    if maps is not None:
        rows = lax.broadcasted_iota(jnp.int32, (comps, lanes), 0)
        basis = [(rows == b).astype(F32) for b in range(comps)]
    eye = basis
    scaled, turned, scaled_maps = [], [], []
    energy = jnp.zeros((comps, lanes), F32)
    for k in range(knots):
        value = resid_ref[pl.ds(k, comps, stride=knots), :]
        if carry is not None:
            value = value + carry
        dcol = col_tiles(dinv_ref, plan, k)
        y = matvec(dcol, value)
        scaled.append(y)
        turned.append(matvec(row_tiles(dinv_ref, plan, k), value))
        energy = energy + value * y
        lcol = col_tiles(couple_ref, plan, k)
        gate = minus[k : k + 1]
        carry = gate * matvec(lcol, value)
        if maps is not None:
            scaled_maps.append([matvec(dcol, col) for col in basis])
            basis = [gate * matvec(lcol, col) for col in basis]
    out = carry
    total = basis
    z, u = None, None
    onward, back = [None] * comps, eye
    for k in reversed(range(knots)):
        lrow = row_tiles(couple_ref, plan, k)
        gate = minus[k : k + 1]
        z = scaled[k] if z is None else scaled[k] + gate * matvec(lrow, z)
        u = turned[k] if u is None else turned[k] + gate * matvec(lrow, u)
        zloc_ref[pl.ds(k, comps, stride=knots), :] = z
        if maps is not None:
            onward_ref, back_ref = maps
            onward = [
                scaled_maps[k][b]
                if onward[b] is None
                else scaled_maps[k][b] + gate * matvec(lrow, onward[b])
                for b in range(comps)
            ]
            back = [gate * matvec(lrow, back[b]) for b in range(comps)]
            for b in range(comps):
                spot = pl.ds(b * knots + k, comps, stride=comps * knots)
                onward_ref[spot, :] = onward[b]
                back_ref[spot, :] = back[b]
    return out, z, z + u, energy, total, onward


def scale_land(plan, pinv_ref, land):
    pairs = plan.pairs
    result = []
    for a in range(3):
        total = pinv_ref[pl.ds(3 * a * pairs, pairs), :] * land[0]
        for b in range(1, 3):
            total = total + pinv_ref[pl.ds((3 * a + b) * pairs, pairs), :] * land[b]
        result.append(total)
    return result


def lower_half(shape):
    return lax.broadcasted_iota(jnp.int32, shape, 1) < LB


def roll_half(value):
    return pltpu.roll(value, LB, 1)


def split3(value):
    high = value.astype(BF16)
    rest = value - high.astype(F32)
    mid = rest.astype(BF16)
    low = (rest - mid.astype(F32)).astype(BF16)
    return high, mid, low


def pack_first(plan, rw, held, pick_ref, land_z, scalar, items, place_ref, item_ref, tile_ref, send_ref):
    devices, cap, comps = plan.devices, plan.cap, plan.comps
    half = lower_half(land_z[0].shape)
    z0, z1, z2 = land_z
    r0, r1, r2 = roll_half(z0), roll_half(z1), roll_half(z2)
    zero = jnp.zeros_like(z0)
    first = jnp.concatenate([jnp.where(half, z0, r1), jnp.where(half, r0, z1)], axis=0)
    second = jnp.concatenate([jnp.where(half, z2, zero), jnp.where(half, r2, zero)], axis=0)
    both = jnp.concatenate([first, second], axis=1)
    stacked = jnp.concatenate(list(split3(both)), axis=0)
    pick = pick_ref[...]
    picks = jnp.concatenate([pick, pick, pick], axis=0)
    rows = bf_dot(picks, stacked, TN)
    spot = lax.broadcasted_iota(jnp.int32, (devices, LANES), 1) == LB
    for c in range(cap):
        part = rows[c * devices : (c + 1) * devices]
        tail = part[:, LANES:]
        if c == 0:
            tail = jnp.where(spot, scalar, tail)
        send_ref[pl.ds(c, devices, stride=rw), :] = part[:, :LANES]
        send_ref[pl.ds(cap + c, devices, stride=rw), :] = tail
    for unused in range(2 * cap, plan.zrows):
        send_ref[pl.ds(unused, devices, stride=rw), :] = jnp.zeros((devices, LANES), F32)
    item_ref[...] = jnp.zeros_like(item_ref)
    for index, item in enumerate(items):
        item_ref[index, pl.ds(0, comps), :] = item
    tile_ref[...] = jnp.zeros_like(tile_ref)
    mine = place_ref[1]
    for k in range(held):
        tile_ref[pl.ds(comps * k, comps), :] = item_ref[k * plan.n_lm + mine, pl.ds(0, comps), :]
    tile = tile_ref[...]
    for d in range(devices):
        send_ref[pl.ds(d * rw + plan.zrows, rw - plan.zrows), :] = tile


def leader(place_ref):
    return (place_ref[1] == 0).astype(F32)


def start_kernel(
    plan,
    place_ref,
    resid_ref,
    rhs_ref,
    couple_ref,
    dinv_ref,
    cuts_ref,
    pinv_ref,
    damp_ref,
    list_ref,
    send_ref,
    zloc_ref,
    onward_ref,
    back_ref,
    land_ref,
    land_z_ref,
    land_damp_ref,
    land_pinv_ref,
    pick_ref,
    item_ref,
    tile_ref,
):
    pairs = plan.pairs
    for j in range(pairs):
        cut = pl.ds(j * LANES, LANES)
        land_ref[pl.ds(j, 3, stride=pairs), :] = rhs_ref[:, cut]
        land_damp_ref[pl.ds(j, 3, stride=pairs), :] = damp_ref[:, cut]
        for a in range(3):
            land_pinv_ref[pl.ds(3 * a * pairs + j, 3, stride=pairs), :] = pinv_ref[a, :, cut]
    index = lax.broadcasted_iota(jnp.int32, (plan.blocks, plan.slots), 0)
    wanted = list_ref[...]
    wanted = (wanted % 2) * pairs + wanted // 2
    pick_ref[...] = (index == wanted).astype(F32).astype(BF16)
    land = [land_ref[pl.ds(a * pairs, pairs), :] for a in range(3)]
    land_z = scale_land(plan, land_pinv_ref, land)
    energy = jnp.zeros((pairs, LANES), F32)
    for a in range(3):
        land_z_ref[pl.ds(a * pairs, pairs), :] = land_z[a]
        energy = energy + land[a] * land_z[a]
    out, v1, v12, knot_energy, total, inner = local_sweeps(
        plan, resid_ref, couple_ref, dinv_ref, cuts_ref, zloc_ref, (onward_ref, back_ref)
    )
    scalar = whole_sum(energy) + leader(place_ref) * whole_sum(knot_energy)
    pack_first(
        plan, plan.rw0, plan.held0, pick_ref, land_z, scalar, [out, v1, v12] + total + inner,
        place_ref, item_ref, tile_ref, send_ref,
    )


def product_kernel(first, plan, *refs):
    refs = list(refs)
    place_ref, recv_ref, zloc_ref, onward_ref, back_ref, land_z_ref = refs[:6]
    knot_damp_ref, land_damp_ref, jk_ref, jl_ref, link_ref, sel_ref, spread_ref = refs[6:13]
    refs = refs[13:]
    if first:
        rw = plan.rw0
        outs = refs
    else:
        rw = plan.rw
        chain_in_ref, rho_in_ref, knot_in_ref, land_in_ref, slot_in_ref = refs[:5]
        outs = refs[5:]
    send_ref, part_ref, rho_ref, knot_ref, land_ref, slot_ref = outs[:6]
    outs = outs[6:]
    if first:
        chain_ref = outs[0]
        outs = outs[1:]
    else:
        chain_ref = chain_in_ref
    entry_ref, arrive_ref, wide_ref = outs
    comps, knots, cap, devices = plan.comps, plan.knots, plan.cap, plan.devices
    lanes = zloc_ref.shape[1]
    square = comps * comps

    if first:
        for s in range(plan.n_tm):
            for m in range(2 * comps):
                spot = plan.item_row(s, 3 + m, rw)
                chain_ref[pl.ds(s * 2 * square + m * comps, comps), :] = recv_ref[
                    pl.ds(spot, comps), :
                ]

    def item(s, index):
        return recv_ref[pl.ds(plan.item_row(s, index, rw), comps), :]

    incoming = None
    firsts = []
    heat = jnp.zeros((comps, lanes), F32)
    for s in range(plan.n_tm):
        base = s * 2 * square
        v1 = item(s, 1)
        if incoming is None:
            entry_ref[s, pl.ds(0, comps), :] = jnp.zeros((comps, lanes), F32)
            firsts.append(v1)
            incoming = item(s, 0)
        else:
            entry_ref[s, pl.ds(0, comps), :] = incoming
            inner = [chain_ref[pl.ds(base + square + b * comps, comps), :] for b in range(comps)]
            pushed = matvec(inner, incoming)
            heat = heat + incoming * (item(s, 2) + pushed)
            firsts.append(v1 + pushed)
            if s + 1 < plan.n_tm:
                total = [chain_ref[pl.ds(base + b * comps, comps), :] for b in range(comps)]
                incoming = matvec(total, incoming) + item(s, 0)
    arriving = None
    for s in reversed(range(plan.n_tm)):
        base = s * 2 * square
        if arriving is None:
            arrive_ref[s, pl.ds(0, comps), :] = jnp.zeros((comps, lanes), F32)
            arriving = firsts[s]
        else:
            arrive_ref[s, pl.ds(0, comps), :] = arriving
            if s > 0:
                back = [
                    chain_ref[pl.ds(base + a, comps, stride=comps), :] for a in range(comps)
                ]
                arriving = firsts[s] + matvec(back, arriving)

    lane = lax.broadcasted_iota(jnp.int32, (devices, LANES), 1)
    tails = [recv_ref[pl.ds(cap + c, devices, stride=rw), :] for c in range(cap)]
    heads = [recv_ref[pl.ds(c, devices, stride=rw), :] for c in range(cap)]
    rho = whole_sum(jnp.where(lane == LB, tails[0], 0.0)) + whole_sum(heat)
    rho_ref[...] = jnp.broadcast_to(rho, rho_ref.shape)
    if not first:
        beta = rho / rho_in_ref[0:1, 0:1]
    half = lane < LB
    tails = [jnp.where(half, tail, 0.0) for tail in tails]
    slot_dir = []
    for index, rows in enumerate(heads + tails):
        spot = pl.ds(index * devices, devices)
        if not first:
            rows = rows + beta * slot_in_ref[spot, :]
        slot_ref[spot, :] = rows
        slot_dir.append(rows)
    land_dir = land_z_ref[...]
    if not first:
        land_dir = land_dir + beta * land_in_ref[...]
    land_ref[...] = land_dir
    heat = whole_sum(land_damp_ref[...] * land_dir * land_dir)

    mine = place_ref[0]
    entry = entry_ref[mine, pl.ds(0, comps), :]
    arrive = arrive_ref[mine, pl.ds(0, comps), :]
    for a in range(comps):
        total = zloc_ref[pl.ds(a * knots, knots), :]
        for b in range(comps):
            spot = pl.ds((a * comps + b) * knots, knots)
            total = total + onward_ref[spot, :] * entry[b : b + 1]
            total = total + back_ref[spot, :] * arrive[b : b + 1]
        if not first:
            total = total + beta * knot_in_ref[pl.ds(a * knots, knots), :]
        knot_ref[pl.ds(a * knots, knots), :] = total
    knot_dir = knot_ref[...]
    heat = heat + leader(place_ref) * whole_sum(knot_damp_ref[...] * knot_dir * knot_dir)

    groups = lanes // VB
    narrow = knot_dir.astype(BF16)
    padded = jnp.concatenate([narrow, jnp.zeros((LANES - plan.field, lanes), BF16)], axis=0)
    turned = bf_dot(sel_ref[...], padded, NT).astype(BF16)
    joined = jnp.concatenate(
        [turned[i * groups : (i + 1) * groups] for i in range(VB)], axis=1
    )
    knot_rows = bf_dot(joined, spread_ref[...], NN).astype(BF16)
    slot_rows = jnp.concatenate(
        [
            jnp.concatenate(slot_dir[:cap], axis=0).astype(BF16),
            jnp.concatenate(slot_dir[cap:], axis=0).astype(BF16)[:, :LB],
        ],
        axis=1,
    )
    chunk = 512
    knot_total, land_total = None, None
    for start in range(0, plan.rows, chunk):
        cut = pl.ds(start, chunk)
        jk, jl = jk_ref[cut, :], jl_ref[cut, :]
        near = bf_dot(knot_rows, jk, NT)
        far = bf_dot(slot_rows, jl, NT)
        knot_hit = lax.broadcasted_iota(jnp.int32, near.shape, 0) == link_ref[0:1, cut]
        slot_hit = lax.broadcasted_iota(jnp.int32, far.shape, 0) == link_ref[1:2, cut]
        resid = jnp.sum(jnp.where(knot_hit, near, 0.0), axis=0, keepdims=True) + jnp.sum(
            jnp.where(slot_hit, far, 0.0), axis=0, keepdims=True
        )
        knot_side = jnp.where(knot_hit, resid, 0.0).astype(BF16)
        slot_side = jnp.where(slot_hit, resid, 0.0).astype(BF16)
        knot_term = bf_dot(knot_side, jk, NN)
        land_term = bf_dot(slot_side, jl, NN)
        knot_total = knot_term if knot_total is None else knot_total + knot_term
        land_total = land_term if land_total is None else land_total + land_term

    parted = bf_dot(knot_total.astype(BF16), spread_ref[...], NT).astype(BF16)
    piled = jnp.concatenate(
        [parted[:, i * LANES : (i + 1) * LANES] for i in range(VB)], axis=0
    )
    part = bf_dot(piled, sel_ref[...], TN)[: plan.field]
    part_ref[...] = part.astype(BF16)
    heat = heat + whole_sum(part * knot_dir)
    land_total = land_total.astype(BF16).astype(F32)
    lead_rows = land_total[:, :LANES]
    tail_rows = jnp.concatenate(
        [land_total[:, LANES:], jnp.zeros((plan.slots, LANES - LB), F32)], axis=1
    )
    sums = jnp.zeros((devices, LANES), F32)
    for c in range(cap):
        cut = slice(c * devices, (c + 1) * devices)
        sums = sums + lead_rows[cut] * slot_dir[c] + tail_rows[cut] * slot_dir[cap + c]
    heat = heat + whole_sum(sums)
    high, mid, low = [piece.astype(F32) for piece in split3(heat)]
    if 2 * cap < plan.zrows:
        wide_ref[...] = jnp.zeros_like(wide_ref)
    for c in range(cap):
        cut = slice(c * devices, (c + 1) * devices)
        tail = tail_rows[cut]
        if c == 0:
            tail = jnp.where(lane == LB, high, tail)
            tail = jnp.where(lane == LB + 1, mid, tail)
            tail = jnp.where(lane == LB + 2, low, tail)
        wide_ref[pl.ds(c, devices, stride=plan.zrows), :] = lead_rows[cut]
        wide_ref[pl.ds(cap + c, devices, stride=plan.zrows), :] = tail
    send_ref[...] = wide_ref[...].astype(BF16)


def update_kernel(first, last, plan, *refs):
    refs = list(refs)
    place_ref, recv_ref = refs[:2]
    part_refs = refs[2 : 2 + plan.n_lm]
    refs = refs[2 + plan.n_lm :]
    rho_ref, knot_dir_ref, land_dir_ref, knot_resid_ref, land_resid_ref = refs[:5]
    knot_damp_ref, land_damp_ref, pick_ref = refs[5:8]
    refs = refs[8:]
    if not first:
        knot_step_ref, land_step_ref = refs[:2]
        refs = refs[2:]
    if not last:
        couple_ref, dinv_ref, cuts_ref, pinv_ref = refs[:4]
        refs = refs[4:]
    knot_step_out, land_step_out, knot_resid_out, land_resid_out = refs[:4]
    refs = refs[4:]
    if not last:
        send_ref, zloc_ref, land_z_ref = refs[:3]
        refs = refs[3:]
        wide_ref, item_ref, tile_ref = refs
    else:
        wide_ref, step_tmp, resid_tmp = refs
    cap, devices, pairs = plan.cap, plan.devices, plan.pairs

    wide_ref[...] = recv_ref[...].astype(F32)
    lane = lax.broadcasted_iota(jnp.int32, (devices, LANES), 1)
    heads = [wide_ref[pl.ds(c, devices, stride=plan.zrows), :] for c in range(cap)]
    tails = [wide_ref[pl.ds(cap + c, devices, stride=plan.zrows), :] for c in range(cap)]
    scalars = (lane >= LB) & (lane < LB + 3)
    alpha = rho_ref[0:1, 0:1] / whole_sum(jnp.where(scalars, tails[0], 0.0))
    lead = bf_dot(pick_ref[...], jnp.concatenate(heads, axis=0).astype(BF16), NN)
    tail = bf_dot(pick_ref[...], jnp.concatenate(tails, axis=0).astype(BF16), NN)
    half = lower_half((pairs, LANES))
    even, odd = lead[:pairs], lead[pairs:]
    grads = [
        jnp.where(half, even, roll_half(odd)),
        jnp.where(half, roll_half(even), odd),
        jnp.where(half, tail[:pairs], roll_half(tail[pairs:])),
    ]

    parts = [ref[...].astype(F32) for ref in part_refs]
    while len(parts) > 1:
        parts = [parts[i] + parts[i + 1] for i in range(0, len(parts), 2)]
    knot_dir = knot_dir_ref[...]
    knot_q = parts[0] + knot_damp_ref[...] * knot_dir
    step = alpha * knot_dir
    knot_step_out[...] = step if first else knot_step_ref[...] + step
    knot_resid_out[...] = knot_resid_ref[...] - alpha * knot_q

    step_to, resid_to = (step_tmp, resid_tmp) if last else (land_step_out, land_resid_out)
    land = []
    for a in range(3):
        spot = pl.ds(a * pairs, pairs)
        along = land_dir_ref[spot, :]
        q = grads[a] + land_damp_ref[spot, :] * along
        step = alpha * along
        step_to[spot, :] = step if first else land_step_ref[spot, :] + step
        value = land_resid_ref[spot, :] - alpha * q
        resid_to[spot, :] = value
        land.append(value)
    if last:
        for j in range(pairs):
            cut = pl.ds(j * LANES, LANES)
            land_step_out[:, cut] = step_tmp[pl.ds(j, 3, stride=pairs), :]
            land_resid_out[:, cut] = resid_tmp[pl.ds(j, 3, stride=pairs), :]
        return
    land_z = scale_land(plan, pinv_ref, land)
    energy = jnp.zeros((pairs, LANES), F32)
    for a in range(3):
        land_z_ref[pl.ds(a * pairs, pairs), :] = land_z[a]
        energy = energy + land[a] * land_z[a]
    out, v1, v12, knot_energy, _, _ = local_sweeps(
        plan, knot_resid_out, couple_ref, dinv_ref, cuts_ref, zloc_ref
    )
    scalar = whole_sum(energy) + leader(place_ref) * whole_sum(knot_energy)
    pack_first(
        plan, plan.rw, plan.held, pick_ref, land_z, scalar, [out, v1, v12],
        place_ref, item_ref, tile_ref, send_ref,
    )


def call(kernel, name, outs, args, scratch):
    vmem = pl.BlockSpec(memory_space=pltpu.VMEM)
    smem = pl.BlockSpec(memory_space=pltpu.SMEM)
    return pl.pallas_call(
        kernel,
        name=name,
        out_shape=[jax.ShapeDtypeStruct(shape, dtype) for shape, dtype in outs],
        in_specs=[smem] + [vmem] * (len(args) - 1),
        out_specs=[vmem] * len(outs),
        scratch_shapes=scratch,
        compiler_params=pltpu.CompilerParams(vmem_limit_bytes=24 << 20),
    )(*args)


def exchange(blocks, devices):
    rows = blocks.shape[0] // devices
    shaped = blocks.reshape(devices, rows, LANES)
    moved = lax.all_to_all(shaped, AXES, split_axis=0, concat_axis=0, tiled=True)
    return moved.reshape(blocks.shape)


def swap(value, mask):
    count = lax.axis_size("lm")
    return lax.ppermute(value, "lm", [(i, i ^ mask) for i in range(count)])


def on_device(
    knot_right_side,
    land_rhs,
    jac_knot,
    jac_land,
    obs_knot,
    obs_slot,
    obs_count,
    send_list,
    couple,
    knot_dinv,
    cuts,
    land_pinv,
    knot_damp,
    land_damp,
):
    comps, knots, vehicles = knot_right_side.shape
    observed, height, knot_width = jac_knot.shape
    rows = observed * height
    cap = send_list.shape[2]
    n_tm, n_lm = lax.axis_size("tm"), lax.axis_size("lm")
    plan = Plan(
        comps, knots, land_rhs.shape[1], rows, n_tm, n_lm, cap, jac_land.shape[2]
    )
    devices, slots, field, pairs = plan.devices, plan.slots, plan.field, plan.pairs
    square = comps * comps

    place = jnp.stack([lax.axis_index("tm"), lax.axis_index("lm")]).astype(jnp.int32)
    resid = knot_right_side.reshape(field, vehicles)
    couple = couple.reshape(square * knots, vehicles)
    dinv = knot_dinv.reshape(square * knots, vehicles)
    knot_damp = knot_damp.reshape(field, vehicles)
    jk = jac_knot.reshape(rows, knot_width)
    jl = jac_land.reshape(rows, jac_land.shape[2])
    listed = jnp.transpose(send_list[0]).reshape(1, slots)

    live = jnp.arange(height, dtype=jnp.int32)[None, :] < obs_count[:, None]
    slot = (obs_slot % cap) * devices + obs_slot // cap
    links = jnp.stack(
        [jnp.where(live, obs_knot[:, None], -1), jnp.where(live, slot[:, None], -1)]
    ).reshape(2, rows)

    groups = vehicles // VB
    lane = jnp.arange(vehicles, dtype=jnp.int32)
    ordered = (lane % groups) * VB + lane // groups
    sel = (ordered[:, None] == lane[None, :]).astype(BF16)
    spot = jnp.arange(VB * LANES, dtype=jnp.int32)
    aim = jnp.where(spot % LANES < field, (spot % LANES) * VB + spot // LANES, -1)
    spread = (aim[:, None] == jnp.arange(knot_width, dtype=jnp.int32)[None, :]).astype(BF16)

    def items_scratch(held):
        return [
            pltpu.VMEM((held * n_lm, 8, LANES), F32),
            pltpu.VMEM((up8(comps * held), LANES), F32),
        ]

    send, zloc, onward, back, land_resid, land_z, damp, pinv, pick = call(
        functools.partial(start_kernel, plan),
        "start",
        [
            ((devices * plan.rw0, LANES), F32),
            ((field, vehicles), F32),
            ((square * knots, vehicles), F32),
            ((square * knots, vehicles), F32),
            ((3 * pairs, LANES), F32),
            ((3 * pairs, LANES), F32),
            ((3 * pairs, LANES), F32),
            ((9 * pairs, LANES), F32),
            ((plan.blocks, slots), BF16),
        ],
        [place, resid, land_rhs, couple, dinv, cuts, land_pinv, land_damp, listed],
        items_scratch(plan.held0),
    )
    state = None
    chain = None
    steps = None
    for turn in range(ITERS):
        first, last = turn == 0, turn == ITERS - 1
        recv = exchange(send, devices)
        args = [place, recv, zloc, onward, back, land_z, knot_damp, damp, jk, jl, links, sel, spread]
        outs = [
            ((devices * plan.zrows, LANES), BF16),
            ((field, vehicles), BF16),
            ((8, LANES), F32),
            ((field, vehicles), F32),
            ((3 * pairs, LANES), F32),
            ((2 * slots, LANES), F32),
        ]
        if first:
            outs.append(((n_tm * 2 * square, vehicles), F32))
        else:
            args += [chain] + list(state)
        results = call(
            functools.partial(product_kernel, first, plan),
            "product_first" if first else "product",
            outs,
            args,
            [
                pltpu.VMEM((n_tm, 8, vehicles), F32),
                pltpu.VMEM((n_tm, 8, vehicles), F32),
                pltpu.VMEM((devices * plan.zrows, LANES), F32),
            ],
        )
        send, part = results[:2]
        state = results[2:6]
        if first:
            chain = results[6]
        rho, knot_dir, land_dir, _ = state
        parts = [part] + [swap(part, mask) for mask in range(1, n_lm)]
        recv = exchange(send, devices)
        args = [place, recv] + parts
        args += [rho, knot_dir, land_dir, resid, land_resid, knot_damp, damp, pick]
        if not first:
            args += list(steps)
        wide = pltpu.VMEM((devices * plan.zrows, LANES), F32)
        if last:
            outs = [((field, vehicles), F32), ((3, plan.land), F32)] * 2
            scratch = [wide] + [pltpu.VMEM((3 * pairs, LANES), F32)] * 2
        else:
            args += [couple, dinv, cuts, pinv]
            outs = [((field, vehicles), F32), ((3 * pairs, LANES), F32)] * 2
            outs += [
                ((devices * plan.rw, LANES), F32),
                ((field, vehicles), F32),
                ((3 * pairs, LANES), F32),
            ]
            scratch = [wide] + items_scratch(plan.held)
        results = call(
            functools.partial(update_kernel, first, last, plan),
            "update_last" if last else "update",
            outs,
            args,
            scratch,
        )
        steps = results[:2]
        resid, land_resid = results[2:4]
        if not last:
            send, zloc, land_z = results[4:]
    shape = (comps, knots, vehicles)
    return (steps[0].reshape(shape), steps[1], resid.reshape(shape), land_resid)


def solution(mesh):
    return jax.shard_map(
        on_device,
        mesh=mesh,
        in_specs=(
            P(None, "tm", None),
            P(None, ("tm", "lm")),
            P(("tm", "lm"), None, None),
            P(("tm", "lm"), None, None),
            P(("tm", "lm")),
            P(("tm", "lm")),
            P(("tm", "lm")),
            P(("tm", "lm"), None, None),
            P(None, None, "tm", None),
            P(None, None, "tm", None),
            P("tm", None),
            P(None, None, ("tm", "lm")),
            P(None, "tm", None),
            P(None, ("tm", "lm")),
        ),
        out_specs=(
            P(None, "tm", None),
            P(None, ("tm", "lm")),
            P(None, "tm", None),
            P(None, ("tm", "lm")),
        ),
        check_vma=False,
    )
```

profile of v0, /device:TPU:0, one launch (start us, length us, event | category | flops | bytes accessed | tf_op | source)
XLA Modules:
  0.0 170.1 jit_solution(3354432813744233655)
XLA Ops:
  1.6 1.0 copy-done.4
  2.6 1.0 copy-done.6
  7.7 2.5 %start.1 = (f32[1024,128]{1,0:T(8,128)S(1)}, f32[96,128]{1,0:T(8,128)S(1)}, f32[576,128]{1,0:T(8,128)S(1)}, f32[576,128]{1,0:T(8,128)S(1)}, f32[96,128]{1,0:T(8,...) custom-call(s32[2]{0:T(128)S(1)} %pad_add_fusion.1.place_ref.refs_0_, ...), custom_call_target="tpu_custom_call" | custom-call | tf_op jit(solution)/shard_map/start/pallas_call | solution.py:502
  15.6 7.3 %all-to-all-start = ((f32[32,32,128]{2,1,0:T(8,128)}), f32[32,32,128]{2,1,0:T(8,128)S(1)}, u32[]{:S(2)}, u32[]{:S(2)}) async-start(f32[32,32,128]{2,1,0:T(8,128)} %bitcast.52), calls=%async_computation | async-start | bytes 1048576 | tf_op jit(solution)/shard_map/all_to_all | solution.py:516
  23.9 14.6 %all-to-all-done = f32[32,32,128]{2,1,0:T(8,128)S(1)} async-done(((f32[32,32,128]{2,1,0:T(8,128)}), f32[32,32,128]{2,1,0:T(8,128)S(1)}, u32[]{:S(2)}, u32[]{:S(2)}) %all-to-all-start) | async-done | bytes 524320 | tf_op jit(solution)/shard_map/all_to_all | solution.py:516
  39.3 1.4 copy-done.1
  40.7 1.0 copy-done.9
  41.7 1.0 copy-done.13
  42.7 1.0 copy-done.17
  46.0 4.0 %product_first.1 = (bf16[256,128]{1,0:T(8,128)(2,1)S(1)}, bf16[96,128]{1,0:T(8,128)(2,1)S(1)}, f32[8,128]{1,0:T(8,128)S(1)}, f32[96,128]{1,0:T(8,128)S(1)}, f32[...) custom-call(s32[2]{0:T(128)S(1)} %copy-done.78, f32[1024,128]{1,0:T(8,128)S(1)} %bitcast.43, ...), custom_call_target="tpu_custom_call" | custom-call | tf_op jit(solution)/shard_map/product_first/pallas_call | solution.py:502
  53.8 3.3 %all-to-all-start.1 = ((bf16[32,8,128]{2,1,0:T(8,128)(2,1)}), bf16[32,8,128]{2,1,0:T(8,128)(2,1)}, u32[]{:S(2)}, u32[]{:S(2)}) async-start(bf16[32,8,128]{2,1,0:T(8,128)(2,1)} %bitcast.59), calls=%async_computation.1 | async-start | bytes 131072 | tf_op jit(solution)/shard_map/all_to_all | solution.py:516
  57.1 1.4 collective-permute-start.2
  59.1 1.7 collective-permute-done.2.refs_5_
  61.4 1.2 collective-permute-done.1.refs_4_
  64.5 1.0 copy-done.23
  73.0 1.8 %update.2 = (f32[96,128]{1,0:T(8,128)S(1)}, f32[96,128]{1,0:T(8,128)S(1)}, f32[96,128]{1,0:T(8,128)S(1)}, f32[96,128]{1,0:T(8,128)S(1)}, f32[512,128]{1,0:T(8,12...) custom-call(s32[2]{0:T(128)S(1)} %copy-done.79, bf16[256,128]{1,0:T(8,128)(2,1)} %bitcast.13.refs_1_, ...), custom_call_target="tpu_custom_call" | custom-call | tf_op jit(solution)/shard_map/update/pallas_call | solution.py:502
  74.8 14.4 %all_to_all.30 = f32[32,16,128]{2,1,0:T(8,128)S(1)} all-to-all(f32[32,16,128]{2,1,0:T(8,128)S(1)} %bitcast.54), channel_id=1, replica_groups=mesh['tm'=8,'lm'=4] {'tm','lm'}, dimensions={0} | all-to-all | bytes 524288 | tf_op jit(solution)/shard_map/all_to_all | solution.py:516
  96.0 4.0 %product.2 = (bf16[256,128]{1,0:T(8,128)(2,1)S(1)}, bf16[96,128]{1,0:T(8,128)(2,1)S(1)}, f32[8,128]{1,0:T(8,128)S(1)}, f32[96,128]{1,0:T(8,128)S(1)}, f32[96,128]{1,0:T(8,128)S(1)}, /*index=5*/f32[256,128]{1,0:T(8,128)S(1)}) custom-call(s32[2]{0:T(128)S(1)} %copy-done.80, f32[512,128]{1,0:T(8,128)S(1)} %bitcast.51, f32[96,128]{1,0:T(8,128)S(1)} %get-tuple-element.64.refs_2_, ...), custom_call_target="tpu_custom_call" | custom-call | tf_op jit(solution)/shard_map/product/pallas_call | solution.py:502
  103.1 3.3 %all-to-all-start.3 = ((bf16[32,8,128]{2,1,0:T(8,128)(2,1)}), bf16[32,8,128]{2,1,0:T(8,128)(2,1)}, u32[]{:S(2)}, u32[]{:S(2)}) async-start(bf16[32,8,128]{2,1,0:T(8,128)(2,1)} %bitcast.58), calls=%async_computation.3 | async-start | bytes 131072 | tf_op jit(solution)/shard_map/all_to_all | solution.py:516
  106.4 1.4 collective-permute-start.5
  108.3 1.7 collective-permute-done.5.refs_5_
  110.6 1.2 collective-permute-done.4.refs_4_
  113.8 1.0 copy-done.24
  123.8 1.8 %update.3 = (f32[96,128]{1,0:T(8,128)S(1)}, f32[96,128]{1,0:T(8,128)S(1)}, f32[96,128]{1,0:T(8,128)S(1)}, f32[96,128]{1,0:T(8,128)S(1)}, f32[512,128]{1,0:T(8,12...) custom-call(s32[2]{0:T(128)S(1)} %copy-done.81, bf16[256,128]{1,0:T(8,128)(2,1)} %bitcast.17.refs_1_, ...), custom_call_target="tpu_custom_call" | custom-call | tf_op jit(solution)/shard_map/update/pallas_call | solution.py:502
  125.7 14.4 %all_to_all.31 = f32[32,16,128]{2,1,0:T(8,128)S(1)} all-to-all(f32[32,16,128]{2,1,0:T(8,128)S(1)} %bitcast.53), channel_id=1, replica_groups=mesh['tm'=8,'lm'=4] {'tm','lm'}, dimensions={0} | all-to-all | bytes 524288 | tf_op jit(solution)/shard_map/all_to_all | solution.py:516
  146.0 4.7 %product.3 = (bf16[256,128]{1,0:T(8,128)(2,1)}, bf16[96,128]{1,0:T(8,128)(2,1)S(1)}, f32[8,128]{1,0:T(8,128)S(1)}, f32[96,128]{1,0:T(8,128)S(1)}, f32[96,128]{1,0:T(8,128)S(1)}, /*index=5*/f32[256,128]{1,0:T(8,128)}) custom-call(s32[2]{0:T(128)S(1)} %copy-done.82, f32[512,128]{1,0:T(8,128)S(1)} %bitcast.50, f32[96,128]{1,0:T(8,128)S(1)} %get-tuple-element.78.refs_2_, ...), custom_call_target="tpu_custom_call" | custom-call | tf_op jit(solution)/shard_map/product/pallas_call | solution.py:502
  152.6 2.6 %all-to-all-start.5 = ((bf16[32,8,128]{2,1,0:T(8,128)(2,1)}), bf16[32,8,128]{2,1,0:T(8,128)(2,1)S(1)}, u32[]{:S(2)}, u32[]{:S(2)}) async-start(bf16[32,8,128]{2,1,0:T(8,128)(2,1)} %bitcast.20), calls=%async_computation.5 | async-start | bytes 131072 | tf_op jit(solution)/shard_map/all_to_all | solution.py:516
  155.1 1.4 collective-permute-start.8
  157.1 1.4 collective-permute-done.8.refs_5_
  158.5 1.9 %collective-permute-done.7.refs_4_ = bf16[96,128]{1,0:T(8,128)(2,1)S(1)} collective-permute-done((bf16[96,128]{1,0:T(8,128)(2,1)S(1)}, bf16[96,128]{1,0:T(8,128)(2,1)S(1)}, u32[]{:S(2)}, u32[]{:S(2)}) %collective-permute-start.7) | collective-permute-done | bytes 24608 | tf_op jit(solution)/shard_map/ppermute | solution.py:522
  160.4 2.1 %all-to-all-done.5 = bf16[32,8,128]{2,1,0:T(8,128)(2,1)S(1)} async-done(((bf16[32,8,128]{2,1,0:T(8,128)(2,1)}), bf16[32,8,128]{2,1,0:T(8,128)(2,1)S(1)}, u32[]{:S(2)}, u32[]{:S(2)}) %all-to-all-start.5) | async-done | bytes 65568 | tf_op jit(solution)/shard_map/all_to_all | solution.py:516
  168.7 1.4 update_last.1
  (242 shorter events, 65.1 us)
Async XLA Ops:
  0.6 38.7 %copy-start = (bf16[96,32,384]{2,1,0:T(8,128)(2,1)S(1)}, bf16[96,32,384]{2,1,0:T(8,128)(2,1)}, u32[]{:S(2)}) copy-start(bf16[96,32,384]{2,1,0:T(8,128)(2,1)} %param.16) | copy-start | bytes 7077892
  7.7 15.5 %copy-start.110 = (s32[96]{0:T(128)S(1)}, s32[96]{0:T(128)}, u32[]{:S(2)}) copy-start(s32[96]{0:T(128)} %param.19) | copy-start | bytes 1156
  7.7 15.7 %copy-start.108 = (s32[96]{0:T(128)S(1)}, s32[96]{0:T(128)}, u32[]{:S(2)}) copy-start(s32[96]{0:T(128)} %param.18) | copy-start | bytes 1156
  7.7 15.9 %copy-start.109 = (s32[96]{0:T(128)S(1)}, s32[96]{0:T(128)}, u32[]{:S(2)}) copy-start(s32[96]{0:T(128)} %param.20) | copy-start | bytes 1156
  7.7 31.7 %copy-start.18 = (f32[6,16,128]{2,1,0:T(8,128)S(1)}, f32[6,16,128]{2,1,0:T(8,128)}, u32[]{:S(2)}) copy-start(f32[6,16,128]{2,1,0:T(8,128)} %param.26) | copy-start | bytes 147460
  15.6 22.9 %all-to-all-start = ((f32[32,32,128]{2,1,0:T(8,128)}), f32[32,32,128]{2,1,0:T(8,128)S(1)}, u32[]{:S(2)}, u32[]{:S(2)}) async-start(f32[32,32,128]{2,1,0:T(8,128)} %bitcast.52), calls=%async_computation | async-start | bytes 1048576 | tf_op jit(solution)/shard_map/all_to_all | solution.py:516
  46.0 18.5 %copy-start.5 = (f32[6,6,16,128]{3,2,1,0:T(8,128)S(1)}, f32[6,6,16,128]{3,2,1,0:T(8,128)}, u32[]{:S(2)}) copy-start(f32[6,6,16,128]{3,2,1,0:T(8,128)} %param.22) | copy-start | bytes 884740
  46.0 18.5 %copy-start.7 = (f32[6,6,16,128]{3,2,1,0:T(8,128)S(1)}, f32[6,6,16,128]{3,2,1,0:T(8,128)}, u32[]{:S(2)}) copy-start(f32[6,6,16,128]{3,2,1,0:T(8,128)} %param.23) | copy-start | bytes 884740
  46.0 18.6 %copy-start.46 = (s32[16,128]{1,0:T(8,128)S(1)}, s32[16,128]{1,0:T(8,128)}, u32[]{:S(2)}) copy-start(s32[16,128]{1,0:T(8,128)} %refs_18_.1) | copy-start | bytes 24580
  53.8 35.3 %copy-start.29 = (f32[96,128]{1,0:T(8,128)}, f32[96,128]{1,0:T(8,128)S(1)}, u32[]{:S(2)}) copy-start(f32[96,128]{1,0:T(8,128)S(1)} %get-tuple-element.58.refs_7_.refs_15_) | copy-start | bytes 147460
  53.8 10.7 %all-to-all-start.1 = ((bf16[32,8,128]{2,1,0:T(8,128)(2,1)}), bf16[32,8,128]{2,1,0:T(8,128)(2,1)}, u32[]{:S(2)}, u32[]{:S(2)}) async-start(bf16[32,8,128]{2,1,0:T(8,128)(2,1)} %bitcast.59), calls=%async_computation.1 | async-start | bytes 131072 | tf_op jit(solution)/shard_map/all_to_all | solution.py:516
  57.1 3.6 %collective-permute-start.2 = (bf16[96,128]{1,0:T(8,128)(2,1)}, bf16[96,128]{1,0:T(8,128)(2,1)S(1)}, u32[]{:S(2)}, u32[]{:S(2)}) collective-permute-start(bf16[96,128]{1,0:T(8,128)(2,1)} %copy-done.86), channel_id=1, source_target_pairs={{0,3},{1,2},{2,1},{3,0},{4,7},{5,6},{6,5},{7,4},{8,11},{9,10},{10,... | collective-permute-start | bytes 73736 | tf_op jit(solution)/shard_map/ppermute | solution.py:522
  58.5 4.1 %collective-permute-start.1 = (bf16[96,128]{1,0:T(8,128)(2,1)}, bf16[96,128]{1,0:T(8,128)(2,1)S(1)}, u32[]{:S(2)}, u32[]{:S(2)}) collective-permute-start(bf16[96,128]{1,0:T(8,128)(2,1)} %copy-done.86), channel_id=1, source_target_pairs={{0,2},{1,3},{2,0},{3,1},{4,6},{5,7},{6,4},{7,5},{8,10},{9,11},{10,... | collective-permute-start | bytes 73736 | tf_op jit(solution)/shard_map/ppermute | solution.py:522
  58.9 4.3 %collective-permute-start = (bf16[96,128]{1,0:T(8,128)(2,1)}, bf16[96,128]{1,0:T(8,128)(2,1)S(1)}, u32[]{:S(2)}, u32[]{:S(2)}) collective-permute-start(bf16[96,128]{1,0:T(8,128)(2,1)} %copy-done.86), channel_id=1, source_target_pairs={{0,1},{1,0},{2,3},{3,2},{4,5},{5,4},{6,7},{7,6},{8,9},{9,8},{10,11... | collective-permute-start | bytes 73736 | tf_op jit(solution)/shard_map/ppermute | solution.py:522
  64.5 24.7 %copy-start.2 = (bf16[96,32,192]{2,1,0:T(8,128)(2,1)S(1)}, bf16[96,32,192]{2,1,0:T(8,128)(2,1)}, u32[]{:S(2)}) copy-start(bf16[96,32,192]{2,1,0:T(8,128)(2,1)} %param.17) | copy-start | bytes 3538948
  74.8 14.4 %copy-start.57 = (f32[96,128]{1,0:T(8,128)}, f32[96,128]{1,0:T(8,128)S(1)}, u32[]{:S(2)}) copy-start(f32[96,128]{1,0:T(8,128)S(1)} %get-tuple-element.75.refs_14_) | copy-start | bytes 147460
  74.8 14.4 %copy-start.59 = (f32[96,128]{1,0:T(8,128)}, f32[96,128]{1,0:T(8,128)S(1)}, u32[]{:S(2)}) copy-start(f32[96,128]{1,0:T(8,128)S(1)} %get-tuple-element.76.refs_15_) | copy-start | bytes 147460
  74.8 14.4 %copy-start.61 = (f32[96,128]{1,0:T(8,128)}, f32[96,128]{1,0:T(8,128)S(1)}, u32[]{:S(2)}) copy-start(f32[96,128]{1,0:T(8,128)S(1)} %get-tuple-element.73.refs_9_) | copy-start | bytes 147460
  74.8 14.4 %copy-start.63 = (f32[96,128]{1,0:T(8,128)}, f32[96,128]{1,0:T(8,128)S(1)}, u32[]{:S(2)}) copy-start(f32[96,128]{1,0:T(8,128)S(1)} %get-tuple-element.74.refs_10_) | copy-start | bytes 147460
  103.1 10.7 %all-to-all-start.3 = ((bf16[32,8,128]{2,1,0:T(8,128)(2,1)}), bf16[32,8,128]{2,1,0:T(8,128)(2,1)}, u32[]{:S(2)}, u32[]{:S(2)}) async-start(bf16[32,8,128]{2,1,0:T(8,128)(2,1)} %bitcast.58), calls=%async_computation.3 | async-start | bytes 131072 | tf_op jit(solution)/shard_map/all_to_all | solution.py:516
  106.4 3.6 %collective-permute-start.5 = (bf16[96,128]{1,0:T(8,128)(2,1)}, bf16[96,128]{1,0:T(8,128)(2,1)S(1)}, u32[]{:S(2)}, u32[]{:S(2)}) collective-permute-start(bf16[96,128]{1,0:T(8,128)(2,1)} %copy-done.84), channel_id=1, source_target_pairs={{0,3},{1,2},{2,1},{3,0},{4,7},{5,6},{6,5},{7,4},{8,11},{9,10},{10,... | collective-permute-start | bytes 73736 | tf_op jit(solution)/shard_map/ppermute | solution.py:522
  107.8 4.1 %collective-permute-start.4 = (bf16[96,128]{1,0:T(8,128)(2,1)}, bf16[96,128]{1,0:T(8,128)(2,1)S(1)}, u32[]{:S(2)}, u32[]{:S(2)}) collective-permute-start(bf16[96,128]{1,0:T(8,128)(2,1)} %copy-done.84), channel_id=1, source_target_pairs={{0,2},{1,3},{2,0},{3,1},{4,6},{5,7},{6,4},{7,5},{8,10},{9,11},{10,... | collective-permute-start | bytes 73736 | tf_op jit(solution)/shard_map/ppermute | solution.py:522
  108.1 4.3 %collective-permute-start.3 = (bf16[96,128]{1,0:T(8,128)(2,1)}, bf16[96,128]{1,0:T(8,128)(2,1)S(1)}, u32[]{:S(2)}, u32[]{:S(2)}) collective-permute-start(bf16[96,128]{1,0:T(8,128)(2,1)} %copy-done.84), channel_id=1, source_target_pairs={{0,1},{1,0},{2,3},{3,2},{4,5},{5,4},{6,7},{7,6},{8,9},{9,8},{10,11... | collective-permute-start | bytes 73736 | tf_op jit(solution)/shard_map/ppermute | solution.py:522
  113.8 26.3 %copy-start.3 = (bf16[96,32,192]{2,1,0:T(8,128)(2,1)S(1)}, bf16[96,32,192]{2,1,0:T(8,128)(2,1)}, u32[]{:S(2)}) copy-start(bf16[96,32,192]{2,1,0:T(8,128)(2,1)} %param.17) | copy-start | bytes 3538948
  125.6 14.4 %copy-start.65 = (f32[96,128]{1,0:T(8,128)}, f32[96,128]{1,0:T(8,128)S(1)}, u32[]{:S(2)}) copy-start(f32[96,128]{1,0:T(8,128)S(1)} %get-tuple-element.88.refs_14_) | copy-start | bytes 147460
  125.7 14.4 %copy-start.67 = (f32[96,128]{1,0:T(8,128)}, f32[96,128]{1,0:T(8,128)S(1)}, u32[]{:S(2)}) copy-start(f32[96,128]{1,0:T(8,128)S(1)} %get-tuple-element.89.refs_15_) | copy-start | bytes 147460
  125.7 14.4 %copy-start.69 = (f32[96,128]{1,0:T(8,128)}, f32[96,128]{1,0:T(8,128)S(1)}, u32[]{:S(2)}) copy-start(f32[96,128]{1,0:T(8,128)S(1)} %get-tuple-element.86.refs_9_) | copy-start | bytes 147460
  146.0 16.5 %copy-start.40 = (bf16[64,128]{1,0:T(8,128)(2,1)S(1)}, bf16[64,128]{1,0:T(8,128)(2,1)}, u32[]{:S(2)}) copy-start(bf16[64,128]{1,0:T(8,128)(2,1)} %copy-done.37) | copy-start | bytes 49156
  152.6 10.0 %all-to-all-start.5 = ((bf16[32,8,128]{2,1,0:T(8,128)(2,1)}), bf16[32,8,128]{2,1,0:T(8,128)(2,1)S(1)}, u32[]{:S(2)}, u32[]{:S(2)}) async-start(bf16[32,8,128]{2,1,0:T(8,128)(2,1)} %bitcast.20), calls=%async_computation.5 | async-start | bytes 131072 | tf_op jit(solution)/shard_map/all_to_all | solution.py:516
  155.1 3.4 %collective-permute-start.8 = (bf16[96,128]{1,0:T(8,128)(2,1)S(1)}, bf16[96,128]{1,0:T(8,128)(2,1)S(1)}, u32[]{:S(2)}, u32[]{:S(2)}) collective-permute-start(bf16[96,128]{1,0:T(8,128)(2,1)S(1)} %get-tuple-element.82.refs_2_), channel_id=1, source_target_pairs={{0,3},{1,2},{2,1},{3,0},{4,7},{5,6},{6,5},{7,4},{8,11},{9,10},{10,... | collective-permute-start | bytes 73736 | tf_op jit(solution)/shard_map/ppermute | solution.py:522
  156.6 3.8 %collective-permute-start.7 = (bf16[96,128]{1,0:T(8,128)(2,1)S(1)}, bf16[96,128]{1,0:T(8,128)(2,1)S(1)}, u32[]{:S(2)}, u32[]{:S(2)}) collective-permute-start(bf16[96,128]{1,0:T(8,128)(2,1)S(1)} %get-tuple-element.82.refs_2_), channel_id=1, source_target_pairs={{0,2},{1,3},{2,0},{3,1},{4,6},{5,7},{6,4},{7,5},{8,10},{9,11},{10,... | collective-permute-start | bytes 73736 | tf_op jit(solution)/shard_map/ppermute | solution.py:522
  156.9 3.5 %collective-permute-start.6 = (bf16[96,128]{1,0:T(8,128)(2,1)S(1)}, bf16[96,128]{1,0:T(8,128)(2,1)S(1)}, u32[]{:S(2)}, u32[]{:S(2)}) collective-permute-start(bf16[96,128]{1,0:T(8,128)(2,1)S(1)} %get-tuple-element.82.refs_2_), channel_id=1, source_target_pairs={{0,1},{1,0},{2,3},{3,2},{4,5},{5,4},{6,7},{7,6},{8,9},{9,8},{10,11... | collective-permute-start | bytes 73736 | tf_op jit(solution)/shard_map/ppermute | solution.py:522
  (92 other events, 91.4 us)
where the time goes:
time: 173 us; the launch traced here: 170 us
  local copies, waits for them, and re-layouts  70 us (40%)
  blocking collectives  28.7 us (17%)
  waiting for transfers between devices  27.4 us (16%)
  starting transfers between devices  22.2 us (13%)
  Pallas kernels  20.3 us (12%)
    unnamed x222, local copies, waits for them, and re-layouts  68.5 us
    all_to_all x2, blocking collectives, exchange(): lax.all_to_all(shaped, AXES, split_axis=0, concat_axis=0, tiled=True)  28.7 us
    pallas_call x7, Pallas kernels, call(): pl.pallas_call(kernel, name=name, out_shape=[jax.ShapeDtypeStruct(shape,...  20.3 us
    all_to_all x4, waiting for transfers between devices, exchange(): lax.all_to_all(shaped, AXES, split_axis=0, concat_axis=0, tiled=True)  18.2 us
    all_to_all x4, starting transfers between devices, exchange(): lax.all_to_all(shaped, AXES, split_axis=0, concat_axis=0, tiled=True)  16.5 us
    ppermute x9, waiting for transfers between devices, swap(): return lax.ppermute(value, 'lm', [(i, i ^ mask) for i in range(count)])  9.21 us
    ppermute x9, starting transfers between devices, swap(): return lax.ppermute(value, 'lm', [(i, i ^ mask) for i in range(count)])  5.78 us
  transfers between devices with their start and end apart: 13, of which 10 were waited for; matrix products, arithmetic and copies ran while one was open for 1% of the time, Pallas kernels for 0%

commit v1 on v0

--- a/solution.py
+++ b/solution.py
@@ -496,17 +496,49 @@
     )
 
 
+class Arrival:
+    def __init__(self, ref, copy):
+        self.ref, self.copy, self.shape = ref, copy, ref.shape
+
+    def __getitem__(self, index):
+        if self.copy is not None:
+            self.copy.wait()
+            self.copy = None
+        return self.ref[index]
+
+
 def call(kernel, name, outs, args, scratch):
-    vmem = pl.BlockSpec(memory_space=pltpu.VMEM)
-    smem = pl.BlockSpec(memory_space=pltpu.SMEM)
+    count, made = len(args), len(outs)
+
+    def body(*refs):
+        sources, results = refs[:count], refs[count : count + made]
+        landed = refs[count + made : 2 * count + made]
+        rest, sems = refs[2 * count + made : -1], refs[-1]
+        arrivals = []
+        for index in range(count):
+            copy = pltpu.make_async_copy(sources[index], landed[index], sems.at[index])
+            copy.start()
+            arrivals.append(Arrival(landed[index], copy))
+        place = (lax.axis_index("tm"), lax.axis_index("lm"))
+        kernel(place, *arrivals, *results, *rest)
+        for arrival in arrivals:
+            if arrival.copy is not None:
+                arrival.copy.wait()
+
+    def block(shape):
+        return pl.BlockSpec(shape, lambda step: (0,) * len(shape))
+
     return pl.pallas_call(
-        kernel,
+        body,
         name=name,
+        grid=(1,),
         out_shape=[jax.ShapeDtypeStruct(shape, dtype) for shape, dtype in outs],
-        in_specs=[smem] + [vmem] * (len(args) - 1),
-        out_specs=[vmem] * len(outs),
-        scratch_shapes=scratch,
-        compiler_params=pltpu.CompilerParams(vmem_limit_bytes=24 << 20),
+        in_specs=[pl.BlockSpec(memory_space=pl.ANY)] * count,
+        out_specs=[block(shape) for shape, _ in outs],
+        scratch_shapes=[pltpu.VMEM(arg.shape, arg.dtype) for arg in args]
+        + scratch
+        + [pltpu.SemaphoreType.DMA((count,))],
+        compiler_params=pltpu.CompilerParams(vmem_limit_bytes=67_043_328),
     )(*args)
 
 
@@ -549,7 +581,6 @@
     devices, slots, field, pairs = plan.devices, plan.slots, plan.field, plan.pairs
     square = comps * comps
 
-    place = jnp.stack([lax.axis_index("tm"), lax.axis_index("lm")]).astype(jnp.int32)
     resid = knot_right_side.reshape(field, vehicles)
     couple = couple.reshape(square * knots, vehicles)
     dinv = knot_dinv.reshape(square * knots, vehicles)
@@ -592,7 +623,7 @@
             ((9 * pairs, LANES), F32),
             ((plan.blocks, slots), BF16),
         ],
-        [place, resid, land_rhs, couple, dinv, cuts, land_pinv, land_damp, listed],
+        [resid, land_rhs, couple, dinv, cuts, land_pinv, land_damp, listed],
         items_scratch(plan.held0),
     )
     state = None
@@ -601,7 +632,7 @@
     for turn in range(ITERS):
         first, last = turn == 0, turn == ITERS - 1
         recv = exchange(send, devices)
-        args = [place, recv, zloc, onward, back, land_z, knot_damp, damp, jk, jl, links, sel, spread]
+        args = [recv, zloc, onward, back, land_z, knot_damp, damp, jk, jl, links, sel, spread]
         outs = [
             ((devices * plan.zrows, LANES), BF16),
             ((field, vehicles), BF16),
@@ -632,7 +663,7 @@
         rho, knot_dir, land_dir, _ = state
         parts = [part] + [swap(part, mask) for mask in range(1, n_lm)]
         recv = exchange(send, devices)
-        args = [place, recv] + parts
+        args = [recv] + parts
         args += [rho, knot_dir, land_dir, resid, land_resid, knot_damp, damp, pick]
         if not first:
             args += list(steps)

time: 173 us -> 119 us (0.69); the launches traced: 170 us -> 119 us
  local copies, waits for them, and re-layouts: 70 us -> 3.18 us
  Pallas kernels: 20.3 us -> 33.7 us
  other arithmetic: 0.38 us -> 2.95 us
    unnamed x222 -> x0, local copies, waits for them, and re-layouts: 68.5 us -> none
    pallas_call x7, Pallas kernels: 20.3 us -> 33.7 us  [call(): pl.pallas_call(body, name=name, grid=(1,), out_shape=[jax.ShapeDtypeStruc...]
    all_to_all x4, waiting for transfers between devices: 18.2 us -> 16.1 us  [exchange(): lax.all_to_all(shaped, AXES, split_axis=0, concat_axis=0, tiled=True)]
    ppermute x9, waiting for transfers between devices: 9.21 us -> 10.9 us  [swap(): return lax.ppermute(value, 'lm', [(i, i ^ mask) for i in range(count)])]
  transfers between devices with their start and end apart: 13 -> 13, of which waited for: 10 -> 10; matrix products, arithmetic and copies ran while one was open for 1% -> 4% of each run, Pallas kernels for 0% -> 0%
where the time goes in v1:
time: 119 us
  Pallas kernels  33.7 us (28%)
  blocking collectives  27.7 us (23%)
  waiting for transfers between devices  27.1 us (23%)
  starting transfers between devices  23.1 us (19%)
  local copies, waits for them, and re-layouts  3.18 us (3%)
  other arithmetic  2.95 us (2%)
    pallas_call x7, Pallas kernels, call(): pl.pallas_call(body, name=name, grid=(1,), out_shape=[jax.ShapeDtypeStruc...  33.7 us
    all_to_all x2, blocking collectives, exchange(): lax.all_to_all(shaped, AXES, split_axis=0, concat_axis=0, tiled=True)  27.7 us
    all_to_all x4, starting transfers between devices, exchange(): lax.all_to_all(shaped, AXES, split_axis=0, concat_axis=0, tiled=True)  17.4 us
    all_to_all x4, waiting for transfers between devices, exchange(): lax.all_to_all(shaped, AXES, split_axis=0, concat_axis=0, tiled=True)  16.1 us
    ppermute x9, waiting for transfers between devices, swap(): return lax.ppermute(value, 'lm', [(i, i ^ mask) for i in range(count)])  10.9 us
    ppermute x9, starting transfers between devices, swap(): return lax.ppermute(value, 'lm', [(i, i ^ mask) for i in range(count)])  5.78 us
  transfers between devices with their start and end apart: 13, of which 10 were waited for; matrix products, arithmetic and copies ran while one was open for 4% of the time, Pallas kernels for 0%

profile of v1, /device:TPU:0, one launch (start us, length us, event | category | flops | bytes accessed | tf_op | source)
XLA Modules:
  0.0 118.7 jit_solution(18322916388733008236)
XLA Ops:
  0.6 1.3 %reshape.200.refs_7_ = s32[1,128]{1,0:T(1,128)} reshape(s32[4,32]{1,0:T(4,128)} %bitcast.57) | data formatting | bytes 1024 | tf_op jit(solution)/shard_map/reshape | solution.py:590
  1.9 4.1 %start.1 = (f32[1024,128]{1,0:T(8,128)}, f32[96,128]{1,0:T(8,128)}, f32[576,128]{1,0:T(8,128)}, f32[576,128]{1,0:T(8,128)}, f32[96,128]{1,0:T(8,128)}, /*index=5...) custom-call(f32[96,128]{1,0:T(8,128)} %bitcast.52, f32[3,4096]{1,0:T(4,128)} %refs_1_.1, ...), custom_call_target="tpu_custom_call" | custom-call | tf_op jit(solution)/shard_map/start/pallas_call | solution.py:531
  6.0 7.5 %all-to-all-start = ((f32[32,32,128]{2,1,0:T(8,128)}), f32[32,32,128]{2,1,0:T(8,128)}, u32[]{:S(2)}, u32[]{:S(2)}) async-start(f32[32,32,128]{2,1,0:T(8,128)} %bitcast.49), calls=%async_computation | async-start | bytes 1048576 | tf_op jit(solution)/shard_map/all_to_all | solution.py:548
  13.5 0.7 fusion.1.refs_10_
  14.2 0.9 fusion.refs_11_
  15.1 0.7 fusion.14
  15.9 0.7 broadcast_in_dim.32
  16.8 0.7 lt.74
  18.4 10.7 %all-to-all-done = f32[32,32,128]{2,1,0:T(8,128)} async-done(((f32[32,32,128]{2,1,0:T(8,128)}), f32[32,32,128]{2,1,0:T(8,128)}, u32[]{:S(2)}, u32[]{:S(2)}) %all-to-all-start) | async-done | bytes 524320 | tf_op jit(solution)/shard_map/all_to_all | solution.py:548
  29.1 6.7 %product_first.1 = (bf16[256,128]{1,0:T(8,128)(2,1)}, bf16[96,128]{1,0:T(8,128)(2,1)}, f32[8,128]{1,0:T(8,128)}, f32[96,128]{1,0:T(8,128)}, f32[96,128]{1,0:T(8,...) custom-call(f32[1024,128]{1,0:T(8,128)} %bitcast.6.refs_0_, f32[96,128]{1,0:T(8,128)} %get-tuple-element.50.refs_1_, ...), custom_call_target="tpu_custom_call" | custom-call | tf_op jit(solution)/shard_map/product_first/pallas_call | solution.py:531
  35.8 3.3 %all-to-all-start.1 = ((bf16[32,8,128]{2,1,0:T(8,128)(2,1)}), bf16[32,8,128]{2,1,0:T(8,128)(2,1)}, u32[]{:S(2)}, u32[]{:S(2)}) async-start(bf16[32,8,128]{2,1,0:T(8,128)(2,1)} %bitcast.56), calls=%async_computation.1 | async-start | bytes 131072 | tf_op jit(solution)/shard_map/all_to_all | solution.py:548
  39.1 1.4 %collective-permute-start.2 = (bf16[96,128]{1,0:T(8,128)(2,1)}, bf16[96,128]{1,0:T(8,128)(2,1)}, u32[]{:S(2)}, u32[]{:S(2)}) collective-permute-start(bf16[96,128]{1,0:T(8,128)(2,1)} %get-tuple-element.56.refs_1_), channel_id=1, source_target_pairs={{0,3},{1,2},{2,1},{3,0},{4,7},{5,6},{6,5},{7,4},{8,11},{9,10},{10,... | collective-permute-start | bytes 73736 | tf_op jit(solution)/shard_map/ppermute | solution.py:554
  41.0 1.8 %collective-permute-done.2.refs_4_ = bf16[96,128]{1,0:T(8,128)(2,1)} collective-permute-done((bf16[96,128]{1,0:T(8,128)(2,1)}, bf16[96,128]{1,0:T(8,128)(2,1)}, u32[]{:S(2)}, u32[]{:S(2)}) %collective-permute-start.2) | collective-permute-done | bytes 24608 | tf_op jit(solution)/shard_map/ppermute | solution.py:554
  42.8 1.8 %collective-permute-done.1.refs_3_ = bf16[96,128]{1,0:T(8,128)(2,1)} collective-permute-done((bf16[96,128]{1,0:T(8,128)(2,1)}, bf16[96,128]{1,0:T(8,128)(2,1)}, u32[]{:S(2)}, u32[]{:S(2)}) %collective-permute-start.1) | collective-permute-done | bytes 24608 | tf_op jit(solution)/shard_map/ppermute | solution.py:554
  44.7 1.8 %all-to-all-done.1 = bf16[32,8,128]{2,1,0:T(8,128)(2,1)} async-done(((bf16[32,8,128]{2,1,0:T(8,128)(2,1)}), bf16[32,8,128]{2,1,0:T(8,128)(2,1)}, u32[]{:S(2)}, u32[]{:S(2)}) %all-to-all-start.1) | async-done | bytes 65568 | tf_op jit(solution)/shard_map/all_to_all | solution.py:548
  46.5 3.0 %update.2 = (f32[96,128]{1,0:T(8,128)}, f32[96,128]{1,0:T(8,128)}, f32[96,128]{1,0:T(8,128)}, f32[96,128]{1,0:T(8,128)}, f32[512,128]{1,0:T(8,128)}, /*index=5*/f32[96,128]{1,0:T(8,128)}, f32[96,128]{1,0:T(8,128)}) custom-call(bf16[256,128]{1,0:T(8,128)(2,1)} %bitcast.11.refs_0_, bf16[96,128]{1,0:T(8,128)(2,1)} %get-tuple-element.56.refs_1_, ...), custom_call_target="tpu_custom_call" | custom-call | tf_op jit(solution)/shard_map/update/pallas_call | solution.py:531
  49.5 13.9 %all_to_all.30 = f32[32,16,128]{2,1,0:T(8,128)} all-to-all(f32[32,16,128]{2,1,0:T(8,128)} %bitcast.51), channel_id=1, replica_groups=mesh['tm'=8,'lm'=4] {'tm','lm'}, dimensions={0} | all-to-all | bytes 524288 | tf_op jit(solution)/shard_map/all_to_all | solution.py:548
  63.3 7.4 %product.2 = (bf16[256,128]{1,0:T(8,128)(2,1)}, bf16[96,128]{1,0:T(8,128)(2,1)}, f32[8,128]{1,0:T(8,128)}, f32[96,128]{1,0:T(8,128)}, f32[96,128]{1,0:T(8,128)}, /*index=5*/f32[256,128]{1,0:T(8,128)}) custom-call(f32[512,128]{1,0:T(8,128)} %bitcast.48, f32[96,128]{1,0:T(8,128)} %get-tuple-element.64.refs_1_, f32[576,128]{1,0:T(8,128)} %get-tuple-element.51.refs_2_, ...), custom_call_target="tpu_custom_call" | custom-call | tf_op jit(solution)/shard_map/product/pallas_call | solution.py:531
  70.7 3.3 %all-to-all-start.3 = ((bf16[32,8,128]{2,1,0:T(8,128)(2,1)}), bf16[32,8,128]{2,1,0:T(8,128)(2,1)}, u32[]{:S(2)}, u32[]{:S(2)}) async-start(bf16[32,8,128]{2,1,0:T(8,128)(2,1)} %bitcast.55), calls=%async_computation.3 | async-start | bytes 131072 | tf_op jit(solution)/shard_map/all_to_all | solution.py:548
  74.0 1.4 %collective-permute-start.5 = (bf16[96,128]{1,0:T(8,128)(2,1)}, bf16[96,128]{1,0:T(8,128)(2,1)}, u32[]{:S(2)}, u32[]{:S(2)}) collective-permute-start(bf16[96,128]{1,0:T(8,128)(2,1)} %get-tuple-element.69.refs_1_), channel_id=1, source_target_pairs={{0,3},{1,2},{2,1},{3,0},{4,7},{5,6},{6,5},{7,4},{8,11},{9,10},{10,... | collective-permute-start | bytes 73736 | tf_op jit(solution)/shard_map/ppermute | solution.py:554
  76.0 1.8 %collective-permute-done.5.refs_4_ = bf16[96,128]{1,0:T(8,128)(2,1)} collective-permute-done((bf16[96,128]{1,0:T(8,128)(2,1)}, bf16[96,128]{1,0:T(8,128)(2,1)}, u32[]{:S(2)}, u32[]{:S(2)}) %collective-permute-start.5) | collective-permute-done | bytes 24608 | tf_op jit(solution)/shard_map/ppermute | solution.py:554
  77.8 1.8 %collective-permute-done.4.refs_3_ = bf16[96,128]{1,0:T(8,128)(2,1)} collective-permute-done((bf16[96,128]{1,0:T(8,128)(2,1)}, bf16[96,128]{1,0:T(8,128)(2,1)}, u32[]{:S(2)}, u32[]{:S(2)}) %collective-permute-start.4) | collective-permute-done | bytes 24608 | tf_op jit(solution)/shard_map/ppermute | solution.py:554
  79.6 1.8 %all-to-all-done.3 = bf16[32,8,128]{2,1,0:T(8,128)(2,1)} async-done(((bf16[32,8,128]{2,1,0:T(8,128)(2,1)}), bf16[32,8,128]{2,1,0:T(8,128)(2,1)}, u32[]{:S(2)}, u32[]{:S(2)}) %all-to-all-start.3) | async-done | bytes 65568 | tf_op jit(solution)/shard_map/all_to_all | solution.py:548
  81.4 3.0 %update.3 = (f32[96,128]{1,0:T(8,128)}, f32[96,128]{1,0:T(8,128)}, f32[96,128]{1,0:T(8,128)}, f32[96,128]{1,0:T(8,128)}, f32[512,128]{1,0:T(8,128)}, /*index=5*/f32[96,128]{1,0:T(8,128)}, f32[96,128]{1,0:T(8,128)}) custom-call(bf16[256,128]{1,0:T(8,128)(2,1)} %bitcast.15.refs_0_, bf16[96,128]{1,0:T(8,128)(2,1)} %get-tuple-element.69.refs_1_, ...), custom_call_target="tpu_custom_call" | custom-call | tf_op jit(solution)/shard_map/update/pallas_call | solution.py:531
  84.5 13.9 %all_to_all.31 = f32[32,16,128]{2,1,0:T(8,128)} all-to-all(f32[32,16,128]{2,1,0:T(8,128)} %bitcast.50), channel_id=1, replica_groups=mesh['tm'=8,'lm'=4] {'tm','lm'}, dimensions={0} | all-to-all | bytes 524288 | tf_op jit(solution)/shard_map/all_to_all | solution.py:548
  98.3 7.4 %product.3 = (bf16[256,128]{1,0:T(8,128)(2,1)}, bf16[96,128]{1,0:T(8,128)(2,1)}, f32[8,128]{1,0:T(8,128)}, f32[96,128]{1,0:T(8,128)}, f32[96,128]{1,0:T(8,128)}, /*index=5*/f32[256,128]{1,0:T(8,128)}) custom-call(f32[512,128]{1,0:T(8,128)} %bitcast.47, f32[96,128]{1,0:T(8,128)} %get-tuple-element.78.refs_1_, f32[576,128]{1,0:T(8,128)} %get-tuple-element.51.refs_2_, ...), custom_call_target="tpu_custom_call" | custom-call | tf_op jit(solution)/shard_map/product/pallas_call | solution.py:531
  105.7 3.3 %all-to-all-start.5 = ((bf16[32,8,128]{2,1,0:T(8,128)(2,1)}), bf16[32,8,128]{2,1,0:T(8,128)(2,1)}, u32[]{:S(2)}, u32[]{:S(2)}) async-start(bf16[32,8,128]{2,1,0:T(8,128)(2,1)} %bitcast.54), calls=%async_computation.5 | async-start | bytes 131072 | tf_op jit(solution)/shard_map/all_to_all | solution.py:548
  109.1 1.4 %collective-permute-start.8 = (bf16[96,128]{1,0:T(8,128)(2,1)}, bf16[96,128]{1,0:T(8,128)(2,1)}, u32[]{:S(2)}, u32[]{:S(2)}) collective-permute-start(bf16[96,128]{1,0:T(8,128)(2,1)} %get-tuple-element.82.refs_1_), channel_id=1, source_target_pairs={{0,3},{1,2},{2,1},{3,0},{4,7},{5,6},{6,5},{7,4},{8,11},{9,10},{10,... | collective-permute-start | bytes 73736 | tf_op jit(solution)/shard_map/ppermute | solution.py:554
  111.0 1.8 %collective-permute-done.8.refs_4_ = bf16[96,128]{1,0:T(8,128)(2,1)} collective-permute-done((bf16[96,128]{1,0:T(8,128)(2,1)}, bf16[96,128]{1,0:T(8,128)(2,1)}, u32[]{:S(2)}, u32[]{:S(2)}) %collective-permute-start.8) | collective-permute-done | bytes 24608 | tf_op jit(solution)/shard_map/ppermute | solution.py:554
  112.8 1.8 %collective-permute-done.7.refs_3_ = bf16[96,128]{1,0:T(8,128)(2,1)} collective-permute-done((bf16[96,128]{1,0:T(8,128)(2,1)}, bf16[96,128]{1,0:T(8,128)(2,1)}, u32[]{:S(2)}, u32[]{:S(2)}) %collective-permute-start.7) | collective-permute-done | bytes 24608 | tf_op jit(solution)/shard_map/ppermute | solution.py:554
  114.6 1.8 %all-to-all-done.5 = bf16[32,8,128]{2,1,0:T(8,128)(2,1)} async-done(((bf16[32,8,128]{2,1,0:T(8,128)(2,1)}), bf16[32,8,128]{2,1,0:T(8,128)(2,1)}, u32[]{:S(2)}, u32[]{:S(2)}) %all-to-all-start.5) | async-done | bytes 65568 | tf_op jit(solution)/shard_map/all_to_all | solution.py:548
  116.4 2.1 %update_last.1 = (f32[96,128]{1,0:T(8,128)}, f32[3,4096]{1,0:T(4,128)}, f32[96,128]{1,0:T(8,128)}, f32[3,4096]{1,0:T(4,128)}) custom-call(bf16[256,128]{1,0:T(8,128)(2,1)} %bitcast.19.refs_0_, bf16[96,128]{1,0:T(8,128)(2,1)} %get-tuple-element.82.refs_1_, bf16[96,128]{1,0:T(8,128)(2,1)} %collective-permute-done.6.refs_2_, ...), custom_call_target="tpu_custom_call" | custom-call | tf_op jit(solution)/shard_map/update_last/pallas_call | solution.py:531
  (19 shorter events, 2.9 us)
Async XLA Ops:
  6.0 23.1 %all-to-all-start = ((f32[32,32,128]{2,1,0:T(8,128)}), f32[32,32,128]{2,1,0:T(8,128)}, u32[]{:S(2)}, u32[]{:S(2)}) async-start(f32[32,32,128]{2,1,0:T(8,128)} %bitcast.49), calls=%async_computation | async-start | bytes 1048576 | tf_op jit(solution)/shard_map/all_to_all | solution.py:548
  35.8 10.7 %all-to-all-start.1 = ((bf16[32,8,128]{2,1,0:T(8,128)(2,1)}), bf16[32,8,128]{2,1,0:T(8,128)(2,1)}, u32[]{:S(2)}, u32[]{:S(2)}) async-start(bf16[32,8,128]{2,1,0:T(8,128)(2,1)} %bitcast.56), calls=%async_computation.1 | async-start | bytes 131072 | tf_op jit(solution)/shard_map/all_to_all | solution.py:548
  39.1 3.7 %collective-permute-start.2 = (bf16[96,128]{1,0:T(8,128)(2,1)}, bf16[96,128]{1,0:T(8,128)(2,1)}, u32[]{:S(2)}, u32[]{:S(2)}) collective-permute-start(bf16[96,128]{1,0:T(8,128)(2,1)} %get-tuple-element.56.refs_1_), channel_id=1, source_target_pairs={{0,3},{1,2},{2,1},{3,0},{4,7},{5,6},{6,5},{7,4},{8,11},{9,10},{10,... | collective-permute-start | bytes 73736 | tf_op jit(solution)/shard_map/ppermute | solution.py:554
  40.4 4.2 %collective-permute-start.1 = (bf16[96,128]{1,0:T(8,128)(2,1)}, bf16[96,128]{1,0:T(8,128)(2,1)}, u32[]{:S(2)}, u32[]{:S(2)}) collective-permute-start(bf16[96,128]{1,0:T(8,128)(2,1)} %get-tuple-element.56.refs_1_), channel_id=1, source_target_pairs={{0,2},{1,3},{2,0},{3,1},{4,6},{5,7},{6,4},{7,5},{8,10},{9,11},{10,... | collective-permute-start | bytes 73736 | tf_op jit(solution)/shard_map/ppermute | solution.py:554
  40.8 3.8 %collective-permute-start = (bf16[96,128]{1,0:T(8,128)(2,1)}, bf16[96,128]{1,0:T(8,128)(2,1)}, u32[]{:S(2)}, u32[]{:S(2)}) collective-permute-start(bf16[96,128]{1,0:T(8,128)(2,1)} %get-tuple-element.56.refs_1_), channel_id=1, source_target_pairs={{0,1},{1,0},{2,3},{3,2},{4,5},{5,4},{6,7},{7,6},{8,9},{9,8},{10,11... | collective-permute-start | bytes 73736 | tf_op jit(solution)/shard_map/ppermute | solution.py:554
  70.7 10.7 %all-to-all-start.3 = ((bf16[32,8,128]{2,1,0:T(8,128)(2,1)}), bf16[32,8,128]{2,1,0:T(8,128)(2,1)}, u32[]{:S(2)}, u32[]{:S(2)}) async-start(bf16[32,8,128]{2,1,0:T(8,128)(2,1)} %bitcast.55), calls=%async_computation.3 | async-start | bytes 131072 | tf_op jit(solution)/shard_map/all_to_all | solution.py:548
  74.0 3.7 %collective-permute-start.5 = (bf16[96,128]{1,0:T(8,128)(2,1)}, bf16[96,128]{1,0:T(8,128)(2,1)}, u32[]{:S(2)}, u32[]{:S(2)}) collective-permute-start(bf16[96,128]{1,0:T(8,128)(2,1)} %get-tuple-element.69.refs_1_), channel_id=1, source_target_pairs={{0,3},{1,2},{2,1},{3,0},{4,7},{5,6},{6,5},{7,4},{8,11},{9,10},{10,... | collective-permute-start | bytes 73736 | tf_op jit(solution)/shard_map/ppermute | solution.py:554
  75.4 4.2 %collective-permute-start.4 = (bf16[96,128]{1,0:T(8,128)(2,1)}, bf16[96,128]{1,0:T(8,128)(2,1)}, u32[]{:S(2)}, u32[]{:S(2)}) collective-permute-start(bf16[96,128]{1,0:T(8,128)(2,1)} %get-tuple-element.69.refs_1_), channel_id=1, source_target_pairs={{0,2},{1,3},{2,0},{3,1},{4,6},{5,7},{6,4},{7,5},{8,10},{9,11},{10,... | collective-permute-start | bytes 73736 | tf_op jit(solution)/shard_map/ppermute | solution.py:554
  75.8 3.8 %collective-permute-start.3 = (bf16[96,128]{1,0:T(8,128)(2,1)}, bf16[96,128]{1,0:T(8,128)(2,1)}, u32[]{:S(2)}, u32[]{:S(2)}) collective-permute-start(bf16[96,128]{1,0:T(8,128)(2,1)} %get-tuple-element.69.refs_1_), channel_id=1, source_target_pairs={{0,1},{1,0},{2,3},{3,2},{4,5},{5,4},{6,7},{7,6},{8,9},{9,8},{10,11... | collective-permute-start | bytes 73736 | tf_op jit(solution)/shard_map/ppermute | solution.py:554
  105.7 10.7 %all-to-all-start.5 = ((bf16[32,8,128]{2,1,0:T(8,128)(2,1)}), bf16[32,8,128]{2,1,0:T(8,128)(2,1)}, u32[]{:S(2)}, u32[]{:S(2)}) async-start(bf16[32,8,128]{2,1,0:T(8,128)(2,1)} %bitcast.54), calls=%async_computation.5 | async-start | bytes 131072 | tf_op jit(solution)/shard_map/all_to_all | solution.py:548
  109.1 3.7 %collective-permute-start.8 = (bf16[96,128]{1,0:T(8,128)(2,1)}, bf16[96,128]{1,0:T(8,128)(2,1)}, u32[]{:S(2)}, u32[]{:S(2)}) collective-permute-start(bf16[96,128]{1,0:T(8,128)(2,1)} %get-tuple-element.82.refs_1_), channel_id=1, source_target_pairs={{0,3},{1,2},{2,1},{3,0},{4,7},{5,6},{6,5},{7,4},{8,11},{9,10},{10,... | collective-permute-start | bytes 73736 | tf_op jit(solution)/shard_map/ppermute | solution.py:554
  110.4 4.2 %collective-permute-start.7 = (bf16[96,128]{1,0:T(8,128)(2,1)}, bf16[96,128]{1,0:T(8,128)(2,1)}, u32[]{:S(2)}, u32[]{:S(2)}) collective-permute-start(bf16[96,128]{1,0:T(8,128)(2,1)} %get-tuple-element.82.refs_1_), channel_id=1, source_target_pairs={{0,2},{1,3},{2,0},{3,1},{4,6},{5,7},{6,4},{7,5},{8,10},{9,11},{10,... | collective-permute-start | bytes 73736 | tf_op jit(solution)/shard_map/ppermute | solution.py:554
  110.8 3.8 %collective-permute-start.6 = (bf16[96,128]{1,0:T(8,128)(2,1)}, bf16[96,128]{1,0:T(8,128)(2,1)}, u32[]{:S(2)}, u32[]{:S(2)}) collective-permute-start(bf16[96,128]{1,0:T(8,128)(2,1)} %get-tuple-element.82.refs_1_), channel_id=1, source_target_pairs={{0,1},{1,0},{2,3},{3,2},{4,5},{5,4},{6,7},{7,6},{8,9},{9,8},{10,11... | collective-permute-start | bytes 73736 | tf_op jit(solution)/shard_map/ppermute | solution.py:554

commit v2 on v1

--- a/solution.py
+++ b/solution.py
@@ -75,16 +75,15 @@
     ]
 
 
-def local_sweeps(plan, resid_ref, couple_ref, dinv_ref, cuts_ref, zloc_ref, maps=None):
+def local_sweeps(plan, resid_ref, couple_ref, dinv_ref, cuts_ref, zloc_ref, maps=False):
     comps, knots = plan.comps, plan.knots
     lanes = couple_ref.shape[1]
     minus = cuts_ref[...].astype(F32) - 1.0
     carry = None
     basis = []
-    if maps is not None:
+    if maps:
         rows = lax.broadcasted_iota(jnp.int32, (comps, lanes), 0)
         basis = [(rows == b).astype(F32) for b in range(comps)]
-    eye = basis
     scaled, turned, scaled_maps = [], [], []
     energy = jnp.zeros((comps, lanes), F32)
     for k in range(knots):
@@ -99,33 +98,54 @@
         lcol = col_tiles(couple_ref, plan, k)
         gate = minus[k : k + 1]
         carry = gate * matvec(lcol, value)
-        if maps is not None:
+        if maps:
             scaled_maps.append([matvec(dcol, col) for col in basis])
             basis = [gate * matvec(lcol, col) for col in basis]
     out = carry
     total = basis
     z, u = None, None
-    onward, back = [None] * comps, eye
+    onward = [None] * comps
     for k in reversed(range(knots)):
         lrow = row_tiles(couple_ref, plan, k)
         gate = minus[k : k + 1]
         z = scaled[k] if z is None else scaled[k] + gate * matvec(lrow, z)
         u = turned[k] if u is None else turned[k] + gate * matvec(lrow, u)
         zloc_ref[pl.ds(k, comps, stride=knots), :] = z
-        if maps is not None:
-            onward_ref, back_ref = maps
+        if maps:
             onward = [
                 scaled_maps[k][b]
                 if onward[b] is None
                 else scaled_maps[k][b] + gate * matvec(lrow, onward[b])
                 for b in range(comps)
             ]
-            back = [gate * matvec(lrow, back[b]) for b in range(comps)]
-            for b in range(comps):
-                spot = pl.ds(b * knots + k, comps, stride=comps * knots)
-                onward_ref[spot, :] = onward[b]
-                back_ref[spot, :] = back[b]
     return out, z, z + u, energy, total, onward
+
+
+def maps_kernel(plan, place_ref, couple_ref, cuts_ref, dinv_ref, onward_ref, back_ref):
+    comps, knots = plan.comps, plan.knots
+    minus = cuts_ref[...].astype(F32) - 1.0
+    rows = lax.broadcasted_iota(jnp.int32, (comps, couple_ref.shape[1]), 0)
+    eye = [(rows == b).astype(F32) for b in range(comps)]
+    basis, scaled = eye, []
+    for k in range(knots):
+        dcol = col_tiles(dinv_ref, plan, k)
+        scaled.append([matvec(dcol, col) for col in basis])
+        if k + 1 < knots:
+            lcol = col_tiles(couple_ref, plan, k)
+            basis = [minus[k : k + 1] * matvec(lcol, col) for col in basis]
+    onward, back = None, eye
+    for k in reversed(range(knots)):
+        lrow = row_tiles(couple_ref, plan, k)
+        gate = minus[k : k + 1]
+        back = [gate * matvec(lrow, col) for col in back]
+        if onward is None:
+            onward = scaled[k]
+        else:
+            onward = [scaled[k][b] + gate * matvec(lrow, onward[b]) for b in range(comps)]
+        for b in range(comps):
+            spot = pl.ds(b * knots + k, comps, stride=comps * knots)
+            onward_ref[spot, :] = onward[b]
+            back_ref[spot, :] = back[b]
 
 
 def scale_land(plan, pinv_ref, land):
@@ -197,18 +217,16 @@
 def start_kernel(
     plan,
     place_ref,
+    rhs_ref,
+    damp_ref,
+    pinv_ref,
+    list_ref,
+    cuts_ref,
     resid_ref,
-    rhs_ref,
+    dinv_ref,
     couple_ref,
-    dinv_ref,
-    cuts_ref,
-    pinv_ref,
-    damp_ref,
-    list_ref,
     send_ref,
     zloc_ref,
-    onward_ref,
-    back_ref,
     land_ref,
     land_z_ref,
     land_damp_ref,
@@ -226,6 +244,7 @@
             land_pinv_ref[pl.ds(3 * a * pairs + j, 3, stride=pairs), :] = pinv_ref[a, :, cut]
     index = lax.broadcasted_iota(jnp.int32, (plan.blocks, plan.slots), 0)
     wanted = list_ref[...]
+    wanted = jnp.concatenate([wanted[c : c + 1] for c in range(plan.cap)], axis=1)
     wanted = (wanted % 2) * pairs + wanted // 2
     pick_ref[...] = (index == wanted).astype(F32).astype(BF16)
     land = [land_ref[pl.ds(a * pairs, pairs), :] for a in range(3)]
@@ -235,7 +254,7 @@
         land_z_ref[pl.ds(a * pairs, pairs), :] = land_z[a]
         energy = energy + land[a] * land_z[a]
     out, v1, v12, knot_energy, total, inner = local_sweeps(
-        plan, resid_ref, couple_ref, dinv_ref, cuts_ref, zloc_ref, (onward_ref, back_ref)
+        plan, resid_ref, couple_ref, dinv_ref, cuts_ref, zloc_ref, True
     )
     scalar = whole_sum(energy) + leader(place_ref) * whole_sum(knot_energy)
     pack_first(
@@ -246,16 +265,15 @@
 
 def product_kernel(first, plan, *refs):
     refs = list(refs)
-    place_ref, recv_ref, zloc_ref, onward_ref, back_ref, land_z_ref = refs[:6]
-    knot_damp_ref, land_damp_ref, jk_ref, jl_ref, link_ref, sel_ref, spread_ref = refs[6:13]
-    refs = refs[13:]
-    if first:
-        rw = plan.rw0
-        outs = refs
-    else:
-        rw = plan.rw
-        chain_in_ref, rho_in_ref, knot_in_ref, land_in_ref, slot_in_ref = refs[:5]
-        outs = refs[5:]
+    place_ref, recv_ref = refs[:2]
+    refs = refs[2:]
+    rw = plan.rw0 if first else plan.rw
+    if not first:
+        chain_in_ref, rho_in_ref, slot_in_ref, land_in_ref, knot_in_ref = refs[:5]
+        refs = refs[5:]
+    land_z_ref, land_damp_ref, zloc_ref, onward_ref, back_ref = refs[:5]
+    knot_damp_ref, sel_ref, spread_ref, link_ref, jl_ref, jk_ref = refs[5:11]
+    outs = refs[11:]
     send_ref, part_ref, rho_ref, knot_ref, land_ref, slot_ref = outs[:6]
     outs = outs[6:]
     if first:
@@ -417,9 +435,8 @@
 
 def update_kernel(first, last, plan, *refs):
     refs = list(refs)
-    place_ref, recv_ref = refs[:2]
-    part_refs = refs[2 : 2 + plan.n_lm]
-    refs = refs[2 + plan.n_lm :]
+    place_ref = refs[0]
+    refs = refs[1:]
     rho_ref, knot_dir_ref, land_dir_ref, knot_resid_ref, land_resid_ref = refs[:5]
     knot_damp_ref, land_damp_ref, pick_ref = refs[5:8]
     refs = refs[8:]
@@ -429,6 +446,8 @@
     if not last:
         couple_ref, dinv_ref, cuts_ref, pinv_ref = refs[:4]
         refs = refs[4:]
+    part_refs, recv_ref = refs[: plan.n_lm], refs[plan.n_lm]
+    refs = refs[plan.n_lm + 1 :]
     knot_step_out, land_step_out, knot_resid_out, land_resid_out = refs[:4]
     refs = refs[4:]
     if not last:
@@ -507,23 +526,29 @@
         return self.ref[index]
 
 
-def call(kernel, name, outs, args, scratch):
-    count, made = len(args), len(outs)
+def call(kernel, name, outs, args, scratch, loose=0, held=0):
+    count, made = len(args) - held, len(outs)
 
     def body(*refs):
-        sources, results = refs[:count], refs[count : count + made]
-        landed = refs[count + made : 2 * count + made]
-        rest, sems = refs[2 * count + made : -1], refs[-1]
+        sources, refs = refs[:count], refs[count:]
+        kept, refs = refs[:held], refs[held:]
+        results, refs = refs[:made], refs[made:]
+        landed, rest, sems = refs[:count], refs[count:-1], refs[-1]
         arrivals = []
         for index in range(count):
             copy = pltpu.make_async_copy(sources[index], landed[index], sems.at[index])
             copy.start()
             arrivals.append(Arrival(landed[index], copy))
         place = (lax.axis_index("tm"), lax.axis_index("lm"))
-        kernel(place, *arrivals, *results, *rest)
+        kernel(place, *arrivals, *kept, *results, *rest)
         for arrival in arrivals:
             if arrival.copy is not None:
                 arrival.copy.wait()
+
+    args = [
+        pltpu.with_memory_space_constraint(arg, pltpu.HBM) if loose <= index < count else arg
+        for index, arg in enumerate(args)
+    ]
 
     def block(shape):
         return pl.BlockSpec(shape, lambda step: (0,) * len(shape))
@@ -532,13 +557,15 @@
         body,
         name=name,
         grid=(1,),
-        out_shape=[jax.ShapeDtypeStruct(shape, dtype) for shape, dtype in outs],
-        in_specs=[pl.BlockSpec(memory_space=pl.ANY)] * count,
+        out_shape=[pltpu.HBM(shape, dtype) for shape, dtype in outs],
+        in_specs=[pl.BlockSpec(memory_space=pl.ANY)] * loose
+        + [pl.BlockSpec(memory_space=pltpu.HBM)] * (count - loose)
+        + [pl.BlockSpec(memory_space=pltpu.VMEM)] * held,
         out_specs=[block(shape) for shape, _ in outs],
-        scratch_shapes=[pltpu.VMEM(arg.shape, arg.dtype) for arg in args]
+        scratch_shapes=[pltpu.VMEM(arg.shape, arg.dtype) for arg in args[:count]]
         + scratch
         + [pltpu.SemaphoreType.DMA((count,))],
-        compiler_params=pltpu.CompilerParams(vmem_limit_bytes=67_043_328),
+        compiler_params=pltpu.CompilerParams(vmem_limit_bytes=24 << 20),
     )(*args)
 
 
@@ -587,7 +614,7 @@
     knot_damp = knot_damp.reshape(field, vehicles)
     jk = jac_knot.reshape(rows, knot_width)
     jl = jac_land.reshape(rows, jac_land.shape[2])
-    listed = jnp.transpose(send_list[0]).reshape(1, slots)
+    listed = jnp.transpose(send_list[0])
 
     live = jnp.arange(height, dtype=jnp.int32)[None, :] < obs_count[:, None]
     slot = (obs_slot % cap) * devices + obs_slot // cap
@@ -609,22 +636,27 @@
             pltpu.VMEM((up8(comps * held), LANES), F32),
         ]
 
-    send, zloc, onward, back, land_resid, land_z, damp, pinv, pick = call(
+    send, zloc, land_resid, land_z, damp, pinv, pick = call(
         functools.partial(start_kernel, plan),
         "start",
         [
             ((devices * plan.rw0, LANES), F32),
             ((field, vehicles), F32),
-            ((square * knots, vehicles), F32),
-            ((square * knots, vehicles), F32),
             ((3 * pairs, LANES), F32),
             ((3 * pairs, LANES), F32),
             ((3 * pairs, LANES), F32),
             ((9 * pairs, LANES), F32),
             ((plan.blocks, slots), BF16),
         ],
-        [resid, land_rhs, couple, dinv, cuts, land_pinv, land_damp, listed],
+        [land_rhs, land_damp, land_pinv, listed, cuts, resid, dinv, couple],
         items_scratch(plan.held0),
+    )
+    onward, back = call(
+        functools.partial(maps_kernel, plan),
+        "maps",
+        [((square * knots, vehicles), F32)] * 2,
+        [couple, cuts, dinv],
+        [],
     )
     state = None
     chain = None
@@ -632,7 +664,11 @@
     for turn in range(ITERS):
         first, last = turn == 0, turn == ITERS - 1
         recv = exchange(send, devices)
-        args = [recv, zloc, onward, back, land_z, knot_damp, damp, jk, jl, links, sel, spread]
+        args = [recv]
+        if not first:
+            rho, knot_dir, land_dir, slot_dir = state
+            args += [chain, rho, slot_dir, land_dir, knot_dir]
+        args += [land_z, damp, zloc, onward, back, knot_damp, sel, spread, links, jl, jk]
         outs = [
             ((devices * plan.zrows, LANES), BF16),
             ((field, vehicles), BF16),
@@ -643,8 +679,6 @@
         ]
         if first:
             outs.append(((n_tm * 2 * square, vehicles), F32))
-        else:
-            args += [chain] + list(state)
         results = call(
             functools.partial(product_kernel, first, plan),
             "product_first" if first else "product",
@@ -655,6 +689,8 @@
                 pltpu.VMEM((n_tm, 8, vehicles), F32),
                 pltpu.VMEM((devices * plan.zrows, LANES), F32),
             ],
+            loose=1,
+            held=1 if first else 2,
         )
         send, part = results[:2]
         state = results[2:6]
@@ -663,16 +699,17 @@
         rho, knot_dir, land_dir, _ = state
         parts = [part] + [swap(part, mask) for mask in range(1, n_lm)]
         recv = exchange(send, devices)
-        args = [recv] + parts
-        args += [rho, knot_dir, land_dir, resid, land_resid, knot_damp, damp, pick]
+        args = [rho, knot_dir, land_dir, resid, land_resid, knot_damp, damp, pick]
         if not first:
             args += list(steps)
         wide = pltpu.VMEM((devices * plan.zrows, LANES), F32)
+        if not last:
+            args += [couple, dinv, cuts, pinv]
+        args += parts + [recv]
         if last:
             outs = [((field, vehicles), F32), ((3, plan.land), F32)] * 2
             scratch = [wide] + [pltpu.VMEM((3 * pairs, LANES), F32)] * 2
         else:
-            args += [couple, dinv, cuts, pinv]
             outs = [((field, vehicles), F32), ((3 * pairs, LANES), F32)] * 2
             outs += [
                 ((devices * plan.rw, LANES), F32),
@@ -686,6 +723,7 @@
             outs,
             args,
             scratch,
+            held=n_lm,
         )
         steps = results[:2]
         resid, land_resid = results[2:4]

time: 119 us -> 110 us (0.924)
  local copies, waits for them, and re-layouts: 3.18 us -> 0.62 us
  starting transfers between devices: 23.1 us -> 21.3 us
  Pallas kernels: 33.7 us -> 32.1 us
  waiting for transfers between devices: 27.1 us -> 25.7 us
    all_to_all x4, starting transfers between devices: 17.4 us -> 15.5 us  [exchange(): lax.all_to_all(shaped, AXES, split_axis=0, concat_axis=0, tiled=True)]
    pallas_call x7 -> x8, Pallas kernels: 33.7 us -> 32.1 us  [call(): pl.pallas_call(body, name=name, grid=(1,), out_shape=[pltpu.HBM(shape, dt...]
    all_to_all x4, waiting for transfers between devices: 16.1 us -> 14.7 us  [exchange(): lax.all_to_all(shaped, AXES, split_axis=0, concat_axis=0, tiled=True)]
    reshape x1 -> x0, local copies, waits for them, and re-layouts: 1.27 us -> none  [on_device(): listed = jnp.transpose(send_list[0]).reshape(1, slots)]
  transfers between devices with their start and end apart: 13 -> 13, of which waited for: 10 -> 10; matrix products, arithmetic and copies ran while one was open for 4% -> 3% of each run, Pallas kernels for 0% -> 3%
where the time goes in v2:
time: 110 us
  Pallas kernels  32.1 us (29%)
  blocking collectives  26.9 us (24%)
  waiting for transfers between devices  25.7 us (23%)
  starting transfers between devices  21.3 us (19%)
  other arithmetic  2.27 us (2%)
    pallas_call x8, Pallas kernels, call(): pl.pallas_call(body, name=name, grid=(1,), out_shape=[pltpu.HBM(shape, dt...  32.1 us
    all_to_all x2, blocking collectives, exchange(): lax.all_to_all(shaped, AXES, split_axis=0, concat_axis=0, tiled=True)  26.9 us
    all_to_all x4, starting transfers between devices, exchange(): lax.all_to_all(shaped, AXES, split_axis=0, concat_axis=0, tiled=True)  15.5 us
    all_to_all x4, waiting for transfers between devices, exchange(): lax.all_to_all(shaped, AXES, split_axis=0, concat_axis=0, tiled=True)  14.7 us
    ppermute x9, waiting for transfers between devices, swap(): return lax.ppermute(value, 'lm', [(i, i ^ mask) for i in range(count)])  10.9 us
    ppermute x9, starting transfers between devices, swap(): return lax.ppermute(value, 'lm', [(i, i ^ mask) for i in range(count)])  5.8 us
  transfers between devices with their start and end apart: 13, of which 10 were waited for; matrix products, arithmetic and copies ran while one was open for 3% of the time, Pallas kernels for 3%

profile of v2, /device:TPU:0, one launch (start us, length us, event | category | flops | bytes accessed | tf_op | source)
XLA Modules:
  0.0 109.8 jit_solution(17380628113072492196)
XLA Ops:
  0.7 3.7 %start.1 = (f32[1024,128]{1,0:T(8,128)}, f32[96,128]{1,0:T(8,128)}, f32[96,128]{1,0:T(8,128)}, f32[96,128]{1,0:T(8,128)}, f32[96,128]{1,0:T(8,128)}, /*index=5*/f32[288,128]{1,0:T(8,128)}, bf16[64,128]{1,0:T(8,128)(2,1)}) custom-call(f32[3,4096]{1,0:T(4,128)} %refs_0_.1, f32[3,4096]{1,0:T(4,128)} %refs_1_.2, f32[3,3,4096]{2,1,0:T(4,128)} %refs_2_.1, ...), custom_call_target="tpu_custom_call" | custom-call | tf_op jit(solution)/shard_map/start/pallas_call | solution.py:556
  4.4 7.3 %all-to-all-start = ((f32[32,32,128]{2,1,0:T(8,128)}), f32[32,32,128]{2,1,0:T(8,128)S(1)}, u32[]{:S(2)}, u32[]{:S(2)}) async-start(f32[32,32,128]{2,1,0:T(8,128)} %bitcast.55), calls=%async_computation | async-start | bytes 1048576 | tf_op jit(solution)/shard_map/all_to_all | solution.py:575
  11.7 0.7 fusion.1.refs_7_.refs_12_
  12.4 0.9 fusion.refs_8_.refs_13_
  13.3 3.4 %maps.1 = (f32[576,128]{1,0:T(8,128)}, f32[576,128]{1,0:T(8,128)}) custom-call(f32[576,128]{1,0:T(8,128)} %bitcast.46, s32[16,128]{1,0:T(8,128)} %refs_12_.1, f32[576,128]{1,0:T(8,128)} %bitcast.42), custom_call_target="tpu_custom_call" | custom-call | tf_op jit(solution)/shard_map/maps/pallas_call | solution.py:556
  17.4 0.6 pad_add_fusion.refs_9_.refs_14_
  18.1 9.3 %all-to-all-done = f32[32,32,128]{2,1,0:T(8,128)S(1)} async-done(((f32[32,32,128]{2,1,0:T(8,128)}), f32[32,32,128]{2,1,0:T(8,128)S(1)}, u32[]{:S(2)}, u32[]{:S(2)}) %all-to-all-start) | async-done | bytes 524320 | tf_op jit(solution)/shard_map/all_to_all | solution.py:575
  27.3 5.7 %product_first.1 = (bf16[256,128]{1,0:T(8,128)(2,1)}, bf16[96,128]{1,0:T(8,128)(2,1)}, f32[8,128]{1,0:T(8,128)}, f32[96,128]{1,0:T(8,128)}, f32[96,128]{1,0:T(8,...) custom-call(f32[1024,128]{1,0:T(8,128)S(1)} %bitcast.35, f32[96,128]{1,0:T(8,128)} %get-tuple-element.50.refs_1_, ...), custom_call_target="tpu_custom_call" | custom-call | tf_op jit(solution)/shard_map/product_first/pallas_call | solution.py:556
  33.1 3.0 %all-to-all-start.1 = ((bf16[32,8,128]{2,1,0:T(8,128)(2,1)}), bf16[32,8,128]{2,1,0:T(8,128)(2,1)S(1)}, u32[]{:S(2)}, u32[]{:S(2)}) async-start(bf16[32,8,128]{2,1,0:T(8,128)(2,1)} %bitcast.62), calls=%async_computation.1 | async-start | bytes 131072 | tf_op jit(solution)/shard_map/all_to_all | solution.py:575
  36.1 1.6 %collective-permute-start.2 = (bf16[96,128]{1,0:T(8,128)(2,1)}, bf16[96,128]{1,0:T(8,128)(2,1)S(1)}, u32[]{:S(2)}, u32[]{:S(2)}) collective-permute-start(bf16[96,128]{1,0:T(8,128)(2,1)} %get-tuple-element.61.refs_12_), channel_id=1, source_target_pairs={{0,3},{1,2},{2,1},{3,0},{4,7},{5,6},{6,5},{7,4},{8,11},{9,10},{10,... | collective-permute-start | bytes 73736 | tf_op jit(solution)/shard_map/ppermute | solution.py:581
  37.6 0.4 collective-permute-start.1
  38.0 1.7 %collective-permute-done.2.refs_15_ = bf16[96,128]{1,0:T(8,128)(2,1)S(1)} collective-permute-done((bf16[96,128]{1,0:T(8,128)(2,1)}, bf16[96,128]{1,0:T(8,128)(2,1)S(1)}, u32[]{:S(2)}, u32[]{:S(2)}) %collective-permute-start.2) | collective-permute-done | bytes 24608 | tf_op jit(solution)/shard_map/ppermute | solution.py:581
  39.7 2.0 %collective-permute-done.1.refs_14_ = bf16[96,128]{1,0:T(8,128)(2,1)S(1)} collective-permute-done((bf16[96,128]{1,0:T(8,128)(2,1)}, bf16[96,128]{1,0:T(8,128)(2,1)S(1)}, u32[]{:S(2)}, u32[]{:S(2)}) %collective-permute-start.1) | collective-permute-done | bytes 24608 | tf_op jit(solution)/shard_map/ppermute | solution.py:581
  41.7 1.8 %all-to-all-done.1 = bf16[32,8,128]{2,1,0:T(8,128)(2,1)S(1)} async-done(((bf16[32,8,128]{2,1,0:T(8,128)(2,1)}), bf16[32,8,128]{2,1,0:T(8,128)(2,1)S(1)}, u32[]{:S(2)}, u32[]{:S(2)}) %all-to-all-start.1) | async-done | bytes 65568 | tf_op jit(solution)/shard_map/all_to_all | solution.py:575
  43.5 2.9 %update.2 = (f32[96,128]{1,0:T(8,128)}, f32[96,128]{1,0:T(8,128)}, f32[96,128]{1,0:T(8,128)}, f32[96,128]{1,0:T(8,128)}, f32[512,128]{1,0:T(8,128)}, /*index=5*/f32[96,128]{1,0:T(8,128)}, f32[96,128]{1,0:T(8,128)}) custom-call(f32[8,128]{1,0:T(8,128)} %get-tuple-element.55.refs_0_.refs_2_, f32[96,128]{1,0:T(8,128)} %get-tuple-element.56.refs_1_.refs_5_, ...), custom_call_target="tpu_custom_call" | custom-call | tf_op jit(solution)/shard_map/update/pallas_call | solution.py:556
  46.4 13.4 %all_to_all.30 = f32[32,16,128]{2,1,0:T(8,128)S(1)} all-to-all(f32[32,16,128]{2,1,0:T(8,128)} %bitcast.57), channel_id=1, replica_groups=mesh['tm'=8,'lm'=4] {'tm','lm'}, dimensions={0} | all-to-all | bytes 524288 | tf_op jit(solution)/shard_map/all_to_all | solution.py:575
  59.9 5.7 %product.2 = (bf16[256,128]{1,0:T(8,128)(2,1)}, bf16[96,128]{1,0:T(8,128)(2,1)}, f32[8,128]{1,0:T(8,128)}, f32[96,128]{1,0:T(8,128)}, f32[96,128]{1,0:T(8,128)}, /*index=5*/f32[256,128]{1,0:T(8,128)}) custom-call(f32[512,128]{1,0:T(8,128)S(1)} %bitcast.37, f32[576,128]{1,0:T(8,128)} %get-tuple-element.64.refs_1_, ...), custom_call_target="tpu_custom_call" | custom-call | tf_op jit(solution)/shard_map/product/pallas_call | solution.py:556
  65.5 2.6 %all-to-all-start.3 = ((bf16[32,8,128]{2,1,0:T(8,128)(2,1)}), bf16[32,8,128]{2,1,0:T(8,128)(2,1)S(1)}, u32[]{:S(2)}, u32[]{:S(2)}) async-start(bf16[32,8,128]{2,1,0:T(8,128)(2,1)} %bitcast.61), calls=%async_computation.3 | async-start | bytes 131072 | tf_op jit(solution)/shard_map/all_to_all | solution.py:575
  68.1 1.4 %collective-permute-start.5 = (bf16[96,128]{1,0:T(8,128)(2,1)}, bf16[96,128]{1,0:T(8,128)(2,1)S(1)}, u32[]{:S(2)}, u32[]{:S(2)}) collective-permute-start(bf16[96,128]{1,0:T(8,128)(2,1)} %get-tuple-element.75.refs_14_), channel_id=1, source_target_pairs={{0,3},{1,2},{2,1},{3,0},{4,7},{5,6},{6,5},{7,4},{8,11},{9,10},{10,... | collective-permute-start | bytes 73736 | tf_op jit(solution)/shard_map/ppermute | solution.py:581
  69.6 0.4 collective-permute-start.4
  70.1 1.7 %collective-permute-done.5.refs_17_ = bf16[96,128]{1,0:T(8,128)(2,1)S(1)} collective-permute-done((bf16[96,128]{1,0:T(8,128)(2,1)}, bf16[96,128]{1,0:T(8,128)(2,1)S(1)}, u32[]{:S(2)}, u32[]{:S(2)}) %collective-permute-start.5) | collective-permute-done | bytes 24608 | tf_op jit(solution)/shard_map/ppermute | solution.py:581
  71.8 1.9 %collective-permute-done.4.refs_16_ = bf16[96,128]{1,0:T(8,128)(2,1)S(1)} collective-permute-done((bf16[96,128]{1,0:T(8,128)(2,1)}, bf16[96,128]{1,0:T(8,128)(2,1)S(1)}, u32[]{:S(2)}, u32[]{:S(2)}) %collective-permute-start.4) | collective-permute-done | bytes 24608 | tf_op jit(solution)/shard_map/ppermute | solution.py:581
  73.7 1.8 %all-to-all-done.3 = bf16[32,8,128]{2,1,0:T(8,128)(2,1)S(1)} async-done(((bf16[32,8,128]{2,1,0:T(8,128)(2,1)}), bf16[32,8,128]{2,1,0:T(8,128)(2,1)S(1)}, u32[]{:S(2)}, u32[]{:S(2)}) %all-to-all-start.3) | async-done | bytes 65568 | tf_op jit(solution)/shard_map/all_to_all | solution.py:575
  75.5 3.0 %update.3 = (f32[96,128]{1,0:T(8,128)}, f32[96,128]{1,0:T(8,128)}, f32[96,128]{1,0:T(8,128)}, f32[96,128]{1,0:T(8,128)}, f32[512,128]{1,0:T(8,128)}, /*index=5*/f32[96,128]{1,0:T(8,128)}, f32[96,128]{1,0:T(8,128)}) custom-call(f32[8,128]{1,0:T(8,128)} %get-tuple-element.68.refs_0_.refs_2_, f32[96,128]{1,0:T(8,128)} %get-tuple-element.69.refs_1_.refs_5_, ...), custom_call_target="tpu_custom_call" | custom-call | tf_op jit(solution)/shard_map/update/pallas_call | solution.py:556
  78.6 13.4 %all_to_all.31 = f32[32,16,128]{2,1,0:T(8,128)S(1)} all-to-all(f32[32,16,128]{2,1,0:T(8,128)} %bitcast.56), channel_id=1, replica_groups=mesh['tm'=8,'lm'=4] {'tm','lm'}, dimensions={0} | all-to-all | bytes 524288 | tf_op jit(solution)/shard_map/all_to_all | solution.py:575
  92.0 5.7 %product.3 = (bf16[256,128]{1,0:T(8,128)(2,1)}, bf16[96,128]{1,0:T(8,128)(2,1)}, f32[8,128]{1,0:T(8,128)}, f32[96,128]{1,0:T(8,128)}, f32[96,128]{1,0:T(8,128)}, /*index=5*/f32[256,128]{1,0:T(8,128)}) custom-call(f32[512,128]{1,0:T(8,128)S(1)} %bitcast.36, f32[576,128]{1,0:T(8,128)} %get-tuple-element.64.refs_1_, ...), custom_call_target="tpu_custom_call" | custom-call | tf_op jit(solution)/shard_map/product/pallas_call | solution.py:556
  97.7 2.6 %all-to-all-start.5 = ((bf16[32,8,128]{2,1,0:T(8,128)(2,1)}), bf16[32,8,128]{2,1,0:T(8,128)(2,1)S(1)}, u32[]{:S(2)}, u32[]{:S(2)}) async-start(bf16[32,8,128]{2,1,0:T(8,128)(2,1)} %bitcast.60), calls=%async_computation.5 | async-start | bytes 131072 | tf_op jit(solution)/shard_map/all_to_all | solution.py:575
  100.3 1.4 %collective-permute-start.8 = (bf16[96,128]{1,0:T(8,128)(2,1)}, bf16[96,128]{1,0:T(8,128)(2,1)S(1)}, u32[]{:S(2)}, u32[]{:S(2)}) collective-permute-start(bf16[96,128]{1,0:T(8,128)(2,1)} %get-tuple-element.88.refs_10_), channel_id=1, source_target_pairs={{0,3},{1,2},{2,1},{3,0},{4,7},{5,6},{6,5},{7,4},{8,11},{9,10},{10,... | collective-permute-start | bytes 73736 | tf_op jit(solution)/shard_map/ppermute | solution.py:581
  102.2 1.7 %collective-permute-done.8.refs_13_ = bf16[96,128]{1,0:T(8,128)(2,1)S(1)} collective-permute-done((bf16[96,128]{1,0:T(8,128)(2,1)}, bf16[96,128]{1,0:T(8,128)(2,1)S(1)}, u32[]{:S(2)}, u32[]{:S(2)}) %collective-permute-start.8) | collective-permute-done | bytes 24608 | tf_op jit(solution)/shard_map/ppermute | solution.py:581
  103.9 1.9 %collective-permute-done.7.refs_12_ = bf16[96,128]{1,0:T(8,128)(2,1)S(1)} collective-permute-done((bf16[96,128]{1,0:T(8,128)(2,1)}, bf16[96,128]{1,0:T(8,128)(2,1)S(1)}, u32[]{:S(2)}, u32[]{:S(2)}) %collective-permute-start.7) | collective-permute-done | bytes 24608 | tf_op jit(solution)/shard_map/ppermute | solution.py:581
  105.8 1.8 %all-to-all-done.5 = bf16[32,8,128]{2,1,0:T(8,128)(2,1)S(1)} async-done(((bf16[32,8,128]{2,1,0:T(8,128)(2,1)}), bf16[32,8,128]{2,1,0:T(8,128)(2,1)S(1)}, u32[]{:S(2)}, u32[]{:S(2)}) %all-to-all-start.5) | async-done | bytes 65568 | tf_op jit(solution)/shard_map/all_to_all | solution.py:575
  107.7 2.0 %update_last.1 = (f32[96,128]{1,0:T(8,128)}, f32[3,4096]{1,0:T(4,128)}, f32[96,128]{1,0:T(8,128)}, f32[3,4096]{1,0:T(4,128)}) custom-call(f32[8,128]{1,0:T(8,128)} %get-tuple-element.81.refs_0_, f32[96,128]{1,0:T(8,128)} %get-tuple-element.82.refs_1_, f32[96,128]{1,0:T(8,128)} %get-tuple-element.83.refs_2_, f32[96,128]{1,0:T(8,128)} %get-tuple-element.84.refs_3_, ...), custom_call_target="tpu_custom_call" | custom-call | tf_op jit(solution)/shard_map/update_last/pallas_call | solution.py:556
  (31 shorter events, 1.3 us)
Async XLA Ops:
  0.6 12.7 %copy-start.5 = (s32[96]{0:T(128)S(1)}, s32[96]{0:T(128)}, u32[]{:S(2)}) copy-start(s32[96]{0:T(128)} %param.19) | copy-start | bytes 1156
  0.6 16.3 %copy-start.3 = (s32[96]{0:T(128)S(1)}, s32[96]{0:T(128)}, u32[]{:S(2)}) copy-start(s32[96]{0:T(128)} %param.18) | copy-start | bytes 1156
  0.7 16.5 %copy-start.4 = (s32[96]{0:T(128)S(1)}, s32[96]{0:T(128)}, u32[]{:S(2)}) copy-start(s32[96]{0:T(128)} %param.20) | copy-start | bytes 1156
  0.7 26.7 %copy-start = (bf16[96,32,384]{2,1,0:T(8,128)(2,1)S(1)}, bf16[96,32,384]{2,1,0:T(8,128)(2,1)}, u32[]{:S(2)}) copy-start(bf16[96,32,384]{2,1,0:T(8,128)(2,1)} %param.16) | copy-start | bytes 7077892
  4.4 23.0 %all-to-all-start = ((f32[32,32,128]{2,1,0:T(8,128)}), f32[32,32,128]{2,1,0:T(8,128)S(1)}, u32[]{:S(2)}, u32[]{:S(2)}) async-start(f32[32,32,128]{2,1,0:T(8,128)} %bitcast.55), calls=%async_computation | async-start | bytes 1048576 | tf_op jit(solution)/shard_map/all_to_all | solution.py:575
  33.1 10.4 %all-to-all-start.1 = ((bf16[32,8,128]{2,1,0:T(8,128)(2,1)}), bf16[32,8,128]{2,1,0:T(8,128)(2,1)S(1)}, u32[]{:S(2)}, u32[]{:S(2)}) async-start(bf16[32,8,128]{2,1,0:T(8,128)(2,1)} %bitcast.62), calls=%async_computation.1 | async-start | bytes 131072 | tf_op jit(solution)/shard_map/all_to_all | solution.py:575
  36.1 3.6 %collective-permute-start.2 = (bf16[96,128]{1,0:T(8,128)(2,1)}, bf16[96,128]{1,0:T(8,128)(2,1)S(1)}, u32[]{:S(2)}, u32[]{:S(2)}) collective-permute-start(bf16[96,128]{1,0:T(8,128)(2,1)} %get-tuple-element.61.refs_12_), channel_id=1, source_target_pairs={{0,3},{1,2},{2,1},{3,0},{4,7},{5,6},{6,5},{7,4},{8,11},{9,10},{10,... | collective-permute-start | bytes 73736 | tf_op jit(solution)/shard_map/ppermute | solution.py:581
  37.6 4.1 %collective-permute-start.1 = (bf16[96,128]{1,0:T(8,128)(2,1)}, bf16[96,128]{1,0:T(8,128)(2,1)S(1)}, u32[]{:S(2)}, u32[]{:S(2)}) collective-permute-start(bf16[96,128]{1,0:T(8,128)(2,1)} %get-tuple-element.61.refs_12_), channel_id=1, source_target_pairs={{0,2},{1,3},{2,0},{3,1},{4,6},{5,7},{6,4},{7,5},{8,10},{9,11},{10,... | collective-permute-start | bytes 73736 | tf_op jit(solution)/shard_map/ppermute | solution.py:581
  38.0 3.7 %collective-permute-start = (bf16[96,128]{1,0:T(8,128)(2,1)}, bf16[96,128]{1,0:T(8,128)(2,1)S(1)}, u32[]{:S(2)}, u32[]{:S(2)}) collective-permute-start(bf16[96,128]{1,0:T(8,128)(2,1)} %get-tuple-element.61.refs_12_), channel_id=1, source_target_pairs={{0,1},{1,0},{2,3},{3,2},{4,5},{5,4},{6,7},{7,6},{8,9},{9,8},{10,11... | collective-permute-start | bytes 73736 | tf_op jit(solution)/shard_map/ppermute | solution.py:581
  43.5 16.4 %copy-start.1 = (bf16[96,32,192]{2,1,0:T(8,128)(2,1)S(1)}, bf16[96,32,192]{2,1,0:T(8,128)(2,1)}, u32[]{:S(2)}) copy-start(bf16[96,32,192]{2,1,0:T(8,128)(2,1)} %param.17) | copy-start | bytes 3538948
  65.5 10.0 %all-to-all-start.3 = ((bf16[32,8,128]{2,1,0:T(8,128)(2,1)}), bf16[32,8,128]{2,1,0:T(8,128)(2,1)S(1)}, u32[]{:S(2)}, u32[]{:S(2)}) async-start(bf16[32,8,128]{2,1,0:T(8,128)(2,1)} %bitcast.61), calls=%async_computation.3 | async-start | bytes 131072 | tf_op jit(solution)/shard_map/all_to_all | solution.py:575
  68.1 3.7 %collective-permute-start.5 = (bf16[96,128]{1,0:T(8,128)(2,1)}, bf16[96,128]{1,0:T(8,128)(2,1)S(1)}, u32[]{:S(2)}, u32[]{:S(2)}) collective-permute-start(bf16[96,128]{1,0:T(8,128)(2,1)} %get-tuple-element.75.refs_14_), channel_id=1, source_target_pairs={{0,3},{1,2},{2,1},{3,0},{4,7},{5,6},{6,5},{7,4},{8,11},{9,10},{10,... | collective-permute-start | bytes 73736 | tf_op jit(solution)/shard_map/ppermute | solution.py:581
  69.6 4.1 %collective-permute-start.4 = (bf16[96,128]{1,0:T(8,128)(2,1)}, bf16[96,128]{1,0:T(8,128)(2,1)S(1)}, u32[]{:S(2)}, u32[]{:S(2)}) collective-permute-start(bf16[96,128]{1,0:T(8,128)(2,1)} %get-tuple-element.75.refs_14_), channel_id=1, source_target_pairs={{0,2},{1,3},{2,0},{3,1},{4,6},{5,7},{6,4},{7,5},{8,10},{9,11},{10,... | collective-permute-start | bytes 73736 | tf_op jit(solution)/shard_map/ppermute | solution.py:581
  69.9 3.8 %collective-permute-start.3 = (bf16[96,128]{1,0:T(8,128)(2,1)}, bf16[96,128]{1,0:T(8,128)(2,1)S(1)}, u32[]{:S(2)}, u32[]{:S(2)}) collective-permute-start(bf16[96,128]{1,0:T(8,128)(2,1)} %get-tuple-element.75.refs_14_), channel_id=1, source_target_pairs={{0,1},{1,0},{2,3},{3,2},{4,5},{5,4},{6,7},{7,6},{8,9},{9,8},{10,11... | collective-permute-start | bytes 73736 | tf_op jit(solution)/shard_map/ppermute | solution.py:581
  75.5 16.4 %copy-start.2 = (bf16[96,32,192]{2,1,0:T(8,128)(2,1)S(1)}, bf16[96,32,192]{2,1,0:T(8,128)(2,1)}, u32[]{:S(2)}) copy-start(bf16[96,32,192]{2,1,0:T(8,128)(2,1)} %param.17) | copy-start | bytes 3538948
  97.7 10.0 %all-to-all-start.5 = ((bf16[32,8,128]{2,1,0:T(8,128)(2,1)}), bf16[32,8,128]{2,1,0:T(8,128)(2,1)S(1)}, u32[]{:S(2)}, u32[]{:S(2)}) async-start(bf16[32,8,128]{2,1,0:T(8,128)(2,1)} %bitcast.60), calls=%async_computation.5 | async-start | bytes 131072 | tf_op jit(solution)/shard_map/all_to_all | solution.py:575
  100.3 3.7 %collective-permute-start.8 = (bf16[96,128]{1,0:T(8,128)(2,1)}, bf16[96,128]{1,0:T(8,128)(2,1)S(1)}, u32[]{:S(2)}, u32[]{:S(2)}) collective-permute-start(bf16[96,128]{1,0:T(8,128)(2,1)} %get-tuple-element.88.refs_10_), channel_id=1, source_target_pairs={{0,3},{1,2},{2,1},{3,0},{4,7},{5,6},{6,5},{7,4},{8,11},{9,10},{10,... | collective-permute-start | bytes 73736 | tf_op jit(solution)/shard_map/ppermute | solution.py:581
  101.7 4.1 %collective-permute-start.7 = (bf16[96,128]{1,0:T(8,128)(2,1)}, bf16[96,128]{1,0:T(8,128)(2,1)S(1)}, u32[]{:S(2)}, u32[]{:S(2)}) collective-permute-start(bf16[96,128]{1,0:T(8,128)(2,1)} %get-tuple-element.88.refs_10_), channel_id=1, source_target_pairs={{0,2},{1,3},{2,0},{3,1},{4,6},{5,7},{6,4},{7,5},{8,10},{9,11},{10,... | collective-permute-start | bytes 73736 | tf_op jit(solution)/shard_map/ppermute | solution.py:581
  102.1 3.8 %collective-permute-start.6 = (bf16[96,128]{1,0:T(8,128)(2,1)}, bf16[96,128]{1,0:T(8,128)(2,1)S(1)}, u32[]{:S(2)}, u32[]{:S(2)}) collective-permute-start(bf16[96,128]{1,0:T(8,128)(2,1)} %get-tuple-element.88.refs_10_), channel_id=1, source_target_pairs={{0,1},{1,0},{2,3},{3,2},{4,5},{5,4},{6,7},{7,6},{8,9},{9,8},{10,11... | collective-permute-start | bytes 73736 | tf_op jit(solution)/shard_map/ppermute | solution.py:581

commit v3 on v2

--- a/solution.py
+++ b/solution.py
@@ -49,16 +49,15 @@
         self.pairs = land // LANES
         self.blocks = land // LB
         self.zrows = up8(2 * cap)
-        self.items = 3
         self.items0 = 3 + 2 * comps
-        self.held = -(-self.items // n_lm)
         self.held0 = -(-self.items0 // n_lm)
-        self.rw = self.zrows + up8(comps * self.held)
         self.rw0 = self.zrows + up8(comps * self.held0)
-
-    def item_row(self, source, item, rw):
+        self.per = -(-5 * comps // n_lm)
+        self.rw = self.zrows + up8(self.per)
+
+    def item_row(self, source, item):
         holder = source * self.n_lm + item % self.n_lm
-        return holder * rw + self.zrows + self.comps * (item // self.n_lm)
+        return holder * self.rw0 + self.zrows + self.comps * (item // self.n_lm)
 
 
 def col_tiles(ref, plan, k):
@@ -175,39 +174,71 @@
     return high, mid, low
 
 
-def pack_first(plan, rw, held, pick_ref, land_z, scalar, items, place_ref, item_ref, tile_ref, send_ref):
-    devices, cap, comps = plan.devices, plan.cap, plan.comps
+def land_blocks(land_z):
     half = lower_half(land_z[0].shape)
     z0, z1, z2 = land_z
     r0, r1, r2 = roll_half(z0), roll_half(z1), roll_half(z2)
     zero = jnp.zeros_like(z0)
     first = jnp.concatenate([jnp.where(half, z0, r1), jnp.where(half, r0, z1)], axis=0)
     second = jnp.concatenate([jnp.where(half, z2, zero), jnp.where(half, r2, zero)], axis=0)
-    both = jnp.concatenate([first, second], axis=1)
-    stacked = jnp.concatenate(list(split3(both)), axis=0)
-    pick = pick_ref[...]
-    picks = jnp.concatenate([pick, pick, pick], axis=0)
-    rows = bf_dot(picks, stacked, TN)
-    spot = lax.broadcasted_iota(jnp.int32, (devices, LANES), 1) == LB
+    return jnp.concatenate([first, second], axis=1)
+
+
+def place_land(plan, rw, rows, marks, stage_ref):
+    devices, cap = plan.devices, plan.cap
+    lane = lax.broadcasted_iota(jnp.int32, (devices, LANES), 1)
     for c in range(cap):
         part = rows[c * devices : (c + 1) * devices]
         tail = part[:, LANES:]
         if c == 0:
-            tail = jnp.where(spot, scalar, tail)
-        send_ref[pl.ds(c, devices, stride=rw), :] = part[:, :LANES]
-        send_ref[pl.ds(cap + c, devices, stride=rw), :] = tail
+            for index, mark in enumerate(marks):
+                tail = jnp.where(lane == LB + index, mark, tail)
+        stage_ref[pl.ds(c, devices, stride=rw), :] = part[:, :LANES]
+        stage_ref[pl.ds(cap + c, devices, stride=rw), :] = tail
     for unused in range(2 * cap, plan.zrows):
-        send_ref[pl.ds(unused, devices, stride=rw), :] = jnp.zeros((devices, LANES), F32)
+        stage_ref[pl.ds(unused, devices, stride=rw), :] = jnp.zeros((devices, LANES), F32)
+
+
+def pack_wide(plan, pick_ref, land_z, scalar, items, place_ref, item_ref, tile_ref, send_ref):
+    rw, comps = plan.rw0, plan.comps
+    stacked = jnp.concatenate(list(split3(land_blocks(land_z))), axis=0)
+    pick = pick_ref[...]
+    rows = bf_dot(jnp.concatenate([pick, pick, pick], axis=0), stacked, TN)
+    place_land(plan, rw, rows, [scalar], send_ref)
     item_ref[...] = jnp.zeros_like(item_ref)
     for index, item in enumerate(items):
         item_ref[index, pl.ds(0, comps), :] = item
     tile_ref[...] = jnp.zeros_like(tile_ref)
     mine = place_ref[1]
-    for k in range(held):
+    for k in range(plan.held0):
         tile_ref[pl.ds(comps * k, comps), :] = item_ref[k * plan.n_lm + mine, pl.ds(0, comps), :]
     tile = tile_ref[...]
-    for d in range(devices):
+    for d in range(plan.devices):
         send_ref[pl.ds(d * rw + plan.zrows, rw - plan.zrows), :] = tile
+
+
+def pack_narrow(plan, pick_ref, land_z, scalar, items, place_ref, item_ref, stage_ref, send_ref):
+    rw, comps, per = plan.rw, plan.comps, plan.per
+    rows = bf_dot(pick_ref[...], land_blocks(land_z).astype(BF16), TN)
+    place_land(plan, rw, rows, [piece.astype(F32) for piece in split3(scalar)], stage_ref)
+    out, v1, v12 = items
+    pieces = []
+    for item in (out, v1):
+        high, low, _ = split3(item)
+        pieces += [high.astype(F32), low.astype(F32)]
+    pieces.append(v12)
+    item_ref[...] = jnp.zeros_like(item_ref)
+    for index, piece in enumerate(pieces):
+        begin = 0
+        while begin < comps:
+            flat = comps * index + begin
+            run = min(comps - begin, per - flat % per)
+            item_ref[flat // per, pl.ds(flat % per, run), :] = piece[begin : begin + run]
+            begin += run
+    tile = item_ref[place_ref[1]]
+    for d in range(plan.devices):
+        stage_ref[pl.ds(d * rw + plan.zrows, rw - plan.zrows), :] = tile
+    send_ref[...] = stage_ref[...].astype(BF16)
 
 
 def leader(place_ref):
@@ -257,8 +288,8 @@
         plan, resid_ref, couple_ref, dinv_ref, cuts_ref, zloc_ref, True
     )
     scalar = whole_sum(energy) + leader(place_ref) * whole_sum(knot_energy)
-    pack_first(
-        plan, plan.rw0, plan.held0, pick_ref, land_z, scalar, [out, v1, v12] + total + inner,
+    pack_wide(
+        plan, pick_ref, land_z, scalar, [out, v1, v12] + total + inner,
         place_ref, item_ref, tile_ref, send_ref,
     )
 
@@ -281,7 +312,8 @@
         outs = outs[1:]
     else:
         chain_ref = chain_in_ref
-    entry_ref, arrive_ref, wide_ref = outs
+    entry_ref, arrive_ref, wide_ref = outs[:3]
+    outs = outs[3:]
     comps, knots, cap, devices = plan.comps, plan.knots, plan.cap, plan.devices
     lanes = zloc_ref.shape[1]
     square = comps * comps
@@ -289,13 +321,29 @@
     if first:
         for s in range(plan.n_tm):
             for m in range(2 * comps):
-                spot = plan.item_row(s, 3 + m, rw)
+                spot = plan.item_row(s, 3 + m)
                 chain_ref[pl.ds(s * 2 * square + m * comps, comps), :] = recv_ref[
                     pl.ds(spot, comps), :
                 ]
 
-    def item(s, index):
-        return recv_ref[pl.ds(plan.item_row(s, index, rw), comps), :]
+        def item(s, index):
+            return recv_ref[pl.ds(plan.item_row(s, index), comps), :]
+
+    else:
+        got_ref, flat_ref = outs
+        got_ref[...] = recv_ref[...].astype(F32)
+        recv_ref = got_ref
+        per = plan.per
+        for d in range(devices):
+            flat_ref[pl.ds(d * per, per), :] = got_ref[pl.ds(d * rw + plan.zrows, per), :]
+
+        def item(s, index):
+            base = s * plan.n_lm * per
+            if index == 2:
+                return flat_ref[pl.ds(base + 4 * comps, comps), :]
+            begin = base + 2 * index * comps
+            high = flat_ref[pl.ds(begin, comps), :]
+            return high + flat_ref[pl.ds(begin + comps, comps), :]
 
     incoming = None
     firsts = []
@@ -333,7 +381,8 @@
     lane = lax.broadcasted_iota(jnp.int32, (devices, LANES), 1)
     tails = [recv_ref[pl.ds(cap + c, devices, stride=rw), :] for c in range(cap)]
     heads = [recv_ref[pl.ds(c, devices, stride=rw), :] for c in range(cap)]
-    rho = whole_sum(jnp.where(lane == LB, tails[0], 0.0)) + whole_sum(heat)
+    marked = (lane >= LB) & (lane < LB + (1 if first else 3))
+    rho = whole_sum(jnp.where(marked, tails[0], 0.0)) + whole_sum(heat)
     rho_ref[...] = jnp.broadcast_to(rho, rho_ref.shape)
     if not first:
         beta = rho / rho_in_ref[0:1, 0:1]
@@ -453,7 +502,7 @@
     if not last:
         send_ref, zloc_ref, land_z_ref = refs[:3]
         refs = refs[3:]
-        wide_ref, item_ref, tile_ref = refs
+        wide_ref, item_ref, stage_ref = refs
     else:
         wide_ref, step_tmp, resid_tmp = refs
     cap, devices, pairs = plan.cap, plan.devices, plan.pairs
@@ -509,9 +558,8 @@
         plan, knot_resid_out, couple_ref, dinv_ref, cuts_ref, zloc_ref
     )
     scalar = whole_sum(energy) + leader(place_ref) * whole_sum(knot_energy)
-    pack_first(
-        plan, plan.rw, plan.held, pick_ref, land_z, scalar, [out, v1, v12],
-        place_ref, item_ref, tile_ref, send_ref,
+    pack_narrow(
+        plan, pick_ref, land_z, scalar, [out, v1, v12], place_ref, item_ref, stage_ref, send_ref
     )
 
 
@@ -526,47 +574,54 @@
         return self.ref[index]
 
 
-def call(kernel, name, outs, args, scratch, loose=0, held=0):
-    count, made = len(args) - held, len(outs)
+def call(kernel, name, outs, args, scratch):
+    args = [arg if isinstance(arg, tuple) else (arg, "far") for arg in args]
+    outs = [out if len(out) == 3 else out + ("far",) for out in outs]
+    count, made = len(args), len(outs)
+    moved = [index for index in range(count) if args[index][1] != "here"]
+    values = [
+        pltpu.with_memory_space_constraint(arg, pltpu.HBM) if where == "far" else arg
+        for arg, where in args
+    ]
 
     def body(*refs):
-        sources, refs = refs[:count], refs[count:]
-        kept, refs = refs[:held], refs[held:]
+        sources, refs = list(refs[:count]), refs[count:]
         results, refs = refs[:made], refs[made:]
-        landed, rest, sems = refs[:count], refs[count:-1], refs[-1]
-        arrivals = []
-        for index in range(count):
-            copy = pltpu.make_async_copy(sources[index], landed[index], sems.at[index])
+        landed, rest, sems = refs[: len(moved)], refs[len(moved) : -1], refs[-1]
+        for spot, index in enumerate(moved):
+            copy = pltpu.make_async_copy(sources[index], landed[spot], sems.at[spot])
             copy.start()
-            arrivals.append(Arrival(landed[index], copy))
+            sources[index] = Arrival(landed[spot], copy)
         place = (lax.axis_index("tm"), lax.axis_index("lm"))
-        kernel(place, *arrivals, *kept, *results, *rest)
-        for arrival in arrivals:
-            if arrival.copy is not None:
-                arrival.copy.wait()
-
-    args = [
-        pltpu.with_memory_space_constraint(arg, pltpu.HBM) if loose <= index < count else arg
-        for index, arg in enumerate(args)
-    ]
-
-    def block(shape):
+        kernel(place, *sources, *results, *rest)
+        for index in moved:
+            if sources[index].copy is not None:
+                sources[index].copy.wait()
+
+    def entry(where):
+        space = {"here": pltpu.VMEM, "far": pltpu.HBM, "any": pl.ANY}[where]
+        return pl.BlockSpec(memory_space=space)
+
+    def block(shape, where):
+        if where == "here":
+            return entry(where)
         return pl.BlockSpec(shape, lambda step: (0,) * len(shape))
 
     return pl.pallas_call(
         body,
         name=name,
         grid=(1,),
-        out_shape=[pltpu.HBM(shape, dtype) for shape, dtype in outs],
-        in_specs=[pl.BlockSpec(memory_space=pl.ANY)] * loose
-        + [pl.BlockSpec(memory_space=pltpu.HBM)] * (count - loose)
-        + [pl.BlockSpec(memory_space=pltpu.VMEM)] * held,
-        out_specs=[block(shape) for shape, _ in outs],
-        scratch_shapes=[pltpu.VMEM(arg.shape, arg.dtype) for arg in args[:count]]
+        out_shape=[
+            (pltpu.VMEM if where == "here" else pltpu.HBM)(shape, dtype)
+            for shape, dtype, where in outs
+        ],
+        in_specs=[entry(where) for _, where in args],
+        out_specs=[block(shape, where) for shape, _, where in outs],
+        scratch_shapes=[pltpu.VMEM(args[index][0].shape, args[index][0].dtype) for index in moved]
         + scratch
-        + [pltpu.SemaphoreType.DMA((count,))],
+        + [pltpu.SemaphoreType.DMA((len(moved),))],
         compiler_params=pltpu.CompilerParams(vmem_limit_bytes=24 << 20),
-    )(*args)
+    )(*values)
 
 
 def exchange(blocks, devices):
@@ -630,26 +685,24 @@
     aim = jnp.where(spot % LANES < field, (spot % LANES) * VB + spot // LANES, -1)
     spread = (aim[:, None] == jnp.arange(knot_width, dtype=jnp.int32)[None, :]).astype(BF16)
 
-    def items_scratch(held):
-        return [
-            pltpu.VMEM((held * n_lm, 8, LANES), F32),
-            pltpu.VMEM((up8(comps * held), LANES), F32),
-        ]
 
     send, zloc, land_resid, land_z, damp, pinv, pick = call(
         functools.partial(start_kernel, plan),
         "start",
         [
             ((devices * plan.rw0, LANES), F32),
-            ((field, vehicles), F32),
-            ((3 * pairs, LANES), F32),
-            ((3 * pairs, LANES), F32),
+            ((field, vehicles), F32, "here"),
+            ((3 * pairs, LANES), F32, "here"),
+            ((3 * pairs, LANES), F32, "here"),
             ((3 * pairs, LANES), F32),
             ((9 * pairs, LANES), F32),
             ((plan.blocks, slots), BF16),
         ],
         [land_rhs, land_damp, land_pinv, listed, cuts, resid, dinv, couple],
-        items_scratch(plan.held0),
+        [
+            pltpu.VMEM((plan.held0 * n_lm, 8, LANES), F32),
+            pltpu.VMEM((up8(comps * plan.held0), LANES), F32),
+        ],
     )
     onward, back = call(
         functools.partial(maps_kernel, plan),
@@ -664,21 +717,22 @@
     for turn in range(ITERS):
         first, last = turn == 0, turn == ITERS - 1
         recv = exchange(send, devices)
-        args = [recv]
+        args = [(recv, "any" if first else "here")]
         if not first:
             rho, knot_dir, land_dir, slot_dir = state
-            args += [chain, rho, slot_dir, land_dir, knot_dir]
-        args += [land_z, damp, zloc, onward, back, knot_damp, sel, spread, links, jl, jk]
+            args += [(chain, "here"), rho]
+            args += [(value, "here") for value in (slot_dir, land_dir, knot_dir)]
+        args += [(land_z, "here"), damp, (zloc, "here"), onward, back, knot_damp, sel, spread, links, jl, (jk, "here")]
         outs = [
             ((devices * plan.zrows, LANES), BF16),
             ((field, vehicles), BF16),
             ((8, LANES), F32),
-            ((field, vehicles), F32),
-            ((3 * pairs, LANES), F32),
-            ((2 * slots, LANES), F32),
+            ((field, vehicles), F32, "here"),
+            ((3 * pairs, LANES), F32, "here"),
+            ((2 * slots, LANES), F32, "here"),
         ]
         if first:
-            outs.append(((n_tm * 2 * square, vehicles), F32))
+            outs.append(((n_tm * 2 * square, vehicles), F32, "here"))
         results = call(
             functools.partial(product_kernel, first, plan),
             "product_first" if first else "product",
@@ -688,9 +742,15 @@
                 pltpu.VMEM((n_tm, 8, vehicles), F32),
                 pltpu.VMEM((n_tm, 8, vehicles), F32),
                 pltpu.VMEM((devices * plan.zrows, LANES), F32),
-            ],
-            loose=1,
-            held=1 if first else 2,
+            ]
+            + (
+                []
+                if first
+                else [
+                    pltpu.VMEM((devices * plan.rw, LANES), F32),
+                    pltpu.VMEM((devices * plan.per, LANES), F32),
+                ]
+            ),
         )
         send, part = results[:2]
         state = results[2:6]
@@ -699,31 +759,35 @@
         rho, knot_dir, land_dir, _ = state
         parts = [part] + [swap(part, mask) for mask in range(1, n_lm)]
         recv = exchange(send, devices)
-        args = [rho, knot_dir, land_dir, resid, land_resid, knot_damp, damp, pick]
+        args = [rho, (knot_dir, "here"), (land_dir, "here")]
+        args += [(resid, "far" if first else "here"), (land_resid, "here"), knot_damp, damp, pick]
         if not first:
-            args += list(steps)
+            args += [(value, "here") for value in steps]
         wide = pltpu.VMEM((devices * plan.zrows, LANES), F32)
         if not last:
             args += [couple, dinv, cuts, pinv]
-        args += parts + [recv]
+        args += parts[:1] + [(value, "here") for value in parts[1:] + [recv]]
         if last:
             outs = [((field, vehicles), F32), ((3, plan.land), F32)] * 2
             scratch = [wide] + [pltpu.VMEM((3 * pairs, LANES), F32)] * 2
         else:
-            outs = [((field, vehicles), F32), ((3 * pairs, LANES), F32)] * 2
+            outs = [((field, vehicles), F32, "here"), ((3 * pairs, LANES), F32, "here")] * 2
             outs += [
-                ((devices * plan.rw, LANES), F32),
-                ((field, vehicles), F32),
-                ((3 * pairs, LANES), F32),
+                ((devices * plan.rw, LANES), BF16),
+                ((field, vehicles), F32, "here"),
+                ((3 * pairs, LANES), F32, "here"),
             ]
-            scratch = [wide] + items_scratch(plan.held)
+            scratch = [
+                wide,
+                pltpu.VMEM((n_lm, up8(plan.per), LANES), F32),
+                pltpu.VMEM((devices * plan.rw, LANES), F32),
+            ]
         results = call(
             functools.partial(update_kernel, first, last, plan),
             "update_last" if last else "update",
             outs,
             args,
             scratch,
-            held=n_lm,
         )
         steps = results[:2]
         resid, land_resid = results[2:4]

time: 110 us -> 105 us (0.955)
  blocking collectives: 26.9 us -> 22.1 us
    all_to_all x2, blocking collectives: 26.9 us -> 22.1 us  [exchange(): lax.all_to_all(shaped, AXES, split_axis=0, concat_axis=0, tiled=True)]
where the time goes in v3:
time: 105 us; the launch traced here: 104 us
  Pallas kernels  31.3 us (30%)
  waiting for transfers between devices  25.7 us (24%)
  blocking collectives  22.1 us (21%)
  starting transfers between devices  21.3 us (20%)
  other arithmetic  2.28 us (2%)
    pallas_call x8, Pallas kernels, call(): pl.pallas_call(body, name=name, grid=(1,), out_shape=[(pltpu.VMEM if wher...  31.3 us
    all_to_all x2, blocking collectives, exchange(): lax.all_to_all(shaped, AXES, split_axis=0, concat_axis=0, tiled=True)  22.1 us
    all_to_all x4, starting transfers between devices, exchange(): lax.all_to_all(shaped, AXES, split_axis=0, concat_axis=0, tiled=True)  15.5 us
    all_to_all x4, waiting for transfers between devices, exchange(): lax.all_to_all(shaped, AXES, split_axis=0, concat_axis=0, tiled=True)  14.7 us
    ppermute x9, waiting for transfers between devices, swap(): return lax.ppermute(value, 'lm', [(i, i ^ mask) for i in range(count)])  10.9 us
    ppermute x9, starting transfers between devices, swap(): return lax.ppermute(value, 'lm', [(i, i ^ mask) for i in range(count)])  5.8 us
  transfers between devices with their start and end apart: 13, of which 10 were waited for; matrix products, arithmetic and copies ran while one was open for 3% of the time, Pallas kernels for 3%

profile of v3, /device:TPU:0, one launch (start us, length us, event | category | flops | bytes accessed | tf_op | source)
XLA Modules:
  0.0 104.2 jit_solution(11402316272871381750)
XLA Ops:
  0.7 3.7 %start.1 = (f32[1024,128]{1,0:T(8,128)}, f32[96,128]{1,0:T(8,128)S(1)}, f32[96,128]{1,0:T(8,128)S(1)}, f32[96,128]{1,0:T(8,128)S(1)}, f32[96,128]{1,0:T(8,128)},...) custom-call(f32[3,4096]{1,0:T(4,128)} %refs_0_.1, f32[3,4096]{1,0:T(4,128)} %refs_1_.2, f32[3,3,4096]{2,1,0:T(4,128)} %refs_2_.1, ...), custom_call_target="tpu_custom_call" | custom-call | tf_op jit(solution)/shard_map/start/pallas_call | solution.py:610
  4.3 7.3 %all-to-all-start = ((f32[32,32,128]{2,1,0:T(8,128)}), f32[32,32,128]{2,1,0:T(8,128)S(1)}, u32[]{:S(2)}, u32[]{:S(2)}) async-start(f32[32,32,128]{2,1,0:T(8,128)} %bitcast.55), calls=%async_computation | async-start | bytes 1048576 | tf_op jit(solution)/shard_map/all_to_all | solution.py:630
  11.7 0.7 fusion.1.refs_7_.refs_12_
  12.4 0.9 fusion.refs_8_.refs_13_
  13.3 3.4 %maps.1 = (f32[576,128]{1,0:T(8,128)}, f32[576,128]{1,0:T(8,128)}) custom-call(f32[576,128]{1,0:T(8,128)} %bitcast.46, s32[16,128]{1,0:T(8,128)} %refs_12_.1, f32[576,128]{1,0:T(8,128)} %bitcast.42), custom_call_target="tpu_custom_call" | custom-call | tf_op jit(solution)/shard_map/maps/pallas_call | solution.py:610
  17.4 0.6 pad_add_fusion.refs_9_.refs_14_
  18.0 9.2 %all-to-all-done = f32[32,32,128]{2,1,0:T(8,128)S(1)} async-done(((f32[32,32,128]{2,1,0:T(8,128)}), f32[32,32,128]{2,1,0:T(8,128)S(1)}, u32[]{:S(2)}, u32[]{:S(2)}) %all-to-all-start) | async-done | bytes 524320 | tf_op jit(solution)/shard_map/all_to_all | solution.py:630
  27.3 5.7 %product_first.1 = (bf16[256,128]{1,0:T(8,128)(2,1)}, bf16[96,128]{1,0:T(8,128)(2,1)}, f32[8,128]{1,0:T(8,128)}, f32[96,128]{1,0:T(8,128)S(1)}, f32[96,128]{1,0:...) custom-call(f32[1024,128]{1,0:T(8,128)S(1)} %bitcast.32, f32[96,128]{1,0:T(8,128)S(1)} %get-tuple-element.50.refs_1_, ...), custom_call_target="tpu_custom_call" | custom-call | tf_op jit(solution)/shard_map/product_first/pallas_call | solution.py:610
  33.0 3.0 %all-to-all-start.1 = ((bf16[32,8,128]{2,1,0:T(8,128)(2,1)}), bf16[32,8,128]{2,1,0:T(8,128)(2,1)S(1)}, u32[]{:S(2)}, u32[]{:S(2)}) async-start(bf16[32,8,128]{2,1,0:T(8,128)(2,1)} %bitcast.62), calls=%async_computation.1 | async-start | bytes 131072 | tf_op jit(solution)/shard_map/all_to_all | solution.py:630
  36.0 1.6 %collective-permute-start.2 = (bf16[96,128]{1,0:T(8,128)(2,1)}, bf16[96,128]{1,0:T(8,128)(2,1)S(1)}, u32[]{:S(2)}, u32[]{:S(2)}) collective-permute-start(bf16[96,128]{1,0:T(8,128)(2,1)} %get-tuple-element.61.refs_12_), channel_id=1, source_target_pairs={{0,3},{1,2},{2,1},{3,0},{4,7},{5,6},{6,5},{7,4},{8,11},{9,10},{10,... | collective-permute-start | bytes 73736 | tf_op jit(solution)/shard_map/ppermute | solution.py:636
  37.5 0.4 collective-permute-start.1
  37.9 1.7 %collective-permute-done.2.refs_15_ = bf16[96,128]{1,0:T(8,128)(2,1)S(1)} collective-permute-done((bf16[96,128]{1,0:T(8,128)(2,1)}, bf16[96,128]{1,0:T(8,128)(2,1)S(1)}, u32[]{:S(2)}, u32[]{:S(2)}) %collective-permute-start.2) | collective-permute-done | bytes 24608 | tf_op jit(solution)/shard_map/ppermute | solution.py:636
  39.6 2.0 %collective-permute-done.1.refs_14_ = bf16[96,128]{1,0:T(8,128)(2,1)S(1)} collective-permute-done((bf16[96,128]{1,0:T(8,128)(2,1)}, bf16[96,128]{1,0:T(8,128)(2,1)S(1)}, u32[]{:S(2)}, u32[]{:S(2)}) %collective-permute-start.1) | collective-permute-done | bytes 24608 | tf_op jit(solution)/shard_map/ppermute | solution.py:636
  41.6 1.8 %all-to-all-done.1 = bf16[32,8,128]{2,1,0:T(8,128)(2,1)S(1)} async-done(((bf16[32,8,128]{2,1,0:T(8,128)(2,1)}), bf16[32,8,128]{2,1,0:T(8,128)(2,1)S(1)}, u32[]{:S(2)}, u32[]{:S(2)}) %all-to-all-start.1) | async-done | bytes 65568 | tf_op jit(solution)/shard_map/all_to_all | solution.py:630
  43.4 2.7 %update.2 = (f32[96,128]{1,0:T(8,128)S(1)}, f32[96,128]{1,0:T(8,128)S(1)}, f32[96,128]{1,0:T(8,128)S(1)}, f32[96,128]{1,0:T(8,128)S(1)}, bf16[512,128]{1,0:T(8,1...) custom-call(f32[8,128]{1,0:T(8,128)} %get-tuple-element.55.refs_0_.refs_2_, ...), custom_call_target="tpu_custom_call" | custom-call | tf_op jit(solution)/shard_map/update/pallas_call | solution.py:610
  46.1 11.0 %all_to_all.30 = bf16[32,16,128]{2,1,0:T(8,128)(2,1)S(1)} all-to-all(bf16[32,16,128]{2,1,0:T(8,128)(2,1)} %bitcast.59), channel_id=1, replica_groups=mesh['tm'=8,'lm'=4] {'tm','lm'}, dimensions={0} | all-to-all | bytes 262144 | tf_op jit(solution)/shard_map/all_to_all | solution.py:630
  57.1 5.7 %product.2 = (bf16[256,128]{1,0:T(8,128)(2,1)}, bf16[96,128]{1,0:T(8,128)(2,1)}, f32[8,128]{1,0:T(8,128)}, f32[96,128]{1,0:T(8,128)S(1)}, f32[96,128]{1,0:T(8,128)S(1)}, /*index=5*/f32[256,128]{1,0:T(8,128)S(1)}) custom-call(bf16[512,128]{1,0:T(8,128)(2,1)S(1)} %bitcast.34, f32[576,128]{1,0:T(8,128)S(1)} %get-tuple-element.64.refs_1_, ...), custom_call_target="tpu_custom_call" | custom-call | tf_op jit(solution)/shard_map/product/pallas_call | solution.py:610
  62.8 2.6 %all-to-all-start.3 = ((bf16[32,8,128]{2,1,0:T(8,128)(2,1)}), bf16[32,8,128]{2,1,0:T(8,128)(2,1)S(1)}, u32[]{:S(2)}, u32[]{:S(2)}) async-start(bf16[32,8,128]{2,1,0:T(8,128)(2,1)} %bitcast.61), calls=%async_computation.3 | async-start | bytes 131072 | tf_op jit(solution)/shard_map/all_to_all | solution.py:630
  65.4 1.4 %collective-permute-start.5 = (bf16[96,128]{1,0:T(8,128)(2,1)}, bf16[96,128]{1,0:T(8,128)(2,1)S(1)}, u32[]{:S(2)}, u32[]{:S(2)}) collective-permute-start(bf16[96,128]{1,0:T(8,128)(2,1)} %get-tuple-element.75.refs_14_), channel_id=1, source_target_pairs={{0,3},{1,2},{2,1},{3,0},{4,7},{5,6},{6,5},{7,4},{8,11},{9,10},{10,... | collective-permute-start | bytes 73736 | tf_op jit(solution)/shard_map/ppermute | solution.py:636
  67.3 1.7 %collective-permute-done.5.refs_17_ = bf16[96,128]{1,0:T(8,128)(2,1)S(1)} collective-permute-done((bf16[96,128]{1,0:T(8,128)(2,1)}, bf16[96,128]{1,0:T(8,128)(2,1)S(1)}, u32[]{:S(2)}, u32[]{:S(2)}) %collective-permute-start.5) | collective-permute-done | bytes 24608 | tf_op jit(solution)/shard_map/ppermute | solution.py:636
  69.1 1.9 %collective-permute-done.4.refs_16_ = bf16[96,128]{1,0:T(8,128)(2,1)S(1)} collective-permute-done((bf16[96,128]{1,0:T(8,128)(2,1)}, bf16[96,128]{1,0:T(8,128)(2,1)S(1)}, u32[]{:S(2)}, u32[]{:S(2)}) %collective-permute-start.4) | collective-permute-done | bytes 24608 | tf_op jit(solution)/shard_map/ppermute | solution.py:636
  71.0 1.8 %all-to-all-done.3 = bf16[32,8,128]{2,1,0:T(8,128)(2,1)S(1)} async-done(((bf16[32,8,128]{2,1,0:T(8,128)(2,1)}), bf16[32,8,128]{2,1,0:T(8,128)(2,1)S(1)}, u32[]{:S(2)}, u32[]{:S(2)}) %all-to-all-start.3) | async-done | bytes 65568 | tf_op jit(solution)/shard_map/all_to_all | solution.py:630
  72.8 2.6 %update.3 = (f32[96,128]{1,0:T(8,128)S(1)}, f32[96,128]{1,0:T(8,128)S(1)}, f32[96,128]{1,0:T(8,128)S(1)}, f32[96,128]{1,0:T(8,128)S(1)}, bf16[512,128]{1,0:T(8,1...) custom-call(f32[8,128]{1,0:T(8,128)} %get-tuple-element.68.refs_0_.refs_2_, ...), custom_call_target="tpu_custom_call" | custom-call | tf_op jit(solution)/shard_map/update/pallas_call | solution.py:610
  75.5 11.0 %all_to_all.31 = bf16[32,16,128]{2,1,0:T(8,128)(2,1)S(1)} all-to-all(bf16[32,16,128]{2,1,0:T(8,128)(2,1)} %bitcast.58), channel_id=1, replica_groups=mesh['tm'=8,'lm'=4] {'tm','lm'}, dimensions={0} | all-to-all | bytes 262144 | tf_op jit(solution)/shard_map/all_to_all | solution.py:630
  86.5 5.7 %product.3 = (bf16[256,128]{1,0:T(8,128)(2,1)}, bf16[96,128]{1,0:T(8,128)(2,1)}, f32[8,128]{1,0:T(8,128)}, f32[96,128]{1,0:T(8,128)S(1)}, f32[96,128]{1,0:T(8,128)S(1)}, /*index=5*/f32[256,128]{1,0:T(8,128)}) custom-call(bf16[512,128]{1,0:T(8,128)(2,1)S(1)} %bitcast.33, f32[576,128]{1,0:T(8,128)S(1)} %get-tuple-element.64.refs_1_, ...), custom_call_target="tpu_custom_call" | custom-call | tf_op jit(solution)/shard_map/product/pallas_call | solution.py:610
  92.2 2.6 %all-to-all-start.5 = ((bf16[32,8,128]{2,1,0:T(8,128)(2,1)}), bf16[32,8,128]{2,1,0:T(8,128)(2,1)S(1)}, u32[]{:S(2)}, u32[]{:S(2)}) async-start(bf16[32,8,128]{2,1,0:T(8,128)(2,1)} %bitcast.60), calls=%async_computation.5 | async-start | bytes 131072 | tf_op jit(solution)/shard_map/all_to_all | solution.py:630
  94.8 1.4 %collective-permute-start.8 = (bf16[96,128]{1,0:T(8,128)(2,1)}, bf16[96,128]{1,0:T(8,128)(2,1)S(1)}, u32[]{:S(2)}, u32[]{:S(2)}) collective-permute-start(bf16[96,128]{1,0:T(8,128)(2,1)} %get-tuple-element.88.refs_10_), channel_id=1, source_target_pairs={{0,3},{1,2},{2,1},{3,0},{4,7},{5,6},{6,5},{7,4},{8,11},{9,10},{10,... | collective-permute-start | bytes 73736 | tf_op jit(solution)/shard_map/ppermute | solution.py:636
  96.3 0.4 collective-permute-start.7
  96.8 1.7 %collective-permute-done.8.refs_13_ = bf16[96,128]{1,0:T(8,128)(2,1)S(1)} collective-permute-done((bf16[96,128]{1,0:T(8,128)(2,1)}, bf16[96,128]{1,0:T(8,128)(2,1)S(1)}, u32[]{:S(2)}, u32[]{:S(2)}) %collective-permute-start.8) | collective-permute-done | bytes 24608 | tf_op jit(solution)/shard_map/ppermute | solution.py:636
  98.5 1.9 %collective-permute-done.7.refs_12_ = bf16[96,128]{1,0:T(8,128)(2,1)S(1)} collective-permute-done((bf16[96,128]{1,0:T(8,128)(2,1)}, bf16[96,128]{1,0:T(8,128)(2,1)S(1)}, u32[]{:S(2)}, u32[]{:S(2)}) %collective-permute-start.7) | collective-permute-done | bytes 24608 | tf_op jit(solution)/shard_map/ppermute | solution.py:636
  100.4 1.8 %all-to-all-done.5 = bf16[32,8,128]{2,1,0:T(8,128)(2,1)S(1)} async-done(((bf16[32,8,128]{2,1,0:T(8,128)(2,1)}), bf16[32,8,128]{2,1,0:T(8,128)(2,1)S(1)}, u32[]{:S(2)}, u32[]{:S(2)}) %all-to-all-start.5) | async-done | bytes 65568 | tf_op jit(solution)/shard_map/all_to_all | solution.py:630
  102.2 1.8 %update_last.1 = (f32[96,128]{1,0:T(8,128)}, f32[3,4096]{1,0:T(4,128)}, f32[96,128]{1,0:T(8,128)}, f32[3,4096]{1,0:T(4,128)}) custom-call(f32[8,128]{1,0:T(8,128)} %get-tuple-element.81.refs_0_, f32[96,128]{1,0:T(8,128)S(1)} %get-tuple-element.82.refs_1_, f32[96,128]{1,0:T(8,128)S(1)} %get-tuple-element.83.refs_2_, f32[96,128]{1,0:T(8,128)S(1)} %get-tuple-element.84.refs_3_, ...), custom_call_target="tpu_custom_call" | custom-call | tf_op jit(solution)/shard_map/update_last/pallas_call | solution.py:610
  (27 shorter events, 1.3 us)
Async XLA Ops:
  0.6 12.7 %copy-start.3 = (s32[96]{0:T(128)S(1)}, s32[96]{0:T(128)}, u32[]{:S(2)}) copy-start(s32[96]{0:T(128)} %param.19) | copy-start | bytes 1156
  0.6 16.2 %copy-start.1 = (s32[96]{0:T(128)S(1)}, s32[96]{0:T(128)}, u32[]{:S(2)}) copy-start(s32[96]{0:T(128)} %param.18) | copy-start | bytes 1156
  0.7 16.4 %copy-start.2 = (s32[96]{0:T(128)S(1)}, s32[96]{0:T(128)}, u32[]{:S(2)}) copy-start(s32[96]{0:T(128)} %param.20) | copy-start | bytes 1156
  0.7 26.6 %copy-start = (bf16[96,32,384]{2,1,0:T(8,128)(2,1)S(1)}, bf16[96,32,384]{2,1,0:T(8,128)(2,1)}, u32[]{:S(2)}) copy-start(bf16[96,32,384]{2,1,0:T(8,128)(2,1)} %param.16) | copy-start | bytes 7077892
  4.3 23.0 %all-to-all-start = ((f32[32,32,128]{2,1,0:T(8,128)}), f32[32,32,128]{2,1,0:T(8,128)S(1)}, u32[]{:S(2)}, u32[]{:S(2)}) async-start(f32[32,32,128]{2,1,0:T(8,128)} %bitcast.55), calls=%async_computation | async-start | bytes 1048576 | tf_op jit(solution)/shard_map/all_to_all | solution.py:630
  33.0 10.4 %all-to-all-start.1 = ((bf16[32,8,128]{2,1,0:T(8,128)(2,1)}), bf16[32,8,128]{2,1,0:T(8,128)(2,1)S(1)}, u32[]{:S(2)}, u32[]{:S(2)}) async-start(bf16[32,8,128]{2,1,0:T(8,128)(2,1)} %bitcast.62), calls=%async_computation.1 | async-start | bytes 131072 | tf_op jit(solution)/shard_map/all_to_all | solution.py:630
  36.0 3.6 %collective-permute-start.2 = (bf16[96,128]{1,0:T(8,128)(2,1)}, bf16[96,128]{1,0:T(8,128)(2,1)S(1)}, u32[]{:S(2)}, u32[]{:S(2)}) collective-permute-start(bf16[96,128]{1,0:T(8,128)(2,1)} %get-tuple-element.61.refs_12_), channel_id=1, source_target_pairs={{0,3},{1,2},{2,1},{3,0},{4,7},{5,6},{6,5},{7,4},{8,11},{9,10},{10,... | collective-permute-start | bytes 73736 | tf_op jit(solution)/shard_map/ppermute | solution.py:636
  37.5 4.1 %collective-permute-start.1 = (bf16[96,128]{1,0:T(8,128)(2,1)}, bf16[96,128]{1,0:T(8,128)(2,1)S(1)}, u32[]{:S(2)}, u32[]{:S(2)}) collective-permute-start(bf16[96,128]{1,0:T(8,128)(2,1)} %get-tuple-element.61.refs_12_), channel_id=1, source_target_pairs={{0,2},{1,3},{2,0},{3,1},{4,6},{5,7},{6,4},{7,5},{8,10},{9,11},{10,... | collective-permute-start | bytes 73736 | tf_op jit(solution)/shard_map/ppermute | solution.py:636
  37.9 3.7 %collective-permute-start = (bf16[96,128]{1,0:T(8,128)(2,1)}, bf16[96,128]{1,0:T(8,128)(2,1)S(1)}, u32[]{:S(2)}, u32[]{:S(2)}) collective-permute-start(bf16[96,128]{1,0:T(8,128)(2,1)} %get-tuple-element.61.refs_12_), channel_id=1, source_target_pairs={{0,1},{1,0},{2,3},{3,2},{4,5},{5,4},{6,7},{7,6},{8,9},{9,8},{10,11... | collective-permute-start | bytes 73736 | tf_op jit(solution)/shard_map/ppermute | solution.py:636
  62.8 10.0 %all-to-all-start.3 = ((bf16[32,8,128]{2,1,0:T(8,128)(2,1)}), bf16[32,8,128]{2,1,0:T(8,128)(2,1)S(1)}, u32[]{:S(2)}, u32[]{:S(2)}) async-start(bf16[32,8,128]{2,1,0:T(8,128)(2,1)} %bitcast.61), calls=%async_computation.3 | async-start | bytes 131072 | tf_op jit(solution)/shard_map/all_to_all | solution.py:630
  65.4 3.7 %collective-permute-start.5 = (bf16[96,128]{1,0:T(8,128)(2,1)}, bf16[96,128]{1,0:T(8,128)(2,1)S(1)}, u32[]{:S(2)}, u32[]{:S(2)}) collective-permute-start(bf16[96,128]{1,0:T(8,128)(2,1)} %get-tuple-element.75.refs_14_), channel_id=1, source_target_pairs={{0,3},{1,2},{2,1},{3,0},{4,7},{5,6},{6,5},{7,4},{8,11},{9,10},{10,... | collective-permute-start | bytes 73736 | tf_op jit(solution)/shard_map/ppermute | solution.py:636
  66.8 4.1 %collective-permute-start.4 = (bf16[96,128]{1,0:T(8,128)(2,1)}, bf16[96,128]{1,0:T(8,128)(2,1)S(1)}, u32[]{:S(2)}, u32[]{:S(2)}) collective-permute-start(bf16[96,128]{1,0:T(8,128)(2,1)} %get-tuple-element.75.refs_14_), channel_id=1, source_target_pairs={{0,2},{1,3},{2,0},{3,1},{4,6},{5,7},{6,4},{7,5},{8,10},{9,11},{10,... | collective-permute-start | bytes 73736 | tf_op jit(solution)/shard_map/ppermute | solution.py:636
  67.2 3.8 %collective-permute-start.3 = (bf16[96,128]{1,0:T(8,128)(2,1)}, bf16[96,128]{1,0:T(8,128)(2,1)S(1)}, u32[]{:S(2)}, u32[]{:S(2)}) collective-permute-start(bf16[96,128]{1,0:T(8,128)(2,1)} %get-tuple-element.75.refs_14_), channel_id=1, source_target_pairs={{0,1},{1,0},{2,3},{3,2},{4,5},{5,4},{6,7},{7,6},{8,9},{9,8},{10,11... | collective-permute-start | bytes 73736 | tf_op jit(solution)/shard_map/ppermute | solution.py:636
  92.2 10.0 %all-to-all-start.5 = ((bf16[32,8,128]{2,1,0:T(8,128)(2,1)}), bf16[32,8,128]{2,1,0:T(8,128)(2,1)S(1)}, u32[]{:S(2)}, u32[]{:S(2)}) async-start(bf16[32,8,128]{2,1,0:T(8,128)(2,1)} %bitcast.60), calls=%async_computation.5 | async-start | bytes 131072 | tf_op jit(solution)/shard_map/all_to_all | solution.py:630
  94.8 3.7 %collective-permute-start.8 = (bf16[96,128]{1,0:T(8,128)(2,1)}, bf16[96,128]{1,0:T(8,128)(2,1)S(1)}, u32[]{:S(2)}, u32[]{:S(2)}) collective-permute-start(bf16[96,128]{1,0:T(8,128)(2,1)} %get-tuple-element.88.refs_10_), channel_id=1, source_target_pairs={{0,3},{1,2},{2,1},{3,0},{4,7},{5,6},{6,5},{7,4},{8,11},{9,10},{10,... | collective-permute-start | bytes 73736 | tf_op jit(solution)/shard_map/ppermute | solution.py:636
  96.3 4.1 %collective-permute-start.7 = (bf16[96,128]{1,0:T(8,128)(2,1)}, bf16[96,128]{1,0:T(8,128)(2,1)S(1)}, u32[]{:S(2)}, u32[]{:S(2)}) collective-permute-start(bf16[96,128]{1,0:T(8,128)(2,1)} %get-tuple-element.88.refs_10_), channel_id=1, source_target_pairs={{0,2},{1,3},{2,0},{3,1},{4,6},{5,7},{6,4},{7,5},{8,10},{9,11},{10,... | collective-permute-start | bytes 73736 | tf_op jit(solution)/shard_map/ppermute | solution.py:636
  96.6 3.8 %collective-permute-start.6 = (bf16[96,128]{1,0:T(8,128)(2,1)}, bf16[96,128]{1,0:T(8,128)(2,1)S(1)}, u32[]{:S(2)}, u32[]{:S(2)}) collective-permute-start(bf16[96,128]{1,0:T(8,128)(2,1)} %get-tuple-element.88.refs_10_), channel_id=1, source_target_pairs={{0,1},{1,0},{2,3},{3,2},{4,5},{5,4},{6,7},{7,6},{8,9},{9,8},{10,11... | collective-permute-start | bytes 73736 | tf_op jit(solution)/shard_map/ppermute | solution.py:636

commit v4 on v3

--- a/solution.py
+++ b/solution.py
@@ -49,7 +49,7 @@
         self.pairs = land // LANES
         self.blocks = land // LB
         self.zrows = up8(2 * cap)
-        self.items0 = 3 + 2 * comps
+        self.items0 = 5 + 4 * comps
         self.held0 = -(-self.items0 // n_lm)
         self.rw0 = self.zrows + up8(comps * self.held0)
         self.per = -(-5 * comps // n_lm)
@@ -199,34 +199,39 @@
         stage_ref[pl.ds(unused, devices, stride=rw), :] = jnp.zeros((devices, LANES), F32)
 
 
-def pack_wide(plan, pick_ref, land_z, scalar, items, place_ref, item_ref, tile_ref, send_ref):
+def in_pieces(items, alone):
+    pieces = []
+    for index, item in enumerate(items):
+        if index in alone:
+            pieces.append(item)
+        else:
+            high, low, _ = split3(item)
+            pieces += [high.astype(F32), low.astype(F32)]
+    return pieces
+
+
+def pack_start(plan, pick_ref, land_z, scalar, items, place_ref, item_ref, tile_ref, stage_ref, send_ref):
     rw, comps = plan.rw0, plan.comps
-    stacked = jnp.concatenate(list(split3(land_blocks(land_z))), axis=0)
-    pick = pick_ref[...]
-    rows = bf_dot(jnp.concatenate([pick, pick, pick], axis=0), stacked, TN)
-    place_land(plan, rw, rows, [scalar], send_ref)
+    rows = bf_dot(pick_ref[...], land_blocks(land_z).astype(BF16), TN)
+    place_land(plan, rw, rows, [piece.astype(F32) for piece in split3(scalar)], stage_ref)
     item_ref[...] = jnp.zeros_like(item_ref)
-    for index, item in enumerate(items):
-        item_ref[index, pl.ds(0, comps), :] = item
+    for index, piece in enumerate(in_pieces(items, (2,))):
+        item_ref[index, pl.ds(0, comps), :] = piece
     tile_ref[...] = jnp.zeros_like(tile_ref)
     mine = place_ref[1]
     for k in range(plan.held0):
         tile_ref[pl.ds(comps * k, comps), :] = item_ref[k * plan.n_lm + mine, pl.ds(0, comps), :]
     tile = tile_ref[...]
     for d in range(plan.devices):
-        send_ref[pl.ds(d * rw + plan.zrows, rw - plan.zrows), :] = tile
+        stage_ref[pl.ds(d * rw + plan.zrows, rw - plan.zrows), :] = tile
+    send_ref[...] = stage_ref[...].astype(BF16)
 
 
 def pack_narrow(plan, pick_ref, land_z, scalar, items, place_ref, item_ref, stage_ref, send_ref):
     rw, comps, per = plan.rw, plan.comps, plan.per
     rows = bf_dot(pick_ref[...], land_blocks(land_z).astype(BF16), TN)
     place_land(plan, rw, rows, [piece.astype(F32) for piece in split3(scalar)], stage_ref)
-    out, v1, v12 = items
-    pieces = []
-    for item in (out, v1):
-        high, low, _ = split3(item)
-        pieces += [high.astype(F32), low.astype(F32)]
-    pieces.append(v12)
+    pieces = in_pieces(items, (2,))
     item_ref[...] = jnp.zeros_like(item_ref)
     for index, piece in enumerate(pieces):
         begin = 0
@@ -265,6 +270,7 @@
     pick_ref,
     item_ref,
     tile_ref,
+    stage_ref,
 ):
     pairs = plan.pairs
     for j in range(pairs):
@@ -288,9 +294,9 @@
         plan, resid_ref, couple_ref, dinv_ref, cuts_ref, zloc_ref, True
     )
     scalar = whole_sum(energy) + leader(place_ref) * whole_sum(knot_energy)
-    pack_wide(
+    pack_start(
         plan, pick_ref, land_z, scalar, [out, v1, v12] + total + inner,
-        place_ref, item_ref, tile_ref, send_ref,
+        place_ref, item_ref, tile_ref, stage_ref, send_ref,
     )
 
 
@@ -303,8 +309,8 @@
         chain_in_ref, rho_in_ref, slot_in_ref, land_in_ref, knot_in_ref = refs[:5]
         refs = refs[5:]
     land_z_ref, land_damp_ref, zloc_ref, onward_ref, back_ref = refs[:5]
-    knot_damp_ref, sel_ref, spread_ref, link_ref, jl_ref, jk_ref = refs[5:11]
-    outs = refs[11:]
+    knot_damp_ref, sel_ref, link_ref, jl_ref, jk_ref = refs[5:10]
+    outs = refs[10:]
     send_ref, part_ref, rho_ref, knot_ref, land_ref, slot_ref = outs[:6]
     outs = outs[6:]
     if first:
@@ -318,21 +324,26 @@
     lanes = zloc_ref.shape[1]
     square = comps * comps
 
+    got_ref = outs[0]
+    got_ref[...] = recv_ref[...].astype(F32)
+    recv_ref = got_ref
     if first:
+
+        def piece(s, index):
+            return got_ref[pl.ds(plan.item_row(s, index), comps), :]
+
+        def item(s, index):
+            if index == 2:
+                return piece(s, 4)
+            spot = 2 * index if index < 2 else 2 * index - 1
+            return piece(s, spot) + piece(s, spot + 1)
+
         for s in range(plan.n_tm):
             for m in range(2 * comps):
-                spot = plan.item_row(s, 3 + m)
-                chain_ref[pl.ds(s * 2 * square + m * comps, comps), :] = recv_ref[
-                    pl.ds(spot, comps), :
-                ]
-
-        def item(s, index):
-            return recv_ref[pl.ds(plan.item_row(s, index), comps), :]
+                chain_ref[pl.ds(s * 2 * square + m * comps, comps), :] = item(s, 3 + m)
 
     else:
-        got_ref, flat_ref = outs
-        got_ref[...] = recv_ref[...].astype(F32)
-        recv_ref = got_ref
+        flat_ref = outs[1]
         per = plan.per
         for d in range(devices):
             flat_ref[pl.ds(d * per, per), :] = got_ref[pl.ds(d * rw + plan.zrows, per), :]
@@ -381,7 +392,7 @@
     lane = lax.broadcasted_iota(jnp.int32, (devices, LANES), 1)
     tails = [recv_ref[pl.ds(cap + c, devices, stride=rw), :] for c in range(cap)]
     heads = [recv_ref[pl.ds(c, devices, stride=rw), :] for c in range(cap)]
-    marked = (lane >= LB) & (lane < LB + (1 if first else 3))
+    marked = (lane >= LB) & (lane < LB + 3)
     rho = whole_sum(jnp.where(marked, tails[0], 0.0)) + whole_sum(heat)
     rho_ref[...] = jnp.broadcast_to(rho, rho_ref.shape)
     if not first:
@@ -417,13 +428,10 @@
     heat = heat + leader(place_ref) * whole_sum(knot_damp_ref[...] * knot_dir * knot_dir)
 
     groups = lanes // VB
-    narrow = knot_dir.astype(BF16)
-    padded = jnp.concatenate([narrow, jnp.zeros((LANES - plan.field, lanes), BF16)], axis=0)
-    turned = bf_dot(sel_ref[...], padded, NT).astype(BF16)
-    joined = jnp.concatenate(
+    turned = bf_dot(sel_ref[...], knot_dir.astype(BF16), NT)
+    knot_rows = jnp.concatenate(
         [turned[i * groups : (i + 1) * groups] for i in range(VB)], axis=1
-    )
-    knot_rows = bf_dot(joined, spread_ref[...], NN).astype(BF16)
+    ).astype(BF16)
     slot_rows = jnp.concatenate(
         [
             jnp.concatenate(slot_dir[:cap], axis=0).astype(BF16),
@@ -431,13 +439,20 @@
         ],
         axis=1,
     )
-    chunk = 512
+    chunk = plan.rows // 3 if plan.rows % (3 * LANES) == 0 else plan.rows
     knot_total, land_total = None, None
+
+    def ahead(start):
+        cut = pl.ds(start, chunk)
+        near = bf_dot(knot_rows, jk_ref[cut, :], NT)
+        return near, bf_dot(slot_rows, jl_ref[cut, :], NT)
+
+    ready = ahead(0)
     for start in range(0, plan.rows, chunk):
+        near, far = ready
+        if start + chunk < plan.rows:
+            ready = ahead(start + chunk)
         cut = pl.ds(start, chunk)
-        jk, jl = jk_ref[cut, :], jl_ref[cut, :]
-        near = bf_dot(knot_rows, jk, NT)
-        far = bf_dot(slot_rows, jl, NT)
         knot_hit = lax.broadcasted_iota(jnp.int32, near.shape, 0) == link_ref[0:1, cut]
         slot_hit = lax.broadcasted_iota(jnp.int32, far.shape, 0) == link_ref[1:2, cut]
         resid = jnp.sum(jnp.where(knot_hit, near, 0.0), axis=0, keepdims=True) + jnp.sum(
@@ -445,16 +460,15 @@
         )
         knot_side = jnp.where(knot_hit, resid, 0.0).astype(BF16)
         slot_side = jnp.where(slot_hit, resid, 0.0).astype(BF16)
-        knot_term = bf_dot(knot_side, jk, NN)
-        land_term = bf_dot(slot_side, jl, NN)
+        knot_term = bf_dot(knot_side, jk_ref[cut, :], NN)
+        land_term = bf_dot(slot_side, jl_ref[cut, :], NN)
         knot_total = knot_term if knot_total is None else knot_total + knot_term
         land_total = land_term if land_total is None else land_total + land_term
 
-    parted = bf_dot(knot_total.astype(BF16), spread_ref[...], NT).astype(BF16)
     piled = jnp.concatenate(
-        [parted[:, i * LANES : (i + 1) * LANES] for i in range(VB)], axis=0
-    )
-    part = bf_dot(piled, sel_ref[...], TN)[: plan.field]
+        [knot_total[:, i * plan.field : (i + 1) * plan.field] for i in range(VB)], axis=0
+    ).astype(BF16)
+    part = bf_dot(piled, sel_ref[...], TN)
     part_ref[...] = part.astype(BF16)
     heat = heat + whole_sum(part * knot_dir)
     land_total = land_total.astype(BF16).astype(F32)
@@ -480,6 +494,13 @@
         wide_ref[pl.ds(c, devices, stride=plan.zrows), :] = lead_rows[cut]
         wide_ref[pl.ds(cap + c, devices, stride=plan.zrows), :] = tail
     send_ref[...] = wide_ref[...].astype(BF16)
+
+
+def order_kernel(plan, place_ref, order_ref, jk_ref, out_ref):
+    chunk = 512
+    for start in range(0, plan.rows, chunk):
+        cut = pl.ds(start, chunk)
+        out_ref[cut, :] = bf_dot(jk_ref[cut, :], order_ref[...], NT).astype(BF16)
 
 
 def update_kernel(first, last, plan, *refs):
@@ -681,16 +702,15 @@
     lane = jnp.arange(vehicles, dtype=jnp.int32)
     ordered = (lane % groups) * VB + lane // groups
     sel = (ordered[:, None] == lane[None, :]).astype(BF16)
-    spot = jnp.arange(VB * LANES, dtype=jnp.int32)
-    aim = jnp.where(spot % LANES < field, (spot % LANES) * VB + spot // LANES, -1)
-    spread = (aim[:, None] == jnp.arange(knot_width, dtype=jnp.int32)[None, :]).astype(BF16)
-
+    spot = jnp.arange(knot_width, dtype=jnp.int32)
+    aim = (spot % field) * VB + spot // field
+    order = (aim[:, None] == spot[None, :]).astype(BF16)
 
     send, zloc, land_resid, land_z, damp, pinv, pick = call(
         functools.partial(start_kernel, plan),
         "start",
         [
-            ((devices * plan.rw0, LANES), F32),
+            ((devices * plan.rw0, LANES), BF16),
             ((field, vehicles), F32, "here"),
             ((3 * pairs, LANES), F32, "here"),
             ((3 * pairs, LANES), F32, "here"),
@@ -702,6 +722,7 @@
         [
             pltpu.VMEM((plan.held0 * n_lm, 8, LANES), F32),
             pltpu.VMEM((up8(comps * plan.held0), LANES), F32),
+            pltpu.VMEM((devices * plan.rw0, LANES), F32),
         ],
     )
     onward, back = call(
@@ -709,6 +730,13 @@
         "maps",
         [((square * knots, vehicles), F32)] * 2,
         [couple, cuts, dinv],
+        [],
+    )
+    (jk,) = call(
+        functools.partial(order_kernel, plan),
+        "order",
+        [((rows, knot_width), BF16, "here")],
+        [order, jk],
         [],
     )
     state = None
@@ -722,7 +750,7 @@
             rho, knot_dir, land_dir, slot_dir = state
             args += [(chain, "here"), rho]
             args += [(value, "here") for value in (slot_dir, land_dir, knot_dir)]
-        args += [(land_z, "here"), damp, (zloc, "here"), onward, back, knot_damp, sel, spread, links, jl, (jk, "here")]
+        args += [(land_z, "here"), damp, (zloc, "here"), onward, back, knot_damp, sel, links, jl, (jk, "here")]
         outs = [
             ((devices * plan.zrows, LANES), BF16),
             ((field, vehicles), BF16),
@@ -743,14 +771,10 @@
                 pltpu.VMEM((n_tm, 8, vehicles), F32),
                 pltpu.VMEM((devices * plan.zrows, LANES), F32),
             ]
-            + (
-                []
-                if first
-                else [
-                    pltpu.VMEM((devices * plan.rw, LANES), F32),
-                    pltpu.VMEM((devices * plan.per, LANES), F32),
-                ]
-            ),
+            + [
+                pltpu.VMEM((devices * (plan.rw0 if first else plan.rw), LANES), F32),
+                pltpu.VMEM((devices * plan.per, LANES), F32),
+            ],
         )
         send, part = results[:2]
         state = results[2:6]

time: 105 us -> 101 us (0.962)
  waiting for transfers between devices: 25.7 us -> 20.9 us
    all_to_all x4, waiting for transfers between devices: 14.7 us -> 10.1 us  [exchange(): lax.all_to_all(shaped, AXES, split_axis=0, concat_axis=0, tiled=True)]
    pallas_call x8 -> x9, Pallas kernels: 31.3 us -> 32 us  [call(): pl.pallas_call(body, name=name, grid=(1,), out_shape=[(pltpu.VMEM if wher...]
  transfers between devices with their start and end apart: 13 -> 13, of which waited for: 10 -> 10; matrix products, arithmetic and copies ran while one was open for 3% -> 3% of each run, Pallas kernels for 3% -> 7%
where the time goes in v4:
time: 101 us; the launch traced here: 100 us
  Pallas kernels  32 us (32%)
  blocking collectives  22.1 us (22%)
  starting transfers between devices  21.2 us (21%)
  waiting for transfers between devices  20.9 us (21%)
  other arithmetic  2.24 us (2%)
  between operations  1.01 us (1%)
    pallas_call x9, Pallas kernels, call(): pl.pallas_call(body, name=name, grid=(1,), out_shape=[(pltpu.VMEM if wher...  32 us
    all_to_all x2, blocking collectives, exchange(): lax.all_to_all(shaped, AXES, split_axis=0, concat_axis=0, tiled=True)  22.1 us
    all_to_all x4, starting transfers between devices, exchange(): lax.all_to_all(shaped, AXES, split_axis=0, concat_axis=0, tiled=True)  15.4 us
    ppermute x9, waiting for transfers between devices, swap(): return lax.ppermute(value, 'lm', [(i, i ^ mask) for i in range(count)])  10.8 us
    all_to_all x4, waiting for transfers between devices, exchange(): lax.all_to_all(shaped, AXES, split_axis=0, concat_axis=0, tiled=True)  10.1 us
    ppermute x9, starting transfers between devices, swap(): return lax.ppermute(value, 'lm', [(i, i ^ mask) for i in range(count)])  5.8 us
  transfers between devices with their start and end apart: 13, of which 10 were waited for; matrix products, arithmetic and copies ran while one was open for 3% of the time, Pallas kernels for 7%

profile of v4, /device:TPU:0, one launch (start us, length us, event | category | flops | bytes accessed | tf_op | source)
XLA Modules:
  0.0 100.1 jit_solution(9729225526829957546)
XLA Ops:
  0.7 3.5 %start.1 = (bf16[1792,128]{1,0:T(8,128)(2,1)}, f32[96,128]{1,0:T(8,128)S(1)}, f32[96,128]{1,0:T(8,128)S(1)}, f32[96,128]{1,0:T(8,128)S(1)}, f32[96,128]{1,0:T(8,...) custom-call(f32[3,4096]{1,0:T(4,128)} %refs_0_.1, f32[3,4096]{1,0:T(4,128)} %refs_1_.2, f32[3,3,4096]{2,1,0:T(4,128)} %refs_2_.1, ...), custom_call_target="tpu_custom_call" | custom-call | tf_op jit(solution)/shard_map/start/pallas_call | solution.py:631
  4.2 7.3 %all-to-all-start = ((bf16[32,56,128]{2,1,0:T(8,128)(2,1)}), bf16[32,56,128]{2,1,0:T(8,128)(2,1)S(1)}, u32[]{:S(2)}, u32[]{:S(2)}) async-start(bf16[32,56,128]{2,1,0:T(8,128)(2,1)} %bitcast.53), calls=%async_computation | async-start | bytes 917504 | tf_op jit(solution)/shard_map/all_to_all | solution.py:651
  11.6 3.4 %maps.1 = (f32[576,128]{1,0:T(8,128)}, f32[576,128]{1,0:T(8,128)}) custom-call(f32[576,128]{1,0:T(8,128)} %bitcast.43, s32[16,128]{1,0:T(8,128)} %refs_12_.1, f32[576,128]{1,0:T(8,128)} %bitcast.39), custom_call_target="tpu_custom_call" | custom-call | tf_op jit(solution)/shard_map/maps/pallas_call | solution.py:631
  15.0 0.7 fusion.1.refs_7_.refs_12_
  16.4 0.8 fusion.refs_0_
  17.2 3.4 %order.1.refs_10_.refs_15_ = bf16[3072,384]{1,0:T(8,128)(2,1)S(1)} custom-call(bf16[384,384]{1,0:T(8,128)(2,1)} %fusion.refs_0_, bf16[3072,384]{1,0:T(8,128)(2,1)} %bitcast.46), custom_call_target="tpu_custom_call" | custom-call | tf_op jit(solution)/shard_map/order/pallas_call | solution.py:631
  20.7 0.6 pad_add_fusion.refs_8_.refs_13_
  21.3 4.6 %all-to-all-done = bf16[32,56,128]{2,1,0:T(8,128)(2,1)S(1)} async-done(((bf16[32,56,128]{2,1,0:T(8,128)(2,1)}), bf16[32,56,128]{2,1,0:T(8,128)(2,1)S(1)}, u32[]{:S(2)}, u32[]{:S(2)}) %all-to-all-start) | async-done | bytes 458784 | tf_op jit(solution)/shard_map/all_to_all | solution.py:651
  26.0 5.0 %product_first.1 = (bf16[256,128]{1,0:T(8,128)(2,1)}, bf16[96,128]{1,0:T(8,128)(2,1)}, f32[8,128]{1,0:T(8,128)}, f32[96,128]{1,0:T(8,128)S(1)}, f32[96,128]{1,0:...) custom-call(bf16[1792,128]{1,0:T(8,128)(2,1)S(1)} %bitcast.29, f32[96,128]{1,0:T(8,128)S(1)} %get-tuple-element.50.refs_1_, ...), custom_call_target="tpu_custom_call" | custom-call | tf_op jit(solution)/shard_map/product_first/pallas_call | solution.py:631
  31.0 2.8 %all-to-all-start.1 = ((bf16[32,8,128]{2,1,0:T(8,128)(2,1)}), bf16[32,8,128]{2,1,0:T(8,128)(2,1)S(1)}, u32[]{:S(2)}, u32[]{:S(2)}) async-start(bf16[32,8,128]{2,1,0:T(8,128)(2,1)} %bitcast.60), calls=%async_computation.1 | async-start | bytes 131072 | tf_op jit(solution)/shard_map/all_to_all | solution.py:651
  33.7 1.6 %collective-permute-start.2 = (bf16[96,128]{1,0:T(8,128)(2,1)}, bf16[96,128]{1,0:T(8,128)(2,1)S(1)}, u32[]{:S(2)}, u32[]{:S(2)}) collective-permute-start(bf16[96,128]{1,0:T(8,128)(2,1)} %get-tuple-element.61.refs_12_), channel_id=1, source_target_pairs={{0,3},{1,2},{2,1},{3,0},{4,7},{5,6},{6,5},{7,4},{8,11},{9,10},{10,... | collective-permute-start | bytes 73736 | tf_op jit(solution)/shard_map/ppermute | solution.py:657
  35.7 1.7 %collective-permute-done.2.refs_15_ = bf16[96,128]{1,0:T(8,128)(2,1)S(1)} collective-permute-done((bf16[96,128]{1,0:T(8,128)(2,1)}, bf16[96,128]{1,0:T(8,128)(2,1)S(1)}, u32[]{:S(2)}, u32[]{:S(2)}) %collective-permute-start.2) | collective-permute-done | bytes 24608 | tf_op jit(solution)/shard_map/ppermute | solution.py:657
  37.4 2.0 %collective-permute-done.1.refs_14_ = bf16[96,128]{1,0:T(8,128)(2,1)S(1)} collective-permute-done((bf16[96,128]{1,0:T(8,128)(2,1)}, bf16[96,128]{1,0:T(8,128)(2,1)S(1)}, u32[]{:S(2)}, u32[]{:S(2)}) %collective-permute-start.1) | collective-permute-done | bytes 24608 | tf_op jit(solution)/shard_map/ppermute | solution.py:657
  39.4 1.8 %all-to-all-done.1 = bf16[32,8,128]{2,1,0:T(8,128)(2,1)S(1)} async-done(((bf16[32,8,128]{2,1,0:T(8,128)(2,1)}), bf16[32,8,128]{2,1,0:T(8,128)(2,1)S(1)}, u32[]{:S(2)}, u32[]{:S(2)}) %all-to-all-start.1) | async-done | bytes 65568 | tf_op jit(solution)/shard_map/all_to_all | solution.py:651
  41.2 2.7 %update.2 = (f32[96,128]{1,0:T(8,128)S(1)}, f32[96,128]{1,0:T(8,128)S(1)}, f32[96,128]{1,0:T(8,128)S(1)}, f32[96,128]{1,0:T(8,128)S(1)}, bf16[512,128]{1,0:T(8,1...) custom-call(f32[8,128]{1,0:T(8,128)} %get-tuple-element.55.refs_0_.refs_2_, ...), custom_call_target="tpu_custom_call" | custom-call | tf_op jit(solution)/shard_map/update/pallas_call | solution.py:631
  43.8 11.0 %all_to_all.30 = bf16[32,16,128]{2,1,0:T(8,128)(2,1)S(1)} all-to-all(bf16[32,16,128]{2,1,0:T(8,128)(2,1)} %bitcast.57), channel_id=1, replica_groups=mesh['tm'=8,'lm'=4] {'tm','lm'}, dimensions={0} | all-to-all | bytes 262144 | tf_op jit(solution)/shard_map/all_to_all | solution.py:651
  54.9 4.8 %product.2 = (bf16[256,128]{1,0:T(8,128)(2,1)}, bf16[96,128]{1,0:T(8,128)(2,1)}, f32[8,128]{1,0:T(8,128)}, f32[96,128]{1,0:T(8,128)S(1)}, f32[96,128]{1,0:T(8,128)S(1)}, /*index=5*/f32[256,128]{1,0:T(8,128)S(1)}) custom-call(bf16[512,128]{1,0:T(8,128)(2,1)S(1)} %bitcast.31, f32[576,128]{1,0:T(8,128)S(1)} %get-tuple-element.64.refs_1_, ...), custom_call_target="tpu_custom_call" | custom-call | tf_op jit(solution)/shard_map/product/pallas_call | solution.py:631
  59.6 2.8 %all-to-all-start.3 = ((bf16[32,8,128]{2,1,0:T(8,128)(2,1)}), bf16[32,8,128]{2,1,0:T(8,128)(2,1)S(1)}, u32[]{:S(2)}, u32[]{:S(2)}) async-start(bf16[32,8,128]{2,1,0:T(8,128)(2,1)} %bitcast.59), calls=%async_computation.3 | async-start | bytes 131072 | tf_op jit(solution)/shard_map/all_to_all | solution.py:651
  62.4 1.3 %collective-permute-start.5 = (bf16[96,128]{1,0:T(8,128)(2,1)}, bf16[96,128]{1,0:T(8,128)(2,1)S(1)}, u32[]{:S(2)}, u32[]{:S(2)}) collective-permute-start(bf16[96,128]{1,0:T(8,128)(2,1)} %get-tuple-element.75.refs_14_), channel_id=1, source_target_pairs={{0,3},{1,2},{2,1},{3,0},{4,7},{5,6},{6,5},{7,4},{8,11},{9,10},{10,... | collective-permute-start | bytes 73736 | tf_op jit(solution)/shard_map/ppermute | solution.py:657
  63.7 0.4 collective-permute-start.4
  64.4 1.8 %collective-permute-done.5.refs_17_ = bf16[96,128]{1,0:T(8,128)(2,1)S(1)} collective-permute-done((bf16[96,128]{1,0:T(8,128)(2,1)}, bf16[96,128]{1,0:T(8,128)(2,1)S(1)}, u32[]{:S(2)}, u32[]{:S(2)}) %collective-permute-start.5) | collective-permute-done | bytes 24608 | tf_op jit(solution)/shard_map/ppermute | solution.py:657
  66.2 1.6 %collective-permute-done.4.refs_16_ = bf16[96,128]{1,0:T(8,128)(2,1)S(1)} collective-permute-done((bf16[96,128]{1,0:T(8,128)(2,1)}, bf16[96,128]{1,0:T(8,128)(2,1)S(1)}, u32[]{:S(2)}, u32[]{:S(2)}) %collective-permute-start.4) | collective-permute-done | bytes 24608 | tf_op jit(solution)/shard_map/ppermute | solution.py:657
  67.8 1.8 %all-to-all-done.3 = bf16[32,8,128]{2,1,0:T(8,128)(2,1)S(1)} async-done(((bf16[32,8,128]{2,1,0:T(8,128)(2,1)}), bf16[32,8,128]{2,1,0:T(8,128)(2,1)S(1)}, u32[]{:S(2)}, u32[]{:S(2)}) %all-to-all-start.3) | async-done | bytes 65568 | tf_op jit(solution)/shard_map/all_to_all | solution.py:651
  69.7 2.6 %update.3 = (f32[96,128]{1,0:T(8,128)S(1)}, f32[96,128]{1,0:T(8,128)S(1)}, f32[96,128]{1,0:T(8,128)S(1)}, f32[96,128]{1,0:T(8,128)S(1)}, bf16[512,128]{1,0:T(8,1...) custom-call(f32[8,128]{1,0:T(8,128)} %get-tuple-element.68.refs_0_.refs_2_, ...), custom_call_target="tpu_custom_call" | custom-call | tf_op jit(solution)/shard_map/update/pallas_call | solution.py:631
  72.3 11.1 %all_to_all.31 = bf16[32,16,128]{2,1,0:T(8,128)(2,1)S(1)} all-to-all(bf16[32,16,128]{2,1,0:T(8,128)(2,1)} %bitcast.56), channel_id=1, replica_groups=mesh['tm'=8,'lm'=4] {'tm','lm'}, dimensions={0} | all-to-all | bytes 262144 | tf_op jit(solution)/shard_map/all_to_all | solution.py:651
  83.3 4.8 %product.3 = (bf16[256,128]{1,0:T(8,128)(2,1)}, bf16[96,128]{1,0:T(8,128)(2,1)}, f32[8,128]{1,0:T(8,128)}, f32[96,128]{1,0:T(8,128)S(1)}, f32[96,128]{1,0:T(8,128)S(1)}, /*index=5*/f32[256,128]{1,0:T(8,128)}) custom-call(bf16[512,128]{1,0:T(8,128)(2,1)S(1)} %bitcast.30, f32[576,128]{1,0:T(8,128)S(1)} %get-tuple-element.64.refs_1_, ...), custom_call_target="tpu_custom_call" | custom-call | tf_op jit(solution)/shard_map/product/pallas_call | solution.py:631
  88.1 2.6 %all-to-all-start.5 = ((bf16[32,8,128]{2,1,0:T(8,128)(2,1)}), bf16[32,8,128]{2,1,0:T(8,128)(2,1)S(1)}, u32[]{:S(2)}, u32[]{:S(2)}) async-start(bf16[32,8,128]{2,1,0:T(8,128)(2,1)} %bitcast.58), calls=%async_computation.5 | async-start | bytes 131072 | tf_op jit(solution)/shard_map/all_to_all | solution.py:651
  90.7 1.4 %collective-permute-start.8 = (bf16[96,128]{1,0:T(8,128)(2,1)}, bf16[96,128]{1,0:T(8,128)(2,1)S(1)}, u32[]{:S(2)}, u32[]{:S(2)}) collective-permute-start(bf16[96,128]{1,0:T(8,128)(2,1)} %get-tuple-element.88.refs_10_), channel_id=1, source_target_pairs={{0,3},{1,2},{2,1},{3,0},{4,7},{5,6},{6,5},{7,4},{8,11},{9,10},{10,... | collective-permute-start | bytes 73736 | tf_op jit(solution)/shard_map/ppermute | solution.py:657
  92.6 1.7 %collective-permute-done.8.refs_13_ = bf16[96,128]{1,0:T(8,128)(2,1)S(1)} collective-permute-done((bf16[96,128]{1,0:T(8,128)(2,1)}, bf16[96,128]{1,0:T(8,128)(2,1)S(1)}, u32[]{:S(2)}, u32[]{:S(2)}) %collective-permute-start.8) | collective-permute-done | bytes 24608 | tf_op jit(solution)/shard_map/ppermute | solution.py:657
  94.4 1.9 %collective-permute-done.7.refs_12_ = bf16[96,128]{1,0:T(8,128)(2,1)S(1)} collective-permute-done((bf16[96,128]{1,0:T(8,128)(2,1)}, bf16[96,128]{1,0:T(8,128)(2,1)S(1)}, u32[]{:S(2)}, u32[]{:S(2)}) %collective-permute-start.7) | collective-permute-done | bytes 24608 | tf_op jit(solution)/shard_map/ppermute | solution.py:657
  96.3 1.8 %all-to-all-done.5 = bf16[32,8,128]{2,1,0:T(8,128)(2,1)S(1)} async-done(((bf16[32,8,128]{2,1,0:T(8,128)(2,1)}), bf16[32,8,128]{2,1,0:T(8,128)(2,1)S(1)}, u32[]{:S(2)}, u32[]{:S(2)}) %all-to-all-start.5) | async-done | bytes 65568 | tf_op jit(solution)/shard_map/all_to_all | solution.py:651
  98.1 1.8 %update_last.1 = (f32[96,128]{1,0:T(8,128)}, f32[3,4096]{1,0:T(4,128)}, f32[96,128]{1,0:T(8,128)}, f32[3,4096]{1,0:T(4,128)}) custom-call(f32[8,128]{1,0:T(8,128)} %get-tuple-element.81.refs_0_, f32[96,128]{1,0:T(8,128)S(1)} %get-tuple-element.82.refs_1_, f32[96,128]{1,0:T(8,128)S(1)} %get-tuple-element.83.refs_2_, f32[96,128]{1,0:T(8,128)S(1)} %get-tuple-element.84.refs_3_, ...), custom_call_target="tpu_custom_call" | custom-call | tf_op jit(solution)/shard_map/update_last/pallas_call | solution.py:631
  (26 shorter events, 1.8 us)
Async XLA Ops:
  0.6 14.3 %copy-start.2 = (s32[96]{0:T(128)S(1)}, s32[96]{0:T(128)}, u32[]{:S(2)}) copy-start(s32[96]{0:T(128)} %param.19) | copy-start | bytes 1156
  0.6 15.2 %copy-start = (s32[96]{0:T(128)S(1)}, s32[96]{0:T(128)}, u32[]{:S(2)}) copy-start(s32[96]{0:T(128)} %param.18) | copy-start | bytes 1156
  0.7 15.4 %copy-start.1 = (s32[96]{0:T(128)S(1)}, s32[96]{0:T(128)}, u32[]{:S(2)}) copy-start(s32[96]{0:T(128)} %param.20) | copy-start | bytes 1156
  4.2 21.8 %all-to-all-start = ((bf16[32,56,128]{2,1,0:T(8,128)(2,1)}), bf16[32,56,128]{2,1,0:T(8,128)(2,1)S(1)}, u32[]{:S(2)}, u32[]{:S(2)}) async-start(bf16[32,56,128]{2,1,0:T(8,128)(2,1)} %bitcast.53), calls=%async_computation | async-start | bytes 917504 | tf_op jit(solution)/shard_map/all_to_all | solution.py:651
  31.0 10.2 %all-to-all-start.1 = ((bf16[32,8,128]{2,1,0:T(8,128)(2,1)}), bf16[32,8,128]{2,1,0:T(8,128)(2,1)S(1)}, u32[]{:S(2)}, u32[]{:S(2)}) async-start(bf16[32,8,128]{2,1,0:T(8,128)(2,1)} %bitcast.60), calls=%async_computation.1 | async-start | bytes 131072 | tf_op jit(solution)/shard_map/all_to_all | solution.py:651
  33.7 3.6 %collective-permute-start.2 = (bf16[96,128]{1,0:T(8,128)(2,1)}, bf16[96,128]{1,0:T(8,128)(2,1)S(1)}, u32[]{:S(2)}, u32[]{:S(2)}) collective-permute-start(bf16[96,128]{1,0:T(8,128)(2,1)} %get-tuple-element.61.refs_12_), channel_id=1, source_target_pairs={{0,3},{1,2},{2,1},{3,0},{4,7},{5,6},{6,5},{7,4},{8,11},{9,10},{10,... | collective-permute-start | bytes 73736 | tf_op jit(solution)/shard_map/ppermute | solution.py:657
  35.3 4.1 %collective-permute-start.1 = (bf16[96,128]{1,0:T(8,128)(2,1)}, bf16[96,128]{1,0:T(8,128)(2,1)S(1)}, u32[]{:S(2)}, u32[]{:S(2)}) collective-permute-start(bf16[96,128]{1,0:T(8,128)(2,1)} %get-tuple-element.61.refs_12_), channel_id=1, source_target_pairs={{0,2},{1,3},{2,0},{3,1},{4,6},{5,7},{6,4},{7,5},{8,10},{9,11},{10,... | collective-permute-start | bytes 73736 | tf_op jit(solution)/shard_map/ppermute | solution.py:657
  35.7 3.7 %collective-permute-start = (bf16[96,128]{1,0:T(8,128)(2,1)}, bf16[96,128]{1,0:T(8,128)(2,1)S(1)}, u32[]{:S(2)}, u32[]{:S(2)}) collective-permute-start(bf16[96,128]{1,0:T(8,128)(2,1)} %get-tuple-element.61.refs_12_), channel_id=1, source_target_pairs={{0,1},{1,0},{2,3},{3,2},{4,5},{5,4},{6,7},{7,6},{8,9},{9,8},{10,11... | collective-permute-start | bytes 73736 | tf_op jit(solution)/shard_map/ppermute | solution.py:657
  59.6 10.0 %all-to-all-start.3 = ((bf16[32,8,128]{2,1,0:T(8,128)(2,1)}), bf16[32,8,128]{2,1,0:T(8,128)(2,1)S(1)}, u32[]{:S(2)}, u32[]{:S(2)}) async-start(bf16[32,8,128]{2,1,0:T(8,128)(2,1)} %bitcast.59), calls=%async_computation.3 | async-start | bytes 131072 | tf_op jit(solution)/shard_map/all_to_all | solution.py:651
  62.4 3.7 %collective-permute-start.5 = (bf16[96,128]{1,0:T(8,128)(2,1)}, bf16[96,128]{1,0:T(8,128)(2,1)S(1)}, u32[]{:S(2)}, u32[]{:S(2)}) collective-permute-start(bf16[96,128]{1,0:T(8,128)(2,1)} %get-tuple-element.75.refs_14_), channel_id=1, source_target_pairs={{0,3},{1,2},{2,1},{3,0},{4,7},{5,6},{6,5},{7,4},{8,11},{9,10},{10,... | collective-permute-start | bytes 73736 | tf_op jit(solution)/shard_map/ppermute | solution.py:657
  63.7 4.1 %collective-permute-start.4 = (bf16[96,128]{1,0:T(8,128)(2,1)}, bf16[96,128]{1,0:T(8,128)(2,1)S(1)}, u32[]{:S(2)}, u32[]{:S(2)}) collective-permute-start(bf16[96,128]{1,0:T(8,128)(2,1)} %get-tuple-element.75.refs_14_), channel_id=1, source_target_pairs={{0,2},{1,3},{2,0},{3,1},{4,6},{5,7},{6,4},{7,5},{8,10},{9,11},{10,... | collective-permute-start | bytes 73736 | tf_op jit(solution)/shard_map/ppermute | solution.py:657
  64.1 3.7 %collective-permute-start.3 = (bf16[96,128]{1,0:T(8,128)(2,1)}, bf16[96,128]{1,0:T(8,128)(2,1)S(1)}, u32[]{:S(2)}, u32[]{:S(2)}) collective-permute-start(bf16[96,128]{1,0:T(8,128)(2,1)} %get-tuple-element.75.refs_14_), channel_id=1, source_target_pairs={{0,1},{1,0},{2,3},{3,2},{4,5},{5,4},{6,7},{7,6},{8,9},{9,8},{10,11... | collective-permute-start | bytes 73736 | tf_op jit(solution)/shard_map/ppermute | solution.py:657
  88.1 10.0 %all-to-all-start.5 = ((bf16[32,8,128]{2,1,0:T(8,128)(2,1)}), bf16[32,8,128]{2,1,0:T(8,128)(2,1)S(1)}, u32[]{:S(2)}, u32[]{:S(2)}) async-start(bf16[32,8,128]{2,1,0:T(8,128)(2,1)} %bitcast.58), calls=%async_computation.5 | async-start | bytes 131072 | tf_op jit(solution)/shard_map/all_to_all | solution.py:651
  90.7 3.7 %collective-permute-start.8 = (bf16[96,128]{1,0:T(8,128)(2,1)}, bf16[96,128]{1,0:T(8,128)(2,1)S(1)}, u32[]{:S(2)}, u32[]{:S(2)}) collective-permute-start(bf16[96,128]{1,0:T(8,128)(2,1)} %get-tuple-element.88.refs_10_), channel_id=1, source_target_pairs={{0,3},{1,2},{2,1},{3,0},{4,7},{5,6},{6,5},{7,4},{8,11},{9,10},{10,... | collective-permute-start | bytes 73736 | tf_op jit(solution)/shard_map/ppermute | solution.py:657
  92.1 4.1 %collective-permute-start.7 = (bf16[96,128]{1,0:T(8,128)(2,1)}, bf16[96,128]{1,0:T(8,128)(2,1)S(1)}, u32[]{:S(2)}, u32[]{:S(2)}) collective-permute-start(bf16[96,128]{1,0:T(8,128)(2,1)} %get-tuple-element.88.refs_10_), channel_id=1, source_target_pairs={{0,2},{1,3},{2,0},{3,1},{4,6},{5,7},{6,4},{7,5},{8,10},{9,11},{10,... | collective-permute-start | bytes 73736 | tf_op jit(solution)/shard_map/ppermute | solution.py:657
  92.5 3.8 %collective-permute-start.6 = (bf16[96,128]{1,0:T(8,128)(2,1)}, bf16[96,128]{1,0:T(8,128)(2,1)S(1)}, u32[]{:S(2)}, u32[]{:S(2)}) collective-permute-start(bf16[96,128]{1,0:T(8,128)(2,1)} %get-tuple-element.88.refs_10_), channel_id=1, source_target_pairs={{0,1},{1,0},{2,3},{3,2},{4,5},{5,4},{6,7},{7,6},{8,9},{9,8},{10,11... | collective-permute-start | bytes 73736 | tf_op jit(solution)/shard_map/ppermute | solution.py:657
